TPU v7x, 768 devices: a whole 4x8x12 slice. The times are simulated.
768 devices in a mesh: gx: 12 (over z_lo, x), gy: 8 (over z_hi, core), gz: 8 (over y).
Axes of the slice: x: 4, y: 8, z: 12 (z_hi: 4, z_lo: 3; z = z_hi * 3 + z_lo), core: 2. Of those that a mesh axis runs over, the one named last changes fastest.
Arguments:
- positions: float32 [3, 36, 24, 24, 2], P(None, 'gx', 'gy', 'gz'), may hold values from 0.7 to 17.3, as said below
- velocity: float32 [3, 36, 24, 24, 2], P(None, 'gx', 'gy', 'gz'), may hold values from -2 to 2
- species: int32 [36, 24, 24, 2], P('gx', 'gy', 'gz'), may hold values from 0 to 4
- region_count: int32 [36, 24, 24], P('gx', 'gy', 'gz'), may hold values from 0 to 2, as said below
- neighbours: int32 [36, 24, 24, 2, 40], P('gx', 'gy', 'gz'), may hold values from -1 to 249, as said below
- basis_weight: bfloat16 [8, 128], replicated, may hold values from -2 to 2
- species_embed: bfloat16 [5, 128], replicated, may hold values from -3 to 3
- weight_map: bfloat16 [128, 64], replicated, may hold values from -0.5 to 0.5
- scalar_map: bfloat16 [64, 128], replicated, may hold values from -0.75 to 0.75
- energy_out: float32 [128], replicated, may hold values from -0.5 to 0.5
- species_energy: float32 [5], replicated, may hold values from -2 to -0.5
Outputs:
- forces: float32 [2, 3, 36, 24, 24, 2], P(None, None, 'gx', 'gy', 'gz')
- energy: float32 [2], replicated
Inputs may be any that keep to these rules, and one draw needn't show every extreme that they name: `region_count`: slots at or above a region's count are empty. every region of the last x layer is full. `positions`: atoms sit on a jittered lattice of spacing 2 inside their region, region (X, Y, Z) covering [6 (X % 3), 6 (X % 3) + 6) and likewise along y and z in its domain's frame; any two slots are 1.4 or more apart. `neighbours`: entries follow the numbering of the steps and name live atoms within lattice distance below 3 spacings; live entries come first, then -1; an empty slot's list is all -1; each unordered pair of atoms appears in at most one list: with p the pair's lattice point that comes first in x, then y, then z, and o the lattice offset from p to the other point, the pair is listed by p's atom if the components of o sum to an even number, else by the other atom. Entries index a 5 x 5 x 5 block of regions around the domain.
All inputs are finite; a program needn't handle non-finite values.
Results may differ from a plain program's by a relative error of at most 0.013.
Values sent between devices are 32-bit elements; how exact they have to be, the bound alone decides.
No kernel may reach another device: no remote copies, remote signals or barrier semaphores. Data moves between devices by JAX's collectives and lax.ppermute only.
A program may use at most 64 MiB of HBM per device.

v0:
```python
import math

import jax
import jax.numpy as jnp
from jax import lax
from jax.sharding import PartitionSpec as P

cutoff = 6.0
env_scale = 0.25
domain_side = 18.0
time_step = 0.15
atom_masses = (1.008, 12.011, 14.007, 15.999, 32.06)


def extended_2(block, sides, width):
    for axis, dim in sides:
        count = lax.axis_size(axis)
        forward = [(i, i + 1) for i in range(count - 1)]
        forward.append((count - 1, 0))
        backward = [(target, source) for source, target in forward]
        low = lax.ppermute(
            lax.slice_in_dim(block, block.shape[dim] - width, None, axis=dim), axis, forward
        )
        high = lax.ppermute(lax.slice_in_dim(block, 0, width, axis=dim), axis, backward)
        block = jnp.concatenate([low, block, high], axis=dim)
    return block


def contract(weight, values):
    return lax.dot_general(
        weight, values, (((0,), (0,)), ((), ())), preferred_element_type=jnp.float32
    )


def edge_front(displace, species_pair, basis_weight, species_embed, weight_map):
    radius = jnp.sqrt(jnp.sum(displace * displace, axis=0))
    direction = displace / radius[None, :]
    scaled = jnp.minimum(radius / cutoff, 1.0)
    envelope = 1.0 - 28.0 * scaled**6 + 48.0 * scaled**7 - 21.0 * scaled**8
    orders = jnp.arange(1, basis_weight.shape[0] + 1).astype(jnp.float32)
    radial = (
        math.sqrt(2.0 / cutoff)
        * jnp.sin(orders[:, None] * (math.pi / cutoff) * radius[None, :])
        / radius[None, :]
    )
    preact = contract(basis_weight, radial.astype(jnp.bfloat16)) + contract(
        species_embed, species_pair
    )
    latent = jax.nn.silu(preact).astype(jnp.bfloat16)
    weights = contract(weight_map, latent) * envelope[None, :]
    moments = jnp.concatenate(
        [weights, weights * direction[0:1], weights * direction[1:2], weights * direction[2:3]],
        axis=0,
    )
    return (latent, weights, direction, envelope, moments)


def spread_rows(centre, list_width):
    return jnp.broadcast_to(
        centre[:, :, None], (centre.shape[0], centre.shape[1], list_width)
    ).reshape(centre.shape[0], centre.shape[1] * list_width)


def edge_energy(
    latent, weights, direction, envelope, centre_env, pair_mask, scalar_map, energy_out
):
    channels = weights.shape[0]
    spread = spread_rows(centre_env, weights.shape[1] // centre_env.shape[1])
    aligned = (
        spread[:channels]
        + direction[0:1] * spread[channels : 2 * channels]
        + direction[1:2] * spread[2 * channels : 3 * channels]
        + direction[2:3] * spread[3 * channels :]
    )
    coupling = (env_scale * weights * aligned).astype(jnp.bfloat16)
    hidden = jax.nn.silu(latent.astype(jnp.float32) + contract(scalar_map, coupling))
    per_pair = envelope * jnp.sum(hidden * energy_out[:, None], axis=0)
    return jnp.sum(per_pair * pair_mask)


def flip_signs(channels):
    return jnp.concatenate(
        [jnp.ones((channels,), jnp.float32), -jnp.ones((3 * channels,), jnp.float32)]
    )[:, None]


def inverse_mass(species):
    table = 1.0 / jnp.array(atom_masses, dtype=jnp.float32)
    return jnp.sum(
        (species[..., None] == jnp.arange(table.shape[0])).astype(jnp.float32) * table, axis=-1
    )


def pair_inputs(extended, own_pos, own_kind, neighbours, kind_values):
    offset_base = ((jnp.arange(5) + 2) // 3 - 1).astype(jnp.float32) * domain_side
    cube_zero = jnp.zeros((5, 5, 5), jnp.float32)
    shifts = jnp.stack(
        [
            cube_zero + offset_base[:, None, None],
            cube_zero + offset_base[None, :, None],
            cube_zero + offset_base[None, None, :],
        ]
    )
    far_pos = (extended[:3] + shifts[..., None]).reshape(3, -1)
    far_kind = extended[3].reshape(-1)
    entries = neighbours.reshape(-1)
    pair_mask = (entries >= 0).astype(jnp.float32)
    safe_index = jnp.maximum(entries, 0)
    centres = own_pos.reshape(3, -1)
    list_width = neighbours.shape[-1]
    near_pos = jnp.broadcast_to(centres[:, :, None], (3, centres.shape[1], list_width)).reshape(
        3, -1
    )
    near_kind = jnp.broadcast_to(
        own_kind.reshape(-1)[:, None], (centres.shape[1], list_width)
    ).reshape(-1)
    displace = jnp.take(far_pos, safe_index, axis=1) - near_pos
    far_species = jnp.take(far_kind, safe_index)
    species_pair = (
        (far_species[None, :] == kind_values[:, None]).astype(jnp.float32)
        + (near_kind[None, :] == kind_values[:, None]).astype(jnp.float32)
    ).astype(jnp.bfloat16)
    return (displace, species_pair, pair_mask, safe_index)


def fold_axis(extended, axis_dim):
    first = lax.index_in_dim(extended, 0, axis_dim) + lax.index_in_dim(extended, 2, axis_dim)
    middle = lax.index_in_dim(extended, 3, axis_dim)
    last = lax.index_in_dim(extended, 4, axis_dim) + lax.index_in_dim(extended, 6, axis_dim)
    return jnp.concatenate([first, middle, last], axis=axis_dim)


def to_ghosts(blocks):
    widened = extended_2(blocks, (("gx", 1),), 1)
    widened = extended_2(widened, (("gy", 2),), 1)
    widened = extended_2(widened, (("gz", 3),), 1)
    return widened


def to_owners(blocks):
    widened = extended_2(blocks, (("gx", 1), ("gy", 2), ("gz", 3)), 1)
    folded = fold_axis(fold_axis(fold_axis(widened, 1), 2), 3)
    return folded


def evaluate(own_pos, own_kind, live_slots, neighbours, params):
    basis_weight, species_embed, weight_map, scalar_map, energy_out, species_energy = params
    sites = own_pos.shape[-1]
    channels = weight_map.shape[1]
    own_count = 27 * sites
    list_width = neighbours.shape[-1]
    kind_values = jnp.arange(species_embed.shape[0]).astype(jnp.float32)
    packed = jnp.concatenate([own_pos, own_kind[None]], axis=0)
    extended = to_ghosts(packed)
    displace, species_pair, pair_mask, safe_index = pair_inputs(
        extended, own_pos, own_kind, neighbours, kind_values
    )

    def front(displace_in):
        return edge_front(displace_in, species_pair, basis_weight, species_embed, weight_map)

    outputs, front_pull = jax.vjp(front, displace)
    latent, weights, direction, envelope, moments = outputs
    masked = moments * pair_mask[None, :]
    centre_sum = jnp.sum(masked.reshape(4 * channels, own_count, list_width), axis=2)
    signs = flip_signs(channels)
    scattered = (
        jnp.zeros((4 * channels, 125 * sites), jnp.float32).at[:, safe_index].add(masked * signs)
    )
    environment = (
        to_owners(scattered.reshape(4 * channels, 5, 5, 5, sites)).reshape(4 * channels, own_count)
        + centre_sum
    )

    def energy_fn(latent_in, weights_in, direction_in, envelope_in, env_in):
        return edge_energy(
            latent_in,
            weights_in,
            direction_in,
            envelope_in,
            env_in,
            pair_mask,
            scalar_map,
            energy_out,
        )

    pair_total, energy_pull = jax.vjp(energy_fn, latent, weights, direction, envelope, environment)
    grad_latent, grad_weights, grad_direction, grad_envelope, grad_env = energy_pull(
        jnp.ones((), jnp.float32)
    )
    ghost_grad = to_ghosts(grad_env.reshape(4 * channels, 3, 3, 3, sites)).reshape(
        4 * channels, 125 * sites
    )
    grad_moments = pair_mask[None, :] * (
        spread_rows(grad_env, list_width) + signs * jnp.take(ghost_grad, safe_index, axis=1)
    )
    (grad_displace,) = front_pull(
        (grad_latent, grad_weights, grad_direction, grad_envelope, grad_moments)
    )
    pushed = (
        jnp.zeros((3, 125 * sites), jnp.float32)
        .at[:, safe_index]
        .add(grad_displace * pair_mask[None, :])
    )
    pulled = -jnp.sum(grad_displace.reshape(3, own_count, list_width), axis=2)
    gradient = to_owners(pushed.reshape(3, 5, 5, 5, sites)).reshape(3, own_count) + pulled
    force = -gradient * live_slots[None, :]
    atom_term = jnp.sum(
        live_slots
        * jnp.sum(
            (own_kind.reshape(-1)[None, :] == kind_values[:, None]).astype(jnp.float32)
            * species_energy[:, None],
            axis=0,
        )
    )
    return (force, pair_total + atom_term)


def shards(
    positions,
    velocity,
    species,
    region_count,
    neighbours,
    basis_weight,
    species_embed,
    weight_map,
    scalar_map,
    energy_out,
    species_energy,
):
    params = (basis_weight, species_embed, weight_map, scalar_map, energy_out, species_energy)
    slot_ids = lax.broadcasted_iota(jnp.int32, species.shape, 3)
    live_slots = (slot_ids < region_count[..., None]).astype(jnp.float32).reshape(-1)
    own_kind = species.astype(jnp.float32)
    force_one, energy_one = evaluate(positions, own_kind, live_slots, neighbours, params)
    force_first = force_one.reshape(positions.shape)
    moved = (
        positions
        + time_step * velocity
        + 0.5 * time_step * time_step * inverse_mass(species)[None] * force_first
    )
    force_two, energy_two = evaluate(moved, own_kind, live_slots, neighbours, params)
    totals = lax.psum((energy_one, energy_two, jnp.sum(live_slots)), ("gx", "gy", "gz"))
    energy = jnp.stack([totals[0], totals[1]]) / totals[2]
    forces = jnp.stack([force_first, force_two.reshape(positions.shape)])
    return (forces, energy)


def solution(mesh):
    placed = (
        P(None, "gx", "gy", "gz", None),
        P(None, "gx", "gy", "gz", None),
        P("gx", "gy", "gz", None),
        P("gx", "gy", "gz"),
        P("gx", "gy", "gz", None, None),
        P(),
        P(),
        P(),
        P(),
        P(),
        P(),
    )
    return jax.shard_map(
        shards,
        mesh=mesh,
        in_specs=placed,
        out_specs=(P(None, None, "gx", "gy", "gz", None), P()),
        check_vma=False,
    )
```

profile of v0, /device:TPU:1, one launch (start us, length us, event | category | flops | bytes accessed | tf_op | source)
XLA Modules:
  0.0 633.1 jit_solution(4861063784536955752)
XLA Ops:
  2.6 8.8 %collective-permute-start.1 = (f32[4,1,3,3,2]{0,4,3,2,1:T(2,128)S(1)}, f32[4,1,3,3,2]{0,4,3,2,1:T(2,128)S(1)}, u32[]{:S(2)}, u32[]{:S(2)}) collective-permute-start(f32[4,1,3,3,2]{0,4,3,2,1:T(2,128)S(1)} %get-tuple-element.151), channel_id=1, source_target_pairs={{64,0},{128,64},{192,128},{256,192},{320,256},{384,320},{448,384},... | collective-permute-start | bytes 872 | tf_op jit(solution)/shard_map/ppermute | solution.py:24
  19.0 6.6 %collective-permute-start.3 = (f32[4,5,1,3,2]{0,4,3,2,1:T(2,128)S(1)}, f32[4,5,1,3,2]{0,4,3,2,1:T(2,128)S(1)}, u32[]{:S(2)}, u32[]{:S(2)}) collective-permute-start(f32[4,5,1,3,2]{0,4,3,2,1:T(2,128)S(1)} %get-tuple-element.155), channel_id=1, source_target_pairs={{8,0},{16,8},{24,16},{32,24},{40,32},{48,40},{56,48},{0,56},{9,1},... | collective-permute-start | bytes 1448 | tf_op jit(solution)/shard_map/ppermute | solution.py:24
  25.6 7.3 %collective-permute-start.2 = (f32[4,5,1,3,2]{0,4,3,2,1:T(2,128)S(1)}, f32[4,5,1,3,2]{0,4,3,2,1:T(2,128)S(1)}, u32[]{:S(2)}, u32[]{:S(2)}) collective-permute-start(f32[4,5,1,3,2]{0,4,3,2,1:T(2,128)S(1)} %get-tuple-element.154), channel_id=1, source_target_pairs={{0,8},{8,16},{16,24},{24,32},{32,40},{40,48},{48,56},{56,0},{1,9},... | collective-permute-start | bytes 1448 | tf_op jit(solution)/shard_map/ppermute | solution.py:21
  50.3 13.2 %gather_fusion.1 = f32[2160]{0:T(1024)S(1)} fusion(f32[250]{0:T(256)S(1)} %reshape_squeeze.6, s32[3072]{0:T(1024)S(1)} %pad_clamp_fusion), kind=kCustom, calls=%fused_computation.1.clone | custom fusion | bytes 25920 | tf_op jit(solution)/shard_map/jit(_take)/gather | solution.py:118
  73.2 17.6 %scatter_custom_fusion = f32[256,250]{0,1:T(8,128)S(1)} fusion(s32[2160]{0:T(1024)} %copy-done.85, f32[2160,256]{1,0:T(8,128)} %copy.185, f32[]{:T(128)} %constant.47.clone.1), kind=kCustom, calls=%fused_computation.183 | custom fusion | flops 552960 | bytes 256512 | tf_op jit(solution)/shard_map/scatter-add | solution.py:168
  93.0 6.4 %collective-permute-start.7 = (f32[256,1,5,5,2]{0,4,3,2,1:T(2,128)S(1)}, f32[256,1,5,5,2]{0,4,3,2,1:T(2,128)S(1)}, u32[]{:S(2)}, u32[]{:S(2)}) collective-permute-start(f32[256,1,5,5,2]{0,4,3,2,1:T(2,128)S(1)} %get-tuple-element.100), channel_id=1, source_target_pairs={{64,0},{128,64},{192,128},{256,192},{320,256},{384,320},{448,384},... | collective-permute-start | bytes 153608 | tf_op jit(solution)/shard_map/ppermute | solution.py:24
  101.2 10.0 %collective-permute-start.9 = (f32[256,7,1,5,2]{0,4,3,2,1:T(2,128)}, f32[256,7,1,5,2]{0,4,3,2,1:T(2,128)S(1)}, u32[]{:S(2)}, u32[]{:S(2)}) collective-permute-start(f32[256,7,1,5,2]{0,4,3,2,1:T(2,128)} %get-tuple-element.91), channel_id=1, source_target_pairs={{8,0},{16,8},{24,16},{32,24},{40,32},{48,40},{56,48},{0,56},{9,1},... | collective-permute-start | bytes 215048 | tf_op jit(solution)/shard_map/ppermute | solution.py:24
  148.0 7.3 %collective-permute-start.13 = (f32[256,1,3,3,2]{0,4,3,2,1:T(2,128)S(1)}, f32[256,1,3,3,2]{0,4,3,2,1:T(2,128)S(1)}, u32[]{:S(2)}, u32[]{:S(2)}) collective-permute-start(f32[256,1,3,3,2]{0,4,3,2,1:T(2,128)S(1)} %get-tuple-element.148), channel_id=1, source_target_pairs={{64,0},{128,64},{192,128},{256,192},{320,256},{384,320},{448,384},... | collective-permute-start | bytes 55304 | tf_op jit(solution)/shard_map/ppermute | solution.py:24
  180.1 6.4 %gather_fusion.2 = f32[2160,256]{1,0:T(8,128)} fusion(f32[256,250]{0,1:T(8,128)S(1)} %reshape.535, s32[3072]{0:T(1024)S(1)} %pad_clamp_fusion), kind=kCustom, calls=%fused_computation.2.clone | custom fusion | bytes 4432320 | tf_op jit(solution)/shard_map/jit(_take)/gather | solution.py:195
  207.2 18.8 %scatter_custom_fusion.1 = f32[3,250]{0,1:T(8,128)S(1)} fusion(s32[2160]{0:T(1024)} %copy-done.85, f32[3,2160]{0,1:T(8,128)S(1)} %add_add_fusion.1, f32[2160]{0:T(1024)S(1)} %convert_element_type.188, f32[]{:T(128)} %constant.47.clone.1), kind=kCustom, calls=%fused_computation.83 | custom fusion | flops 12960 | bytes 38072 | tf_op jit(solution)/shard_map/scatter-add | solution.py:203
  228.3 7.2 %collective-permute-start.19 = (f32[3,1,5,5,2]{0,4,3,2,1:T(2,128)S(1)}, f32[3,1,5,5,2]{0,4,3,2,1:T(2,128)S(1)}, u32[]{:S(2)}, u32[]{:S(2)}) collective-permute-start(f32[3,1,5,5,2]{0,4,3,2,1:T(2,128)S(1)} %get-tuple-element.120), channel_id=1, source_target_pairs={{64,0},{128,64},{192,128},{256,192},{320,256},{384,320},{448,384},... | collective-permute-start | bytes 1808 | tf_op jit(solution)/shard_map/ppermute | solution.py:24
  236.5 8.5 %collective-permute-start.21 = (f32[3,7,1,5,2]{0,4,3,2,1:T(2,128)S(1)}, f32[3,7,1,5,2]{0,4,3,2,1:T(2,128)S(1)}, u32[]{:S(2)}, u32[]{:S(2)}) collective-permute-start(f32[3,7,1,5,2]{0,4,3,2,1:T(2,128)S(1)} %get-tuple-element.109), channel_id=1, source_target_pairs={{8,0},{16,8},{24,16},{32,24},{40,32},{48,40},{56,48},{0,56},{9,1},... | collective-permute-start | bytes 2528 | tf_op jit(solution)/shard_map/ppermute | solution.py:24
  261.3 8.0 %collective-permute-start.25 = (f32[4,1,3,3,2]{0,4,3,2,1:T(2,128)S(1)}, f32[4,1,3,3,2]{0,4,3,2,1:T(2,128)S(1)}, u32[]{:S(2)}, u32[]{:S(2)}) collective-permute-start(f32[4,1,3,3,2]{0,4,3,2,1:T(2,128)S(1)} %get-tuple-element.147), channel_id=1, source_target_pairs={{64,0},{128,64},{192,128},{256,192},{320,256},{384,320},{448,384},... | collective-permute-start | bytes 872 | tf_op jit(solution)/shard_map/ppermute | solution.py:24
  276.8 8.9 %collective-permute-start.27 = (f32[4,5,1,3,2]{0,4,3,2,1:T(2,128)S(1)}, f32[4,5,1,3,2]{0,4,3,2,1:T(2,128)S(1)}, u32[]{:S(2)}, u32[]{:S(2)}) collective-permute-start(f32[4,5,1,3,2]{0,4,3,2,1:T(2,128)S(1)} %get-tuple-element.153), channel_id=1, source_target_pairs={{8,0},{16,8},{24,16},{32,24},{40,32},{48,40},{56,48},{0,56},{9,1},... | collective-permute-start | bytes 1448 | tf_op jit(solution)/shard_map/ppermute | solution.py:24
  308.8 13.2 %gather_fusion.4 = f32[2160]{0:T(1024)S(1)} fusion(f32[250]{0:T(256)S(1)} %reshape_squeeze.7, s32[3072]{0:T(1024)S(1)} %pad_clamp_fusion), kind=kCustom, calls=%fused_computation.4.clone | custom fusion | bytes 25920 | tf_op jit(solution)/shard_map/jit(_take)/gather | solution.py:118
  327.7 17.6 %scatter_custom_fusion.2 = f32[256,250]{0,1:T(8,128)S(1)} fusion(s32[2160]{0:T(1024)} %copy-done.85, f32[2160,256]{1,0:T(8,128)} %copy.223, f32[]{:T(128)} %constant.47.clone.1), kind=kCustom, calls=%fused_computation.181 | custom fusion | flops 552960 | bytes 256512 | tf_op jit(solution)/shard_map/scatter-add | solution.py:168
  347.5 6.4 %collective-permute-start.31 = (f32[256,1,5,5,2]{0,4,3,2,1:T(2,128)S(1)}, f32[256,1,5,5,2]{0,4,3,2,1:T(2,128)S(1)}, u32[]{:S(2)}, u32[]{:S(2)}) collective-permute-start(f32[256,1,5,5,2]{0,4,3,2,1:T(2,128)S(1)} %get-tuple-element.98), channel_id=1, source_target_pairs={{64,0},{128,64},{192,128},{256,192},{320,256},{384,320},{448,384},... | collective-permute-start | bytes 153608 | tf_op jit(solution)/shard_map/ppermute | solution.py:24
  355.0 7.5 %collective-permute-start.33 = (f32[256,7,1,5,2]{0,4,3,2,1:T(2,128)S(1)}, f32[256,7,1,5,2]{0,4,3,2,1:T(2,128)S(1)}, u32[]{:S(2)}, u32[]{:S(2)}) collective-permute-start(f32[256,7,1,5,2]{0,4,3,2,1:T(2,128)S(1)} %get-tuple-element.89), channel_id=1, source_target_pairs={{8,0},{16,8},{24,16},{32,24},{40,32},{48,40},{56,48},{0,56},{9,1},... | collective-permute-start | bytes 215048 | tf_op jit(solution)/shard_map/ppermute | solution.py:24
  398.6 8.3 %collective-permute-start.37 = (f32[256,1,3,3,2]{0,4,3,2,1:T(2,128)S(1)}, f32[256,1,3,3,2]{0,4,3,2,1:T(2,128)S(1)}, u32[]{:S(2)}, u32[]{:S(2)}) collective-permute-start(f32[256,1,3,3,2]{0,4,3,2,1:T(2,128)S(1)} %get-tuple-element.144), channel_id=1, source_target_pairs={{64,0},{128,64},{192,128},{256,192},{320,256},{384,320},{448,384},... | collective-permute-start | bytes 55304 | tf_op jit(solution)/shard_map/ppermute | solution.py:24
  431.1 6.4 %gather_fusion.5 = f32[2160,256]{1,0:T(8,128)} fusion(f32[256,250]{0,1:T(8,128)S(1)} %reshape.551, s32[3072]{0:T(1024)S(1)} %pad_clamp_fusion), kind=kCustom, calls=%fused_computation.5.clone | custom fusion | bytes 4432320 | tf_op jit(solution)/shard_map/jit(_take)/gather | solution.py:195
  457.0 18.9 %scatter_custom_fusion.3 = f32[3,250]{0,1:T(8,128)S(1)} fusion(s32[2160]{0:T(1024)} %copy-done.85, f32[3,2160]{0,1:T(8,128)S(1)} %add_add_fusion, f32[2160]{0:T(1024)S(1)} %convert_element_type.188, f32[]{:T(128)} %constant.47.clone.1), kind=kCustom, calls=%fused_computation.80 | custom fusion | flops 12960 | bytes 38072 | tf_op jit(solution)/shard_map/scatter-add | solution.py:203
  479.2 7.4 %collective-permute-start.43 = (f32[3,1,5,5,2]{0,4,3,2,1:T(2,128)S(1)}, f32[3,1,5,5,2]{0,4,3,2,1:T(2,128)S(1)}, u32[]{:S(2)}, u32[]{:S(2)}) collective-permute-start(f32[3,1,5,5,2]{0,4,3,2,1:T(2,128)S(1)} %get-tuple-element.118), channel_id=1, source_target_pairs={{64,0},{128,64},{192,128},{256,192},{320,256},{384,320},{448,384},... | collective-permute-start | bytes 1808 | tf_op jit(solution)/shard_map/ppermute | solution.py:24
  487.6 7.3 %collective-permute-start.45 = (f32[3,7,1,5,2]{0,4,3,2,1:T(2,128)S(1)}, f32[3,7,1,5,2]{0,4,3,2,1:T(2,128)S(1)}, u32[]{:S(2)}, u32[]{:S(2)}) collective-permute-start(f32[3,7,1,5,2]{0,4,3,2,1:T(2,128)S(1)} %get-tuple-element.107), channel_id=1, source_target_pairs={{8,0},{16,8},{24,16},{32,24},{40,32},{48,40},{56,48},{0,56},{9,1},... | collective-permute-start | bytes 2528 | tf_op jit(solution)/shard_map/ppermute | solution.py:24
  501.8 117.8 %all-reduce.20 = (f32[1]{0:T(128)}, f32[1]{0:T(128)}, f32[]{:T(128)}) all-reduce(f32[1]{0:T(128)} %bitcast.64, f32[1]{0:T(128)} %bitcast.63, f32[]{:T(128)} %get-tuple-element.40), channel_id=1, replica_groups=mesh['gx'=12,'gy'=8,'gz'=8] {'gx','gy','gz'}, use_global_device_ids=true, to_apply=%region_40.44 | all-reduce | flops 3 | bytes 24 | tf_op jit(solution)/shard_map/psum | solution.py:244
  (635 shorter events, 280.6 us)
Async XLA Ops:
  2.6 13.4 %collective-permute-start.1 = (f32[4,1,3,3,2]{0,4,3,2,1:T(2,128)S(1)}, f32[4,1,3,3,2]{0,4,3,2,1:T(2,128)S(1)}, u32[]{:S(2)}, u32[]{:S(2)}) collective-permute-start(f32[4,1,3,3,2]{0,4,3,2,1:T(2,128)S(1)} %get-tuple-element.151), channel_id=1, source_target_pairs={{64,0},{128,64},{192,128},{256,192},{320,256},{384,320},{448,384},... | collective-permute-start | bytes 872 | tf_op jit(solution)/shard_map/ppermute | solution.py:24
  19.0 14.0 %collective-permute-start.3 = (f32[4,5,1,3,2]{0,4,3,2,1:T(2,128)S(1)}, f32[4,5,1,3,2]{0,4,3,2,1:T(2,128)S(1)}, u32[]{:S(2)}, u32[]{:S(2)}) collective-permute-start(f32[4,5,1,3,2]{0,4,3,2,1:T(2,128)S(1)} %get-tuple-element.155), channel_id=1, source_target_pairs={{8,0},{16,8},{24,16},{32,24},{40,32},{48,40},{56,48},{0,56},{9,1},... | collective-permute-start | bytes 1448 | tf_op jit(solution)/shard_map/ppermute | solution.py:24
  25.6 8.8 %collective-permute-start.2 = (f32[4,5,1,3,2]{0,4,3,2,1:T(2,128)S(1)}, f32[4,5,1,3,2]{0,4,3,2,1:T(2,128)S(1)}, u32[]{:S(2)}, u32[]{:S(2)}) collective-permute-start(f32[4,5,1,3,2]{0,4,3,2,1:T(2,128)S(1)} %get-tuple-element.154), channel_id=1, source_target_pairs={{0,8},{8,16},{16,24},{24,32},{32,40},{40,48},{48,56},{56,0},{1,9},... | collective-permute-start | bytes 1448 | tf_op jit(solution)/shard_map/ppermute | solution.py:21
  101.2 17.6 %collective-permute-start.9 = (f32[256,7,1,5,2]{0,4,3,2,1:T(2,128)}, f32[256,7,1,5,2]{0,4,3,2,1:T(2,128)S(1)}, u32[]{:S(2)}, u32[]{:S(2)}) collective-permute-start(f32[256,7,1,5,2]{0,4,3,2,1:T(2,128)} %get-tuple-element.91), channel_id=1, source_target_pairs={{8,0},{16,8},{24,16},{32,24},{40,32},{48,40},{56,48},{0,56},{9,1},... | collective-permute-start | bytes 215048 | tf_op jit(solution)/shard_map/ppermute | solution.py:24
  118.9 9.5 %collective-permute-start.11 = (f32[256,7,7,1,2]{0,4,3,2,1:T(2,128)S(1)}, f32[256,7,7,1,2]{0,4,3,2,1:T(2,128)S(1)}, u32[]{:S(2)}, u32[]{:S(2)}) collective-permute-start(f32[256,7,7,1,2]{0,4,3,2,1:T(2,128)S(1)} %get-tuple-element.83), channel_id=1, source_target_pairs={{1,0},{2,1},{3,2},{4,3},{5,4},{6,5},{7,6},{0,7},{9,8},{10,9},{11,1... | collective-permute-start | bytes 301064 | tf_op jit(solution)/shard_map/ppermute | solution.py:24
  146.0 9.3 %collective-permute-start.12 = (f32[256,1,3,3,2]{0,4,3,2,1:T(2,128)S(1)}, f32[256,1,3,3,2]{0,4,3,2,1:T(2,128)S(1)}, u32[]{:S(2)}, u32[]{:S(2)}) collective-permute-start(f32[256,1,3,3,2]{0,4,3,2,1:T(2,128)S(1)} %get-tuple-element.149), channel_id=1, source_target_pairs={{0,64},{64,128},{128,192},{192,256},{256,320},{320,384},{384,448},... | collective-permute-start | bytes 55304 | tf_op jit(solution)/shard_map/ppermute | solution.py:21
  165.8 13.1 %collective-permute-start.17 = (f32[256,5,5,1,2]{0,4,3,2,1:T(2,128)}, f32[256,5,5,1,2]{0,4,3,2,1:T(2,128)}, u32[]{:S(2)}, u32[]{:S(2)}) collective-permute-start(f32[256,5,5,1,2]{0,4,3,2,1:T(2,128)} %get-tuple-element.113), channel_id=1, source_target_pairs={{1,0},{2,1},{3,2},{4,3},{5,4},{6,5},{7,6},{0,7},{9,8},{10,9},{11,1... | collective-permute-start | bytes 153608 | tf_op jit(solution)/shard_map/ppermute | solution.py:24
  168.9 10.0 %collective-permute-start.16 = (f32[256,5,5,1,2]{0,4,3,2,1:T(2,128)}, f32[256,5,5,1,2]{0,4,3,2,1:T(2,128)}, u32[]{:S(2)}, u32[]{:S(2)}) collective-permute-start(f32[256,5,5,1,2]{0,4,3,2,1:T(2,128)} %get-tuple-element.112), channel_id=1, source_target_pairs={{0,1},{1,2},{2,3},{3,4},{4,5},{5,6},{6,7},{7,0},{8,9},{9,10},{10,1... | collective-permute-start | bytes 153608 | tf_op jit(solution)/shard_map/ppermute | solution.py:21
  226.1 9.4 %collective-permute-start.18 = (f32[3,1,5,5,2]{0,4,3,2,1:T(2,128)S(1)}, f32[3,1,5,5,2]{0,4,3,2,1:T(2,128)S(1)}, u32[]{:S(2)}, u32[]{:S(2)}) collective-permute-start(f32[3,1,5,5,2]{0,4,3,2,1:T(2,128)S(1)} %get-tuple-element.121), channel_id=1, source_target_pairs={{0,64},{64,128},{128,192},{192,256},{256,320},{320,384},{384,448},... | collective-permute-start | bytes 1808 | tf_op jit(solution)/shard_map/ppermute | solution.py:21
  236.5 10.7 %collective-permute-start.21 = (f32[3,7,1,5,2]{0,4,3,2,1:T(2,128)S(1)}, f32[3,7,1,5,2]{0,4,3,2,1:T(2,128)S(1)}, u32[]{:S(2)}, u32[]{:S(2)}) collective-permute-start(f32[3,7,1,5,2]{0,4,3,2,1:T(2,128)S(1)} %get-tuple-element.109), channel_id=1, source_target_pairs={{8,0},{16,8},{24,16},{32,24},{40,32},{48,40},{56,48},{0,56},{9,1},... | collective-permute-start | bytes 2528 | tf_op jit(solution)/shard_map/ppermute | solution.py:24
  248.3 8.7 %collective-permute-start.23 = (f32[3,7,7,1,2]{0,4,3,2,1:T(2,128)S(1)}, f32[3,7,7,1,2]{0,4,3,2,1:T(2,128)S(1)}, u32[]{:S(2)}, u32[]{:S(2)}) collective-permute-start(f32[3,7,7,1,2]{0,4,3,2,1:T(2,128)S(1)} %get-tuple-element.105), channel_id=1, source_target_pairs={{1,0},{2,1},{3,2},{4,3},{5,4},{6,5},{7,6},{0,7},{9,8},{10,9},{11,1... | collective-permute-start | bytes 3536 | tf_op jit(solution)/shard_map/ppermute | solution.py:24
  261.3 10.0 %collective-permute-start.25 = (f32[4,1,3,3,2]{0,4,3,2,1:T(2,128)S(1)}, f32[4,1,3,3,2]{0,4,3,2,1:T(2,128)S(1)}, u32[]{:S(2)}, u32[]{:S(2)}) collective-permute-start(f32[4,1,3,3,2]{0,4,3,2,1:T(2,128)S(1)} %get-tuple-element.147), channel_id=1, source_target_pairs={{64,0},{128,64},{192,128},{256,192},{320,256},{384,320},{448,384},... | collective-permute-start | bytes 872 | tf_op jit(solution)/shard_map/ppermute | solution.py:24
  276.8 13.2 %collective-permute-start.27 = (f32[4,5,1,3,2]{0,4,3,2,1:T(2,128)S(1)}, f32[4,5,1,3,2]{0,4,3,2,1:T(2,128)S(1)}, u32[]{:S(2)}, u32[]{:S(2)}) collective-permute-start(f32[4,5,1,3,2]{0,4,3,2,1:T(2,128)S(1)} %get-tuple-element.153), channel_id=1, source_target_pairs={{8,0},{16,8},{24,16},{32,24},{40,32},{48,40},{56,48},{0,56},{9,1},... | collective-permute-start | bytes 1448 | tf_op jit(solution)/shard_map/ppermute | solution.py:24
  355.0 17.6 %collective-permute-start.33 = (f32[256,7,1,5,2]{0,4,3,2,1:T(2,128)S(1)}, f32[256,7,1,5,2]{0,4,3,2,1:T(2,128)S(1)}, u32[]{:S(2)}, u32[]{:S(2)}) collective-permute-start(f32[256,7,1,5,2]{0,4,3,2,1:T(2,128)S(1)} %get-tuple-element.89), channel_id=1, source_target_pairs={{8,0},{16,8},{24,16},{32,24},{40,32},{48,40},{56,48},{0,56},{9,1},... | collective-permute-start | bytes 215048 | tf_op jit(solution)/shard_map/ppermute | solution.py:24
  362.5 10.1 %collective-permute-start.32 = (f32[256,7,1,5,2]{0,4,3,2,1:T(2,128)S(1)}, f32[256,7,1,5,2]{0,4,3,2,1:T(2,128)S(1)}, u32[]{:S(2)}, u32[]{:S(2)}) collective-permute-start(f32[256,7,1,5,2]{0,4,3,2,1:T(2,128)S(1)} %get-tuple-element.88), channel_id=1, source_target_pairs={{0,8},{8,16},{16,24},{24,32},{32,40},{40,48},{48,56},{56,0},{1,9},... | collective-permute-start | bytes 215048 | tf_op jit(solution)/shard_map/ppermute | solution.py:21
  372.7 9.1 %collective-permute-start.35 = (f32[256,7,7,1,2]{0,4,3,2,1:T(2,128)S(1)}, f32[256,7,7,1,2]{0,4,3,2,1:T(2,128)S(1)}, u32[]{:S(2)}, u32[]{:S(2)}) collective-permute-start(f32[256,7,7,1,2]{0,4,3,2,1:T(2,128)S(1)} %get-tuple-element.81), channel_id=1, source_target_pairs={{1,0},{2,1},{3,2},{4,3},{5,4},{6,5},{7,6},{0,7},{9,8},{10,9},{11,1... | collective-permute-start | bytes 301064 | tf_op jit(solution)/shard_map/ppermute | solution.py:24
  396.7 10.2 %collective-permute-start.36 = (f32[256,1,3,3,2]{0,4,3,2,1:T(2,128)S(1)}, f32[256,1,3,3,2]{0,4,3,2,1:T(2,128)S(1)}, u32[]{:S(2)}, u32[]{:S(2)}) collective-permute-start(f32[256,1,3,3,2]{0,4,3,2,1:T(2,128)S(1)} %get-tuple-element.145), channel_id=1, source_target_pairs={{0,64},{64,128},{128,192},{192,256},{256,320},{320,384},{384,448},... | collective-permute-start | bytes 55304 | tf_op jit(solution)/shard_map/ppermute | solution.py:21
  398.6 9.1 %collective-permute-start.37 = (f32[256,1,3,3,2]{0,4,3,2,1:T(2,128)S(1)}, f32[256,1,3,3,2]{0,4,3,2,1:T(2,128)S(1)}, u32[]{:S(2)}, u32[]{:S(2)}) collective-permute-start(f32[256,1,3,3,2]{0,4,3,2,1:T(2,128)S(1)} %get-tuple-element.144), channel_id=1, source_target_pairs={{64,0},{128,64},{192,128},{256,192},{320,256},{384,320},{448,384},... | collective-permute-start | bytes 55304 | tf_op jit(solution)/shard_map/ppermute | solution.py:24
  416.8 13.1 %collective-permute-start.41 = (f32[256,5,5,1,2]{0,4,3,2,1:T(2,128)}, f32[256,5,5,1,2]{0,4,3,2,1:T(2,128)}, u32[]{:S(2)}, u32[]{:S(2)}) collective-permute-start(f32[256,5,5,1,2]{0,4,3,2,1:T(2,128)} %get-tuple-element.111), channel_id=1, source_target_pairs={{1,0},{2,1},{3,2},{4,3},{5,4},{6,5},{7,6},{0,7},{9,8},{10,9},{11,1... | collective-permute-start | bytes 153608 | tf_op jit(solution)/shard_map/ppermute | solution.py:24
  419.9 10.1 %collective-permute-start.40 = (f32[256,5,5,1,2]{0,4,3,2,1:T(2,128)}, f32[256,5,5,1,2]{0,4,3,2,1:T(2,128)}, u32[]{:S(2)}, u32[]{:S(2)}) collective-permute-start(f32[256,5,5,1,2]{0,4,3,2,1:T(2,128)} %get-tuple-element.110), channel_id=1, source_target_pairs={{0,1},{1,2},{2,3},{3,4},{4,5},{5,6},{6,7},{7,0},{8,9},{9,10},{10,1... | collective-permute-start | bytes 153608 | tf_op jit(solution)/shard_map/ppermute | solution.py:21
  476.1 10.5 %collective-permute-start.42 = (f32[3,1,5,5,2]{0,4,3,2,1:T(2,128)S(1)}, f32[3,1,5,5,2]{0,4,3,2,1:T(2,128)S(1)}, u32[]{:S(2)}, u32[]{:S(2)}) collective-permute-start(f32[3,1,5,5,2]{0,4,3,2,1:T(2,128)S(1)} %get-tuple-element.119), channel_id=1, source_target_pairs={{0,64},{64,128},{128,192},{192,256},{256,320},{320,384},{384,448},... | collective-permute-start | bytes 1808 | tf_op jit(solution)/shard_map/ppermute | solution.py:21
  487.6 132.1 %collective-permute-start.45 = (f32[3,7,1,5,2]{0,4,3,2,1:T(2,128)S(1)}, f32[3,7,1,5,2]{0,4,3,2,1:T(2,128)S(1)}, u32[]{:S(2)}, u32[]{:S(2)}) collective-permute-start(f32[3,7,1,5,2]{0,4,3,2,1:T(2,128)S(1)} %get-tuple-element.107), channel_id=1, source_target_pairs={{8,0},{16,8},{24,16},{32,24},{40,32},{48,40},{56,48},{0,56},{9,1},... | collective-permute-start | bytes 2528 | tf_op jit(solution)/shard_map/ppermute | solution.py:24
  494.9 124.8 %collective-permute-start.44 = (f32[3,7,1,5,2]{0,4,3,2,1:T(2,128)S(1)}, f32[3,7,1,5,2]{0,4,3,2,1:T(2,128)S(1)}, u32[]{:S(2)}, u32[]{:S(2)}) collective-permute-start(f32[3,7,1,5,2]{0,4,3,2,1:T(2,128)S(1)} %get-tuple-element.106), channel_id=1, source_target_pairs={{0,8},{8,16},{16,24},{24,32},{32,40},{40,48},{48,56},{56,0},{1,9},... | collective-permute-start | bytes 2528 | tf_op jit(solution)/shard_map/ppermute | solution.py:21
  619.8 9.0 %collective-permute-start.47 = (f32[3,7,7,1,2]{0,4,3,2,1:T(2,128)S(1)}, f32[3,7,7,1,2]{0,4,3,2,1:T(2,128)S(1)}, u32[]{:S(2)}, u32[]{:S(2)}) collective-permute-start(f32[3,7,7,1,2]{0,4,3,2,1:T(2,128)S(1)} %get-tuple-element.103), channel_id=1, source_target_pairs={{1,0},{2,1},{3,2},{4,3},{5,4},{6,5},{7,6},{0,7},{9,8},{10,9},{11,1... | collective-permute-start | bytes 3536 | tf_op jit(solution)/shard_map/ppermute | solution.py:24
  (169 other events, 1537.0 us)
where the time goes:
time: 644 us; the launch traced here: 633 us
  starting transfers between devices  208 us (32%)
  local copies, waits for them, and re-layouts  130 us (20%)
  other arithmetic  125 us (19%)
  blocking collectives  118 us (18%)
  waiting for transfers between devices  26.8 us (4%)
  matrix products  18.8 us (3%)
  between operations  6.44 us (1%)
    ppermute x24, starting transfers between devices, extended_2(): lax.ppermute(lax.slice_in_dim(block, 0, width, axis=dim), axis, backward)  140 us
    psum x1, blocking collectives, shards(): lax.psum((energy_one, energy_two, jnp.sum(live_slots)), ('gx', 'gy', 'gz'))  118 us
    ppermute x24, starting transfers between devices, extended_2(): lax.ppermute(lax.slice_in_dim(block, block.shape[dim] - width, None, axis...  68.1 us
    scatter-add x2, other arithmetic, evaluate(): pushed = jnp.zeros((3, 125 * sites), jnp.float32).at[:, safe_index].add(g...  37.7 us
    scatter-add x2, other arithmetic, evaluate(): jnp.zeros((4 * channels, 125 * sites), jnp.float32).at[:, safe_index]  35.3 us
    gather x2, local copies, waits for them, and re-layouts, pair_inputs(): far_species = jnp.take(far_kind, safe_index)  26.4 us
    ppermute x24, waiting for transfers between devices, extended_2(): lax.ppermute(lax.slice_in_dim(block, block.shape[dim] - width, None, axis...  21.2 us
    gather x4, local copies, waits for them, and re-layouts, evaluate(): jnp.take(ghost_grad, safe_index, axis=1)  19.2 us
  transfers between devices with their start and end apart: 48, of which 16 were waited for; matrix products, arithmetic and copies ran while one was open for 7% of the time, Pallas kernels for 0%

commit v1 on v0

v1 whole, which is shorter than its diff:
```python
import functools
import math

import jax
import jax.numpy as jnp
from jax import lax
from jax.experimental import pallas as pl
from jax.experimental.pallas import tpu as pltpu
from jax.sharding import PartitionSpec as P

cutoff = 6.0
env_scale = 0.25
domain_side = 18.0
time_step = 0.15
atom_masses = (1.008, 12.011, 14.007, 15.999, 32.06)

CH = 64
LAT = 128
NB = 8
NSPEC = 5
LIST = 24
USED = 392
ROWS = 400
DEPTH = 512
INNER = 256
OWN = 80
TILES = 52
LANES = 128
POS, KIND, KIND3, NEIGH, VEL, LIVE3, LIVE = 0, 6, 8, 16, 64, 72, 80
MISC = NEIGH + 2 * LIST
F32 = jnp.float32
BF16 = jnp.bfloat16


def mm(a, b):
    return lax.dot_general(a, b, (((1,), (0,)), ((), ())), preferred_element_type=F32)


def mm_nt(a, b):
    return lax.dot_general(a, b, (((1,), (1,)), ((), ())), preferred_element_type=F32)


def split2(v):
    high = v.astype(BF16)
    return high, (v - high.astype(F32)).astype(BF16)


def iota(shape, dim):
    return lax.broadcasted_iota(jnp.int32, shape, dim).astype(F32)


def sigmoid(v):
    return 1.0 / (1.0 + jnp.exp(-v))


def row_coords(row):
    xy = jnp.floor(row * 0.125)
    z = row - 8.0 * xy
    x = jnp.floor((xy + 0.5) * (1.0 / 7.0))
    return x, xy - 7.0 * x, z


def away(x, y, z):
    return jnp.maximum(jnp.maximum(jnp.abs(x - 3.0), jnp.abs(y - 3.0)), jnp.abs(z - 3.0))


def far_coords(x, y, z, entry):
    q = jnp.floor(entry * 0.5)
    a = jnp.floor((q + 0.5) * (1.0 / 25.0))
    ab = jnp.floor((q + 0.5) * (1.0 / 5.0))
    steps = (a, ab - 5.0 * a, q - 5.0 * ab)
    far = [3.0 * jnp.floor((v + 1.5) * (1.0 / 3.0)) + s - 2.0 for v, s in zip((x, y, z), steps)]
    shift = [(jnp.floor((s + 2.5) * (1.0 / 3.0)) - 1.0) * domain_side for s in steps]
    return far, shift, entry - 2.0 * q


def one_hot(index, count, depth):
    hit = (iota((count, LANES), 0) == index).astype(F32).astype(BF16)
    if depth > count:
        hit = jnp.concatenate([hit, jnp.zeros((depth - count, LANES), BF16)], axis=0)
    return hit


def build_pairs(rows_ref, table, off_ref, end_ref, pairs_ref, listed_t):
    shape = (ROWS, LANES)
    lane = iota(shape, 1)
    row = iota(shape, 0)
    x, y, z = row_coords(row)
    entry = rows_ref[0:ROWS]
    in_list = (lane >= NEIGH) & (lane < MISC)
    listed = in_list & (entry >= 0.0) & (z < 6.5) & (row < USED)
    far, _, _ = far_coords(x, y, z, entry)
    nearest = jnp.minimum(away(x, y, z), away(*far))
    kept = (listed & (nearest < 1.5), listed & (nearest > 1.5) & (nearest < 2.5))
    upper = (iota((LANES, LANES), 0) <= iota((LANES, LANES), 1)).astype(F32).astype(BF16)
    ones = jnp.ones((LANES, LANES), BF16)
    below = (iota((ROWS, DEPTH), 1) < iota((ROWS, DEPTH), 0)).astype(F32).astype(BF16)
    start = jnp.int32(0)
    counts = []
    for keep in kept:
        keep = keep.astype(F32)
        keep16 = keep.astype(BF16)
        rank = mm(keep16, upper) * keep
        count = mm(keep16, ones)
        padded = jnp.concatenate(
            [count.astype(BF16), jnp.zeros((DEPTH - ROWS, LANES), BF16)], axis=0
        )
        offset = mm(below, padded)
        end = offset + count
        off_ref[...] = offset
        end_ref[...] = end
        total = jnp.max(end)
        high = jnp.floor(offset * (1.0 / 256.0))
        fields = jnp.where(in_list, rank, 0.0)
        for at, value in enumerate((high, offset - 256.0 * high, x, y, z)):
            fields = jnp.where(lane == float(MISC + at), value, fields)
        fields = jnp.concatenate([fields, jnp.zeros((DEPTH - ROWS, LANES), F32)], axis=0)
        fields_t = jnp.transpose(fields)
        table[0 : 2 * LIST] = listed_t
        table[2 * LIST : 4 * LIST + 16] = fields_t[NEIGH : MISC + 16].astype(BF16)
        tiles = (total.astype(jnp.int32) + (LANES - 1)) // LANES

        def body(k, carry, start=start, total=total):
            place = iota((1, LANES), 1) + (k * LANES).astype(F32)
            hit = (off_ref[...] <= place) & (end_ref[...] > place)
            hit = hit.astype(F32).astype(BF16)
            hit = jnp.concatenate([hit, jnp.zeros((DEPTH - ROWS, LANES), BF16)], axis=0)
            got = mm(table[...], hit)
            misc = got[4 * LIST :]
            wanted = place - (256.0 * misc[0:1] + misc[1:2]) + 1.0
            chosen = (got[2 * LIST : 4 * LIST] == wanted).astype(F32)
            entry = jnp.sum(chosen * got[0 : 2 * LIST], axis=0, keepdims=True)
            slot = jnp.sum(chosen[LIST:], axis=0, keepdims=True)
            x, y, z = misc[2:3], misc[3:4], misc[4:5]
            far, shift, far_slot = far_coords(x, y, z, entry)
            valid = place < total
            away_i, away_j = away(x, y, z), away(*far)

            def where(flag, value):
                return jnp.where(flag, value, -1.0)

            def region(c):
                return (c[0] * 7.0 + c[1]) * 8.0 + c[2]

            def inner(c, s):
                return (((c[0] - 1.0) * 5.0 + (c[1] - 1.0)) * 5.0 + (c[2] - 1.0)) * 2.0 + s

            def own(c):
                return ((c[0] - 2.0) * 3.0 + (c[1] - 2.0)) * 8.0 + c[2]

            near = (x, y, z)
            lines = [
                where(valid, region(near)),
                slot,
                where(valid, region(far)),
                far_slot,
                where(valid & (away_i < 2.5), inner(near, slot)),
                where(valid & (away_j < 2.5), inner(far, far_slot)),
                where(valid & (away_i < 1.5), own(near)),
                where(valid & (away_j < 1.5), own(far)),
                valid.astype(F32),
                *shift,
                (valid & (away_i < 1.5)).astype(F32),
                jnp.zeros((3, LANES), F32),
            ]
            pairs_ref[start + k] = jnp.concatenate(lines, axis=0)
            return carry

        lax.fori_loop(0, tiles, body, jnp.int32(0))
        start = start + tiles
        counts.append(start)
    return counts


def turns(radius):
    part = radius * (1.0 / 12.0)
    part = part - jnp.floor(part + 0.5)
    half = part * math.pi
    sq = half * half
    s = jnp.full_like(sq, -1.0 / 39916800.0)
    for c in (1.0 / 362880.0, -1.0 / 5040.0, 1.0 / 120.0, -1.0 / 6.0, 1.0):
        s = s * sq + c
    s = s * half
    c = jnp.full_like(sq, 1.0 / 479001600.0)
    for k in (-1.0 / 3628800.0, 1.0 / 40320.0, -1.0 / 720.0, 1.0 / 24.0, -0.5, 1.0):
        c = c * sq + k
    return 2.0 * s * c, 1.0 - 2.0 * s * s


def evaluate(refs, scratch, counts, own_out):
    pos_t, pairs_ref, w1t, w1, wmt, wm, smt, sm, eo = refs
    env_ref, envs_ref, grad_ref, geo_ref, lat_ref, slope_ref, h_ref, wb_ref, hp_ref, en_ref = (
        scratch
    )
    front, every = counts
    norm = math.sqrt(2.0 / cutoff)

    env_ref[...] = jnp.zeros(env_ref.shape, F32)
    grad_ref[...] = jnp.zeros(grad_ref.shape, F32)
    en_ref[...] = jnp.zeros(en_ref.shape, F32)
    own_out[...] = jnp.zeros(own_out.shape, F32)

    def gathered(index, slot):
        got = mm(pos_t[...], one_hot(index, ROWS, DEPTH))
        full = got[0:8] + got[8:16] + got[16:24]
        second = slot > 0.5
        point = jnp.where(second, full[3:6], full[0:3])
        return point, jnp.where(second, full[7:8], full[6:7])

    def stage_one(t, carry):
        pair = pairs_ref[t]
        valid = pair[8:9]
        near, near_kind = gathered(pair[0:1], pair[1:2])
        far, far_kind = gathered(pair[2:3], pair[3:4])
        d = far - near + pair[9:12]
        square = jnp.sum(d * d, axis=0, keepdims=True)
        square = jnp.where(valid > 0.5, square, 1.0)
        radius = jnp.sqrt(square)
        inverse = 1.0 / radius
        u = d * inverse
        y = jnp.minimum(radius * (1.0 / cutoff), 1.0)
        y2 = y * y
        y5 = y2 * y2 * y
        f = 1.0 + y5 * y * (-28.0 + y * (48.0 - 21.0 * y))
        fd = y5 * (-168.0 + y * (336.0 - 168.0 * y)) * (1.0 / cutoff)
        sin1, cos1 = turns(radius)
        sines, cosines = [jnp.zeros_like(sin1), sin1], [jnp.ones_like(cos1), cos1]
        for _ in range(NB - 1):
            sines.append(2.0 * cos1 * sines[-1] - sines[-2])
            cosines.append(2.0 * cos1 * cosines[-1] - cosines[-2])
        basis = [norm * inverse * s for s in sines[1:]]
        slope = [
            norm * (k * (math.pi / cutoff)) * inverse * c - inverse * b
            for k, (c, b) in enumerate(zip(cosines[1:], basis), 1)
        ]
        kinds = [
            (near_kind == float(k)).astype(F32) + (far_kind == float(k)).astype(F32)
            for k in range(NSPEC)
        ]
        feats = jnp.concatenate(basis + kinds + [jnp.zeros((3, LANES), F32)], axis=0)
        geo_ref[t] = jnp.concatenate(
            [u, inverse, f, fd, jnp.zeros((2, LANES), F32)] + slope, axis=0
        )
        pre = mm(w1t[...], feats.astype(BF16))
        gate = sigmoid(pre)
        lat = (pre * gate).astype(BF16)
        lat_ref[t] = lat
        slope_ref[t] = gate * (1.0 + pre * (1.0 - gate))
        h = mm(wmt[...], lat)
        h_ref[t] = h
        w = h * (f * valid)
        hit_i = one_hot(pair[4:5], INNER, INNER)
        hit_j = one_hot(pair[5:6], INNER, INNER)
        high, low = split2(
            jnp.concatenate([w, w * u[0:1], w * u[1:2], w * u[2:3]], axis=0)
        )
        moments = jnp.concatenate([high, low], axis=1)
        plus, minus = hit_i + hit_j, hit_i - hit_j
        env_ref[0:CH] += mm_nt(moments[0:CH], jnp.concatenate([plus, plus], axis=1))
        env_ref[CH:] += mm_nt(moments[CH:], jnp.concatenate([minus, minus], axis=1))
        return carry

    lax.fori_loop(0, every, stage_one, jnp.int32(0))
    high, low = split2(env_ref[...])
    envs_ref[...] = jnp.concatenate([high, low], axis=1)

    def stage_two(t, carry):
        pair = pairs_ref[t]
        geo = geo_ref[t]
        valid = pair[8:9]
        u = geo[0:3]
        f = geo[4:5]
        hit = one_hot(pair[4:5], INNER, INNER)
        env = mm(envs_ref[...], jnp.concatenate([hit, hit], axis=0))
        aligned = (
            env[0:CH]
            + u[0:1] * env[CH : 2 * CH]
            + u[1:2] * env[2 * CH : 3 * CH]
            + u[2:3] * env[3 * CH :]
        )
        w = h_ref[t] * (f * valid)
        coupling = (env_scale * w * aligned).astype(BF16)
        arg = lat_ref[t].astype(F32) + mm(smt[...], coupling)
        gate = sigmoid(arg)
        hidden = arg * gate
        dotted = jnp.sum(hidden * eo[...], axis=0, keepdims=True)
        en_ref[0:1] += f * dotted * pair[12:13]
        arg_bar = (f * valid) * eo[...] * (gate * (1.0 + arg * (1.0 - gate)))
        arg_bar = arg_bar.astype(BF16)
        hp_ref[t] = arg_bar
        c_bar = mm(sm[...], arg_bar).astype(BF16).astype(F32)
        wb_ref[t] = env_scale * aligned * c_bar
        al_bar = env_scale * w * c_bar
        geo_ref[t, 6:7] = dotted * valid
        u_bar = [
            jnp.sum(al_bar * env[(k + 1) * CH : (k + 2) * CH], axis=0, keepdims=True)
            for k in range(3)
        ]
        pairs_ref[t, 13:16] = jnp.concatenate(u_bar, axis=0)
        high, low = split2(
            jnp.concatenate([al_bar, al_bar * u[0:1], al_bar * u[1:2], al_bar * u[2:3]], axis=0)
        )
        grad_ref[...] += mm_nt(
            jnp.concatenate([high, low], axis=1), jnp.concatenate([hit, hit], axis=1)
        )
        return carry

    lax.fori_loop(0, every, stage_two, jnp.int32(0))
    high, low = split2(grad_ref[...])
    envs_ref[...] = jnp.concatenate([high, low], axis=1)

    def stage_three(t, carry):
        pair = pairs_ref[t]
        geo = geo_ref[t]
        valid = pair[8:9]
        u, inverse, f, fd = geo[0:3], geo[3:4], geo[4:5], geo[5:6]
        hit_i = one_hot(pair[4:5], INNER, INNER)
        hit_j = one_hot(pair[5:6], INNER, INNER)
        plus, minus = hit_i + hit_j, hit_i - hit_j
        grad = envs_ref[...]
        g0 = mm(grad[0:CH], jnp.concatenate([plus, plus], axis=0))
        gv = mm(grad[CH:], jnp.concatenate([minus, minus], axis=0))
        parts = [gv[k * CH : (k + 1) * CH] for k in range(3)]
        h = h_ref[t]
        w = h * (f * valid)
        w_bar = wb_ref[t] + g0 + u[0:1] * parts[0] + u[1:2] * parts[1] + u[2:3] * parts[2]
        u_bar = pair[13:16] + jnp.concatenate(
            [jnp.sum(w * part, axis=0, keepdims=True) for part in parts], axis=0
        )
        f_bar = geo[6:7] + jnp.sum(h * w_bar, axis=0, keepdims=True)
        h_bar = (w_bar * (f * valid)).astype(BF16)
        lat_bar = (mm(wm[...], h_bar).astype(BF16) + hp_ref[t]).astype(F32)
        pre_bar = (lat_bar * slope_ref[t]).astype(BF16)
        basis_bar = mm(w1[...], pre_bar)[0:NB].astype(BF16).astype(F32)
        r_bar = jnp.sum(basis_bar * geo[8:16], axis=0, keepdims=True) + f_bar * fd
        along = jnp.sum(u * u_bar, axis=0, keepdims=True)
        d_bar = (r_bar * u + (u_bar - u * along) * inverse) * valid
        blank = jnp.zeros((2, LANES), F32)

        def slotted(values, slot):
            second = slot > 0.5
            return jnp.concatenate(
                [jnp.where(second, 0.0, values), jnp.where(second, values, 0.0), blank], axis=0
            )

        pulls = jnp.concatenate(
            [slotted(d_bar, pair[1:2]), slotted(-d_bar, pair[3:4])], axis=1
        )
        high, low = split2(jnp.concatenate([pulls, jnp.zeros((120, 2 * LANES), F32)], axis=0))
        where = jnp.concatenate([one_hot(pair[6:7], OWN, OWN), one_hot(pair[7:8], OWN, OWN)], axis=1)
        own_out[...] += mm_nt(where, high) + mm_nt(where, low)
        return carry

    lax.fori_loop(0, front, stage_three, jnp.int32(0))


def load_rows(rows_ref, low, own, high):
    rows_ref[0:ROWS] = jnp.zeros((ROWS, LANES), F32)
    for i in range(7):
        for piece, start, width in ((low, 0, 2), (own, 2, 3), (high, 5, 2)):
            for j in range(width):
                at = (i * 7 + start + j) * 8
                rows_ref[at : at + 8] = piece[i, j]


def own_rows(rows_ref):
    return jnp.concatenate(
        [rows_ref[(i * 7 + 2) * 8 : (i * 7 + 5) * 8] for i in range(2, 5)], axis=0
    )


def position_rows(rows_ref, pos_t):
    rows = jnp.concatenate([rows_ref[0:ROWS], jnp.zeros((DEPTH - ROWS, LANES), F32)], axis=0)
    turned = jnp.transpose(rows)
    top = turned[0:8]
    one = top.astype(BF16)
    rest = top - one.astype(F32)
    two = rest.astype(BF16)
    three = (rest - two.astype(F32)).astype(BF16)
    pos_t[...] = jnp.concatenate(
        [one.astype(F32), two.astype(F32), three.astype(F32), jnp.zeros((8, DEPTH), F32)], axis=0
    ).astype(BF16)
    return turned


def energy_rows(pair_energy, atom_energy, live):
    row = iota((8, LANES), 0)
    return jnp.where(row == 0.0, pair_energy, 0.0) + jnp.where(
        row == 1.0, atom_energy, 0.0
    ) + jnp.where(row == 2.0, live, 0.0)


def first_kernel(low, own, high, w1t, w1, wmt, wm, smt, sm, eo, table_energy,
                 force_out, moved_out, energy_out, pairs_ref, counts_ref,
                 rows_ref, table, off_ref, end_ref, pos_t, own_ref, *scratch):
    load_rows(rows_ref, low, own, high)
    turned = position_rows(rows_ref, pos_t)
    front, every = build_pairs(
        rows_ref, table, off_ref, end_ref, pairs_ref, turned[NEIGH:MISC].astype(BF16)
    )
    counts_ref[0] = front
    counts_ref[1] = every
    refs = (pos_t, pairs_ref, w1t, w1, wmt, wm, smt, sm, eo)
    evaluate(refs, scratch, (front, every), own_ref)
    mine = own_rows(rows_ref)
    lane = iota((72, LANES), 1)
    row = iota((72, LANES), 0)
    z = row - 8.0 * jnp.floor(row * 0.125)
    inside = (z > 1.5) & (z < 4.5)
    live3 = pltpu.roll(mine, LANES - LIVE3, 1)
    kind3 = pltpu.roll(mine, LANES - KIND3, 1)
    speed = pltpu.roll(mine, LANES - VEL, 1)
    force = own_ref[0:72] * live3
    force = jnp.where(inside & (lane < 6.0), force, 0.0)
    force_out[...] = force
    inverse_mass = jnp.zeros((72, LANES), F32)
    for k, mass in enumerate(atom_masses):
        inverse_mass = jnp.where(kind3 == float(k), 1.0 / mass, inverse_mass)
    moved = mine + time_step * speed + 0.5 * time_step * time_step * inverse_mass * force
    moved_out[...] = jnp.where(lane < 6.0, moved, jnp.where(lane < 8.0, mine, 0.0))
    live = pltpu.roll(mine, LANES - LIVE + KIND, 1)
    here = inside & (lane > 5.5) & (lane < 7.5)
    live = jnp.where(here, live, 0.0)
    atom = jnp.zeros((72, LANES), F32)
    for k in range(NSPEC):
        atom = jnp.where(mine == float(k), table_energy[k], atom)
    energy_out[...] = energy_rows(
        jnp.sum(scratch[-1][0:1]), jnp.sum(atom * live), jnp.sum(live)
    )


def second_kernel(low, own, high, w1t, w1, wmt, wm, smt, sm, eo, pairs_in, counts_ref, kept_in,
                  force_out, energy_out,
                  rows_ref, pos_t, own_ref, pairs_ref, *scratch):
    load_rows(rows_ref, low, own, high)
    position_rows(rows_ref, pos_t)
    front, every = counts_ref[0], counts_ref[1]
    pairs_ref[...] = pairs_in[...]
    refs = (pos_t, pairs_ref, w1t, w1, wmt, wm, smt, sm, eo)
    evaluate(refs, scratch, (front, every), own_ref)
    lane = iota((72, LANES), 1)
    row = iota((72, LANES), 0)
    z = row - 8.0 * jnp.floor(row * 0.125)
    force = own_ref[0:72] * kept_in[...]
    force_out[...] = jnp.where((z > 1.5) & (z < 4.5) & (lane < 6.0), force, 0.0)
    energy_out[...] = energy_rows(jnp.sum(scratch[-1][0:1]), 0.0, 0.0)


EVAL_SCRATCH = (
    pltpu.VMEM((4 * CH, INNER), F32),
    pltpu.VMEM((4 * CH, 2 * INNER), BF16),
    pltpu.VMEM((4 * CH, INNER), F32),
    pltpu.VMEM((TILES, 16, LANES), F32),
    pltpu.VMEM((TILES, LAT, LANES), BF16),
    pltpu.VMEM((TILES, LAT, LANES), F32),
    pltpu.VMEM((TILES, CH, LANES), F32),
    pltpu.VMEM((TILES, CH, LANES), F32),
    pltpu.VMEM((TILES, LAT, LANES), BF16),
    pltpu.VMEM((8, LANES), F32),
)
PARAMS = pltpu.CompilerParams(vmem_limit_bytes=20 * 2**20)
VM = pl.BlockSpec(memory_space=pltpu.VMEM)
SM = pl.BlockSpec(memory_space=pltpu.SMEM)


def first_call(pieces, weights, table_energy):
    return pl.pallas_call(
        first_kernel,
        name="first",
        out_shape=(
            jax.ShapeDtypeStruct((72, LANES), F32),
            jax.ShapeDtypeStruct((72, LANES), F32),
            jax.ShapeDtypeStruct((8, LANES), F32),
            jax.ShapeDtypeStruct((TILES, 16, LANES), F32),
            jax.ShapeDtypeStruct((2,), jnp.int32),
        ),
        in_specs=[VM] * (len(pieces) + len(weights)) + [SM],
        out_specs=(VM, VM, VM, VM, SM),
        scratch_shapes=(
            pltpu.VMEM((ROWS, LANES), F32),
            pltpu.VMEM((4 * LIST + 16, DEPTH), BF16),
            pltpu.VMEM((ROWS, LANES), F32),
            pltpu.VMEM((ROWS, LANES), F32),
            pltpu.VMEM((32, DEPTH), BF16),
            pltpu.VMEM((OWN, LANES), F32),
            *EVAL_SCRATCH,
        ),
        compiler_params=PARAMS,
    )(*pieces, *weights, table_energy)


def second_call(pieces, weights, pairs, counts, live3):
    return pl.pallas_call(
        second_kernel,
        name="second",
        out_shape=(
            jax.ShapeDtypeStruct((72, LANES), F32),
            jax.ShapeDtypeStruct((8, LANES), F32),
        ),
        in_specs=[VM] * (len(pieces) + len(weights) + 1) + [SM, VM],
        out_specs=(VM, VM),
        scratch_shapes=(
            pltpu.VMEM((ROWS, LANES), F32),
            pltpu.VMEM((32, DEPTH), BF16),
            pltpu.VMEM((OWN, LANES), F32),
            pltpu.VMEM((TILES, 16, LANES), F32),
            *EVAL_SCRATCH,
        ),
        compiler_params=PARAMS,
    )(*pieces, *weights, pairs, counts, live3)


def swap(low_part, high_part, axis):
    count = lax.axis_size(axis)
    forward = [(i, (i + 1) % count) for i in range(count)]
    backward = [(target, source) for source, target in forward]
    return lax.ppermute(high_part, axis, forward), lax.ppermute(low_part, axis, backward)


def spread(rows):
    low, high = swap(rows[:, :, 0:2], rows[:, :, 1:3], "gz")
    rows = jnp.concatenate([low, rows, high, jnp.zeros((3, 3, 1, LANES), F32)], axis=2)
    low, high = swap(rows[0:2], rows[1:3], "gx")
    rows = jnp.concatenate([low, rows, high], axis=0)
    low, high = swap(rows[:, 0:2], rows[:, 1:3], "gy")
    return low, rows, high


def pack(positions, velocity, species, region_count, neighbours):
    slots = lax.broadcasted_iota(jnp.int32, (3, 3, 3, 2), 3)
    live = (slots < region_count[..., None]).astype(F32)
    kind = species.astype(F32)
    lists = neighbours[..., :LIST].astype(F32).reshape(3, 3, 3, 2 * LIST)

    def thrice(v):
        return jnp.broadcast_to(v[..., None], (3, 3, 3, 2, 3)).reshape(3, 3, 3, 6)

    def vectors(v):
        return v.transpose(1, 2, 3, 4, 0).reshape(3, 3, 3, 6)

    def pad(count):
        return jnp.zeros((3, 3, 3, count), F32)

    return jnp.concatenate(
        [vectors(positions), kind, thrice(kind), pad(2), lists, vectors(velocity), pad(2),
         thrice(live), pad(2), live, pad(LANES - LIVE - 2)],
        axis=-1,
    ), thrice(live)


def unpack(force):
    own = force.reshape(3, 3, 8, LANES)[:, :, 2:5, 0:6]
    return own.reshape(3, 3, 3, 2, 3).transpose(4, 0, 1, 2, 3)


def shards(positions, velocity, species, region_count, neighbours,
           basis_weight, species_embed, weight_map, scalar_map, energy_out, species_energy):
    rows, live3 = pack(positions, velocity, species, region_count, neighbours)
    w1 = jnp.concatenate([basis_weight, species_embed, jnp.zeros((3, LAT), BF16)], axis=0)
    weights = (
        w1.T,
        w1,
        weight_map.T,
        weight_map,
        scalar_map.T,
        scalar_map,
        jnp.broadcast_to(energy_out[:, None], (LAT, LANES)),
    )
    live_rows = jnp.pad(live3, ((0, 0), (0, 0), (2, 3), (0, LANES - 6))).reshape(72, LANES)
    force_one, moved, energy_one, pairs, counts = first_call(
        spread(rows), weights, species_energy
    )
    moved = moved.reshape(3, 3, 8, LANES)[:, :, 2:5]
    force_two, energy_two = second_call(spread(moved), weights, pairs, counts, live_rows)
    partial = jnp.concatenate([energy_one[0:3, 0:1], energy_two[0:1, 0:1]], axis=0)
    for axis in ("gz", "gy", "gx"):
        partial = lax.psum(partial, axis)
    energy = jnp.stack([partial[0, 0] + partial[1, 0], partial[3, 0] + partial[1, 0]])
    forces = jnp.stack([unpack(force_one), unpack(force_two)])
    return forces, energy / partial[2, 0]


def solution(mesh):
    placed = (
        P(None, "gx", "gy", "gz", None),
        P(None, "gx", "gy", "gz", None),
        P("gx", "gy", "gz", None),
        P("gx", "gy", "gz"),
        P("gx", "gy", "gz", None, None),
        P(),
        P(),
        P(),
        P(),
        P(),
        P(),
    )
    return jax.shard_map(
        shards,
        mesh=mesh,
        in_specs=placed,
        out_specs=(P(None, None, "gx", "gy", "gz", None), P()),
        check_vma=False,
    )
```

time: 644 us -> 175 us (0.27)
  the two profiles are of different devices: /device:TPU:1 before, /device:TPU:192 now
where the time goes in v1:
time: 175 us; the launch traced here: 174 us
  blocking collectives  75.5 us (43%)
  starting transfers between devices  55.7 us (32%)
  Pallas kernels  17 us (10%)
  waiting for transfers between devices  10.3 us (6%)
  local copies, waits for them, and re-layouts  8.8 us (5%)
  between operations  3.58 us (2%)
  other arithmetic  3 us (2%)
    psum x3, blocking collectives, shards(): partial = lax.psum(partial, axis)  75.5 us
    ppermute x6, starting transfers between devices, swap(): lax.ppermute(low_part, axis, backward)  35.3 us
    ppermute x6, starting transfers between devices, swap(): lax.ppermute(high_part, axis, forward)  20.4 us
    ppermute x6, waiting for transfers between devices, swap(): lax.ppermute(low_part, axis, backward)  10.3 us
    pallas_call x1, Pallas kernels, first_call(): pl.pallas_call(first_kernel, name='first', out_shape=(jax.ShapeDtypeStruc...  9.9 us
    pallas_call x1, Pallas kernels, second_call(): pl.pallas_call(second_kernel, name='second', out_shape=(jax.ShapeDtypeStr...  7.08 us
    unnamed x24, local copies, waits for them, and re-layouts  5.74 us
  transfers between devices with their start and end apart: 12, of which 6 were waited for; matrix products, arithmetic and copies ran while one was open for 0% of the time, Pallas kernels for 0%

profile of v1, /device:TPU:192, one launch (start us, length us, event | category | flops | bytes accessed | tf_op | source)
XLA Modules:
  0.0 173.8 jit_solution(12389220327021042677)
XLA Ops:
  5.5 3.5 %collective-permute-start = (f32[3,3,2,128]{3,2,1,0:T(2,128)S(1)}, f32[3,3,2,128]{3,2,1,0:T(2,128)S(1)}, u32[]{:S(2)}, u32[]{:S(2)}) collective-permute-start(f32[3,3,2,128]{3,2,1,0:T(2,128)S(1)} %get-tuple-element.30), channel_id=1, source_target_pairs={{0,1},{1,2},{2,3},{3,4},{4,5},{5,6},{6,7},{7,0},{8,9},{9,10},{10,1... | collective-permute-start | bytes 27656 | tf_op jit(solution)/shard_map/ppermute | solution.py:517
  9.0 3.8 %collective-permute-start.1 = (f32[3,3,2,128]{3,2,1,0:T(2,128)S(1)}, f32[3,3,2,128]{3,2,1,0:T(2,128)S(1)}, u32[]{:S(2)}, u32[]{:S(2)}) collective-permute-start(f32[3,3,2,128]{3,2,1,0:T(2,128)S(1)} %get-tuple-element.31), channel_id=1, source_target_pairs={{1,0},{2,1},{3,2},{4,3},{5,4},{6,5},{7,6},{0,7},{9,8},{10,9},{11,1... | collective-permute-start | bytes 27656 | tf_op jit(solution)/shard_map/ppermute | solution.py:517
  12.9 1.6 collective-permute-done.1
  14.6 3.4 %collective-permute-start.2 = (f32[2,3,8,128]{3,2,1,0:T(8,128)S(1)}, f32[2,3,8,128]{3,2,1,0:T(8,128)S(1)}, u32[]{:S(2)}, u32[]{:S(2)}) collective-permute-start(f32[2,3,8,128]{3,2,1,0:T(8,128)S(1)} %get-tuple-element.28), channel_id=1, source_target_pairs={{0,64},{64,128},{128,192},{192,256},{256,320},{320,384},{384,448},... | collective-permute-start | bytes 73736 | tf_op jit(solution)/shard_map/ppermute | solution.py:517
  18.0 8.0 %collective-permute-start.3 = (f32[2,3,8,128]{3,2,1,0:T(8,128)S(1)}, f32[2,3,8,128]{3,2,1,0:T(8,128)S(1)}, u32[]{:S(2)}, u32[]{:S(2)}) collective-permute-start(f32[2,3,8,128]{3,2,1,0:T(8,128)S(1)} %get-tuple-element.29), channel_id=1, source_target_pairs={{64,0},{128,64},{192,128},{256,192},{320,256},{384,320},{448,384},... | collective-permute-start | bytes 73736 | tf_op jit(solution)/shard_map/ppermute | solution.py:517
  26.1 1.4 collective-permute-done.3
  27.6 1.9 %collective-permute-start.4 = (f32[7,2,8,128]{3,2,1,0:T(8,128)S(1)}, f32[7,2,8,128]{3,2,1,0:T(8,128)S(1)}, u32[]{:S(2)}, u32[]{:S(2)}) collective-permute-start(f32[7,2,8,128]{3,2,1,0:T(8,128)S(1)} %get-tuple-element.23), channel_id=1, source_target_pairs={{0,8},{8,16},{16,24},{24,32},{32,40},{40,48},{48,56},{56,0},{1,9},... | collective-permute-start | bytes 172040 | tf_op jit(solution)/shard_map/ppermute | solution.py:517
  29.5 5.4 %collective-permute-start.5 = (f32[7,2,8,128]{3,2,1,0:T(8,128)S(1)}, f32[7,2,8,128]{3,2,1,0:T(8,128)S(1)}, u32[]{:S(2)}, u32[]{:S(2)}) collective-permute-start(f32[7,2,8,128]{3,2,1,0:T(8,128)S(1)} %get-tuple-element.22), channel_id=1, source_target_pairs={{8,0},{16,8},{24,16},{32,24},{40,32},{48,40},{56,48},{0,56},{9,1},... | collective-permute-start | bytes 172040 | tf_op jit(solution)/shard_map/ppermute | solution.py:517
  36.6 1.5 collective-permute-done.5.high
  38.8 9.9 %first.1 = (f32[72,128]{1,0:T(8,128)S(1)}, f32[72,128]{1,0:T(8,128)S(1)}, f32[8,128]{1,0:T(8,128)S(1)}, f32[52,16,128]{2,1,0:T(8,128)S(1)}, s32[2]{0:T(128)S(1)}) custom-call(f32[7,2,8,128]{3,2,1,0:T(8,128)S(1)} %collective-permute-done.4.low, f32[7,3,8,128]{3,2,1,0:T(8,128)S(1)} %fusion.1.own, f32[7,2,8,128]{3,2,1,0:T(8,128)S(1)} %collective-permute-done.5.high, ...), custom_call_target="tpu_custom_call" | custom-call | tf_op jit(solution)/shard_map/first/pallas_call | solution.py:467
  48.8 3.5 %collective-permute-start.6 = (f32[3,3,2,128]{3,2,1,0:T(2,128)S(1)}, f32[3,3,2,128]{3,2,1,0:T(2,128)S(1)}, u32[]{:S(2)}, u32[]{:S(2)}) collective-permute-start(f32[3,3,2,128]{3,2,1,0:T(2,128)S(1)} %get-tuple-element.26), channel_id=1, source_target_pairs={{0,1},{1,2},{2,3},{3,4},{4,5},{5,6},{6,7},{7,0},{8,9},{9,10},{10,1... | collective-permute-start | bytes 27656 | tf_op jit(solution)/shard_map/ppermute | solution.py:517
  52.3 3.6 %collective-permute-start.7 = (f32[3,3,2,128]{3,2,1,0:T(2,128)S(1)}, f32[3,3,2,128]{3,2,1,0:T(2,128)S(1)}, u32[]{:S(2)}, u32[]{:S(2)}) collective-permute-start(f32[3,3,2,128]{3,2,1,0:T(2,128)S(1)} %get-tuple-element.27), channel_id=1, source_target_pairs={{1,0},{2,1},{3,2},{4,3},{5,4},{6,5},{7,6},{0,7},{9,8},{10,9},{11,1... | collective-permute-start | bytes 27656 | tf_op jit(solution)/shard_map/ppermute | solution.py:517
  55.9 2.3 %collective-permute-done.7 = f32[3,3,2,128]{3,2,1,0:T(2,128)S(1)} collective-permute-done((f32[3,3,2,128]{3,2,1,0:T(2,128)S(1)}, f32[3,3,2,128]{3,2,1,0:T(2,128)S(1)}, u32[]{:S(2)}, u32[]{:S(2)}) %collective-permute-start.7) | collective-permute-done | bytes 9248 | tf_op jit(solution)/shard_map/ppermute | solution.py:517
  58.2 1.9 %collective-permute-start.8 = (f32[2,3,8,128]{3,2,1,0:T(8,128)S(1)}, f32[2,3,8,128]{3,2,1,0:T(8,128)S(1)}, u32[]{:S(2)}, u32[]{:S(2)}) collective-permute-start(f32[2,3,8,128]{3,2,1,0:T(8,128)S(1)} %get-tuple-element.24), channel_id=1, source_target_pairs={{0,64},{64,128},{128,192},{192,256},{256,320},{320,384},{384,448},... | collective-permute-start | bytes 73736 | tf_op jit(solution)/shard_map/ppermute | solution.py:517
  60.1 12.6 %collective-permute-start.9 = (f32[2,3,8,128]{3,2,1,0:T(8,128)S(1)}, f32[2,3,8,128]{3,2,1,0:T(8,128)S(1)}, u32[]{:S(2)}, u32[]{:S(2)}) collective-permute-start(f32[2,3,8,128]{3,2,1,0:T(8,128)S(1)} %get-tuple-element.25), channel_id=1, source_target_pairs={{64,0},{128,64},{192,128},{256,192},{320,256},{384,320},{448,384},... | collective-permute-start | bytes 73736 | tf_op jit(solution)/shard_map/ppermute | solution.py:517
  72.7 1.5 collective-permute-done.9
  74.2 6.2 %collective-permute-start.10 = (f32[7,2,8,128]{3,2,1,0:T(8,128)S(1)}, f32[7,2,8,128]{3,2,1,0:T(8,128)S(1)}, u32[]{:S(2)}, u32[]{:S(2)}) collective-permute-start(f32[7,2,8,128]{3,2,1,0:T(8,128)S(1)} %get-tuple-element.21), channel_id=1, source_target_pairs={{0,8},{8,16},{16,24},{24,32},{32,40},{40,48},{48,56},{56,0},{1,9},... | collective-permute-start | bytes 172040 | tf_op jit(solution)/shard_map/ppermute | solution.py:517
  80.4 1.9 %collective-permute-start.11 = (f32[7,2,8,128]{3,2,1,0:T(8,128)S(1)}, f32[7,2,8,128]{3,2,1,0:T(8,128)S(1)}, u32[]{:S(2)}, u32[]{:S(2)}) collective-permute-start(f32[7,2,8,128]{3,2,1,0:T(8,128)S(1)} %get-tuple-element.20), channel_id=1, source_target_pairs={{8,0},{16,8},{24,16},{32,24},{40,32},{48,40},{56,48},{0,56},{9,1},... | collective-permute-start | bytes 172040 | tf_op jit(solution)/shard_map/ppermute | solution.py:517
  82.4 2.0 %collective-permute-done.11.high = f32[7,2,8,128]{3,2,1,0:T(8,128)S(1)} collective-permute-done((f32[7,2,8,128]{3,2,1,0:T(8,128)S(1)}, f32[7,2,8,128]{3,2,1,0:T(8,128)S(1)}, u32[]{:S(2)}, u32[]{:S(2)}) %collective-permute-start.11) | collective-permute-done | bytes 57376 | tf_op jit(solution)/shard_map/ppermute | solution.py:517
  84.4 7.1 %second.1 = (f32[72,128]{1,0:T(8,128)S(1)}, f32[8,128]{1,0:T(8,128)S(1)}) custom-call(f32[7,2,8,128]{3,2,1,0:T(8,128)S(1)} %collective-permute-done.10.low, f32[7,3,8,128]{3,2,1,0:T(8,128)S(1)} %fusion.3.own, f32[7,2,8,128]{3,2,1,0:T(8,128)S(1)} %collective-permute-done.11.high, bf16[128,16]{1,0:T(8,128)(2,1)S(1)} %copy.34.w1t, ...), custom_call_target="tpu_custom_call" | custom-call | tf_op jit(solution)/shard_map/second/pallas_call | solution.py:493
  92.7 17.7 %psum.21 = f32[4,1]{0,1:T(1,128)S(1)} all-reduce(f32[4,1]{0,1:T(1,128)S(1)} %pad_maximum_fusion.5), channel_id=1, replica_groups=mesh['gx'=12,'gy'=8,'gz'=8] {'gz'}, use_global_device_ids=true, to_apply=%region_0.1 | all-reduce | flops 4 | bytes 32 | tf_op jit(solution)/shard_map/psum | solution.py:577
  110.4 16.3 %psum.22 = f32[4,1]{0,1:T(1,128)S(1)} all-reduce(f32[4,1]{0,1:T(1,128)S(1)} %psum.21), channel_id=1, replica_groups=mesh['gx'=12,'gy'=8,'gz'=8] {'gy'}, use_global_device_ids=true, to_apply=%region_1.2 | all-reduce | flops 4 | bytes 32 | tf_op jit(solution)/shard_map/psum | solution.py:577
  126.8 41.5 %psum.23 = f32[4,1]{0,1:T(1,128)S(1)} all-reduce(f32[4,1]{0,1:T(1,128)S(1)} %psum.22), channel_id=1, replica_groups=mesh['gx'=12,'gy'=8,'gz'=8] {'gx'}, use_global_device_ids=true, to_apply=%region_2.3 | all-reduce | flops 4 | bytes 32 | tf_op jit(solution)/shard_map/psum | solution.py:577
  172.6 1.2 maximum_divide_fusion
  (74 shorter events, 10.6 us)
Async XLA Ops:
  1.5 0.7 copy-start.6
  2.4 0.8 copy-start.3
  3.4 0.7 copy-start.4
  4.2 0.7 copy-start.5
  5.5 7.4 %collective-permute-start = (f32[3,3,2,128]{3,2,1,0:T(2,128)S(1)}, f32[3,3,2,128]{3,2,1,0:T(2,128)S(1)}, u32[]{:S(2)}, u32[]{:S(2)}) collective-permute-start(f32[3,3,2,128]{3,2,1,0:T(2,128)S(1)} %get-tuple-element.30), channel_id=1, source_target_pairs={{0,1},{1,2},{2,3},{3,4},{4,5},{5,6},{6,7},{7,0},{8,9},{9,10},{10,1... | collective-permute-start | bytes 27656 | tf_op jit(solution)/shard_map/ppermute | solution.py:517
  9.0 5.6 %collective-permute-start.1 = (f32[3,3,2,128]{3,2,1,0:T(2,128)S(1)}, f32[3,3,2,128]{3,2,1,0:T(2,128)S(1)}, u32[]{:S(2)}, u32[]{:S(2)}) collective-permute-start(f32[3,3,2,128]{3,2,1,0:T(2,128)S(1)} %get-tuple-element.31), channel_id=1, source_target_pairs={{1,0},{2,1},{3,2},{4,3},{5,4},{6,5},{7,6},{0,7},{9,8},{10,9},{11,1... | collective-permute-start | bytes 27656 | tf_op jit(solution)/shard_map/ppermute | solution.py:517
  14.6 11.5 %copy-start.8 = (bf16[8,128]{1,0:T(8,128)(2,1)S(1)}, bf16[8,128]{1,0:T(8,128)(2,1)}, u32[]{:S(2)}) copy-start(bf16[8,128]{1,0:T(8,128)(2,1)} %param.16) | copy-start | bytes 6148
  14.6 11.5 %copy-start.7 = (bf16[5,128]{1,0:T(8,128)(2,1)S(1)}, bf16[5,128]{1,0:T(8,128)(2,1)}, u32[]{:S(2)}) copy-start(bf16[5,128]{1,0:T(8,128)(2,1)} %param.17) | copy-start | bytes 3844
  14.6 11.5 %collective-permute-start.2 = (f32[2,3,8,128]{3,2,1,0:T(8,128)S(1)}, f32[2,3,8,128]{3,2,1,0:T(8,128)S(1)}, u32[]{:S(2)}, u32[]{:S(2)}) collective-permute-start(f32[2,3,8,128]{3,2,1,0:T(8,128)S(1)} %get-tuple-element.28), channel_id=1, source_target_pairs={{0,64},{64,128},{128,192},{192,256},{256,320},{320,384},{384,448},... | collective-permute-start | bytes 73736 | tf_op jit(solution)/shard_map/ppermute | solution.py:517
  18.0 9.5 %collective-permute-start.3 = (f32[2,3,8,128]{3,2,1,0:T(8,128)S(1)}, f32[2,3,8,128]{3,2,1,0:T(8,128)S(1)}, u32[]{:S(2)}, u32[]{:S(2)}) collective-permute-start(f32[2,3,8,128]{3,2,1,0:T(8,128)S(1)} %get-tuple-element.29), channel_id=1, source_target_pairs={{64,0},{128,64},{192,128},{256,192},{320,256},{384,320},{448,384},... | collective-permute-start | bytes 73736 | tf_op jit(solution)/shard_map/ppermute | solution.py:517
  27.6 9.0 %collective-permute-start.4 = (f32[7,2,8,128]{3,2,1,0:T(8,128)S(1)}, f32[7,2,8,128]{3,2,1,0:T(8,128)S(1)}, u32[]{:S(2)}, u32[]{:S(2)}) collective-permute-start(f32[7,2,8,128]{3,2,1,0:T(8,128)S(1)} %get-tuple-element.23), channel_id=1, source_target_pairs={{0,8},{8,16},{16,24},{24,32},{32,40},{40,48},{48,56},{56,0},{1,9},... | collective-permute-start | bytes 172040 | tf_op jit(solution)/shard_map/ppermute | solution.py:517
  29.5 8.6 %collective-permute-start.5 = (f32[7,2,8,128]{3,2,1,0:T(8,128)S(1)}, f32[7,2,8,128]{3,2,1,0:T(8,128)S(1)}, u32[]{:S(2)}, u32[]{:S(2)}) collective-permute-start(f32[7,2,8,128]{3,2,1,0:T(8,128)S(1)} %get-tuple-element.22), channel_id=1, source_target_pairs={{8,0},{16,8},{24,16},{32,24},{40,32},{48,40},{56,48},{0,56},{9,1},... | collective-permute-start | bytes 172040 | tf_op jit(solution)/shard_map/ppermute | solution.py:517
  35.0 0.7 copy-start.1
  35.7 0.7 copy-start
  36.5 1.6 copy-start.9
  38.2 0.7 copy-start.2
  48.8 7.1 %collective-permute-start.6 = (f32[3,3,2,128]{3,2,1,0:T(2,128)S(1)}, f32[3,3,2,128]{3,2,1,0:T(2,128)S(1)}, u32[]{:S(2)}, u32[]{:S(2)}) collective-permute-start(f32[3,3,2,128]{3,2,1,0:T(2,128)S(1)} %get-tuple-element.26), channel_id=1, source_target_pairs={{0,1},{1,2},{2,3},{3,4},{4,5},{5,6},{6,7},{7,0},{8,9},{9,10},{10,1... | collective-permute-start | bytes 27656 | tf_op jit(solution)/shard_map/ppermute | solution.py:517
  52.3 5.9 %collective-permute-start.7 = (f32[3,3,2,128]{3,2,1,0:T(2,128)S(1)}, f32[3,3,2,128]{3,2,1,0:T(2,128)S(1)}, u32[]{:S(2)}, u32[]{:S(2)}) collective-permute-start(f32[3,3,2,128]{3,2,1,0:T(2,128)S(1)} %get-tuple-element.27), channel_id=1, source_target_pairs={{1,0},{2,1},{3,2},{4,3},{5,4},{6,5},{7,6},{0,7},{9,8},{10,9},{11,1... | collective-permute-start | bytes 27656 | tf_op jit(solution)/shard_map/ppermute | solution.py:517
  58.2 14.5 %collective-permute-start.8 = (f32[2,3,8,128]{3,2,1,0:T(8,128)S(1)}, f32[2,3,8,128]{3,2,1,0:T(8,128)S(1)}, u32[]{:S(2)}, u32[]{:S(2)}) collective-permute-start(f32[2,3,8,128]{3,2,1,0:T(8,128)S(1)} %get-tuple-element.24), channel_id=1, source_target_pairs={{0,64},{64,128},{128,192},{192,256},{256,320},{320,384},{384,448},... | collective-permute-start | bytes 73736 | tf_op jit(solution)/shard_map/ppermute | solution.py:517
  60.1 14.1 %collective-permute-start.9 = (f32[2,3,8,128]{3,2,1,0:T(8,128)S(1)}, f32[2,3,8,128]{3,2,1,0:T(8,128)S(1)}, u32[]{:S(2)}, u32[]{:S(2)}) collective-permute-start(f32[2,3,8,128]{3,2,1,0:T(8,128)S(1)} %get-tuple-element.25), channel_id=1, source_target_pairs={{64,0},{128,64},{192,128},{256,192},{320,256},{384,320},{448,384},... | collective-permute-start | bytes 73736 | tf_op jit(solution)/shard_map/ppermute | solution.py:517
  74.2 8.2 %collective-permute-start.10 = (f32[7,2,8,128]{3,2,1,0:T(8,128)S(1)}, f32[7,2,8,128]{3,2,1,0:T(8,128)S(1)}, u32[]{:S(2)}, u32[]{:S(2)}) collective-permute-start(f32[7,2,8,128]{3,2,1,0:T(8,128)S(1)} %get-tuple-element.21), channel_id=1, source_target_pairs={{0,8},{8,16},{16,24},{24,32},{32,40},{40,48},{48,56},{56,0},{1,9},... | collective-permute-start | bytes 172040 | tf_op jit(solution)/shard_map/ppermute | solution.py:517
  80.4 4.0 %collective-permute-start.11 = (f32[7,2,8,128]{3,2,1,0:T(8,128)S(1)}, f32[7,2,8,128]{3,2,1,0:T(8,128)S(1)}, u32[]{:S(2)}, u32[]{:S(2)}) collective-permute-start(f32[7,2,8,128]{3,2,1,0:T(8,128)S(1)} %get-tuple-element.20), channel_id=1, source_target_pairs={{8,0},{16,8},{24,16},{32,24},{40,32},{48,40},{56,48},{0,56},{9,1},... | collective-permute-start | bytes 172040 | tf_op jit(solution)/shard_map/ppermute | solution.py:517

commit v2 on v1

--- a/solution.py
+++ b/solution.py
@@ -383,11 +383,11 @@
     return turned
 
 
-def energy_rows(pair_energy, atom_energy, live):
-    row = iota((8, LANES), 0)
-    return jnp.where(row == 0.0, pair_energy, 0.0) + jnp.where(
-        row == 1.0, atom_energy, 0.0
-    ) + jnp.where(row == 2.0, live, 0.0)
+def energy_row(first, second, live):
+    lane = iota((1, LANES), 1)
+    return jnp.where(lane == 0.0, first, 0.0) + jnp.where(lane == 1.0, second, 0.0) + jnp.where(
+        lane == 2.0, live, 0.0
+    )
 
 
 def first_kernel(low, own, high, w1t, w1, wmt, wm, smt, sm, eo, table_energy,
@@ -424,12 +424,11 @@
     atom = jnp.zeros((72, LANES), F32)
     for k in range(NSPEC):
         atom = jnp.where(mine == float(k), table_energy[k], atom)
-    energy_out[...] = energy_rows(
-        jnp.sum(scratch[-1][0:1]), jnp.sum(atom * live), jnp.sum(live)
-    )
-
-
-def second_kernel(low, own, high, w1t, w1, wmt, wm, smt, sm, eo, pairs_in, counts_ref, kept_in,
+    atoms = jnp.sum(atom * live)
+    energy_out[...] = energy_row(jnp.sum(scratch[-1][0:1]) + atoms, atoms, jnp.sum(live))
+
+
+def second_kernel(low, own, high, w1t, w1, wmt, wm, smt, sm, eo, pairs_in, counts_ref, kept_in, energy_in,
                   force_out, energy_out,
                   rows_ref, pos_t, own_ref, pairs_ref, *scratch):
     load_rows(rows_ref, low, own, high)
@@ -443,7 +442,7 @@
     z = row - 8.0 * jnp.floor(row * 0.125)
     force = own_ref[0:72] * kept_in[...]
     force_out[...] = jnp.where((z > 1.5) & (z < 4.5) & (lane < 6.0), force, 0.0)
-    energy_out[...] = energy_rows(jnp.sum(scratch[-1][0:1]), 0.0, 0.0)
+    energy_out[...] = energy_in[...] + energy_row(0.0, jnp.sum(scratch[-1][0:1]), 0.0)
 
 
 EVAL_SCRATCH = (
@@ -470,7 +469,7 @@
         out_shape=(
             jax.ShapeDtypeStruct((72, LANES), F32),
             jax.ShapeDtypeStruct((72, LANES), F32),
-            jax.ShapeDtypeStruct((8, LANES), F32),
+            jax.ShapeDtypeStruct((1, LANES), F32),
             jax.ShapeDtypeStruct((TILES, 16, LANES), F32),
             jax.ShapeDtypeStruct((2,), jnp.int32),
         ),
@@ -489,15 +488,15 @@
     )(*pieces, *weights, table_energy)
 
 
-def second_call(pieces, weights, pairs, counts, live3):
+def second_call(pieces, weights, pairs, counts, live3, energy):
     return pl.pallas_call(
         second_kernel,
         name="second",
         out_shape=(
             jax.ShapeDtypeStruct((72, LANES), F32),
-            jax.ShapeDtypeStruct((8, LANES), F32),
+            jax.ShapeDtypeStruct((1, LANES), F32),
         ),
-        in_specs=[VM] * (len(pieces) + len(weights) + 1) + [SM, VM],
+        in_specs=[VM] * (len(pieces) + len(weights) + 1) + [SM, VM, VM],
         out_specs=(VM, VM),
         scratch_shapes=(
             pltpu.VMEM((ROWS, LANES), F32),
@@ -507,14 +506,26 @@
             *EVAL_SCRATCH,
         ),
         compiler_params=PARAMS,
-    )(*pieces, *weights, pairs, counts, live3)
+    )(*pieces, *weights, pairs, counts, live3, energy)
 
 
 def swap(low_part, high_part, axis):
     count = lax.axis_size(axis)
-    forward = [(i, (i + 1) % count) for i in range(count)]
-    backward = [(target, source) for source, target in forward]
-    return lax.ppermute(high_part, axis, forward), lax.ppermute(low_part, axis, backward)
+    even = lax.axis_index(axis) % 2 == 0
+    inner = [(i, i ^ 1) for i in range(count)]
+    outer = [(i, (i - 1) % count if i % 2 == 0 else (i + 1) % count) for i in range(count)]
+    with jax.named_scope("outer"):
+        across = lax.ppermute(jnp.where(even, low_part, high_part), axis, outer)
+    with jax.named_scope("inner"):
+        within = lax.ppermute(jnp.where(even, high_part, low_part), axis, inner)
+    return jnp.where(even, across, within), jnp.where(even, within, across)
+
+
+def everywhere(row, axes):
+    count = math.prod(lax.axis_size(axis) for axis in axes)
+    rows = jnp.broadcast_to(row[None], (count, 1, LANES))
+    rows = lax.all_to_all(rows, axes, 0, 0, tiled=False)
+    return jnp.sum(rows, axis=0)
 
 
 def spread(rows):
@@ -571,13 +582,12 @@
         spread(rows), weights, species_energy
     )
     moved = moved.reshape(3, 3, 8, LANES)[:, :, 2:5]
-    force_two, energy_two = second_call(spread(moved), weights, pairs, counts, live_rows)
-    partial = jnp.concatenate([energy_one[0:3, 0:1], energy_two[0:1, 0:1]], axis=0)
-    for axis in ("gz", "gy", "gx"):
-        partial = lax.psum(partial, axis)
-    energy = jnp.stack([partial[0, 0] + partial[1, 0], partial[3, 0] + partial[1, 0]])
+    force_two, energies = second_call(
+        spread(moved), weights, pairs, counts, live_rows, energy_one
+    )
+    totals = everywhere(everywhere(energies, ("gx", "gy")), ("gz",))
     forces = jnp.stack([unpack(force_one), unpack(force_two)])
-    return forces, energy / partial[2, 0]
+    return forces, totals[0, 0:2] / totals[0, 2]
 
 
 def solution(mesh):

time: 175 us -> 136 us (0.78)
  the two profiles are of different devices: /device:TPU:192 before, /device:TPU:1 now
where the time goes in v2:
time: 136 us; the launch traced here: 134 us
  starting transfers between devices  76.9 us (57%)
  waiting for transfers between devices  27.3 us (20%)
  Pallas kernels  17 us (12%)
  local copies, waits for them, and re-layouts  10.7 us (8%)
  other arithmetic  1.61 us (1%)
    ppermute x6, starting transfers between devices, swap(): across = lax.ppermute(jnp.where(even, low_part, high_part), axis, outer)  45.4 us
    all_to_all x2, starting transfers between devices, everywhere(): rows = lax.all_to_all(rows, axes, 0, 0, tiled=False)  18.4 us
    all_to_all x2, waiting for transfers between devices, everywhere(): rows = lax.all_to_all(rows, axes, 0, 0, tiled=False)  17.1 us
    ppermute x6, starting transfers between devices, swap(): within = lax.ppermute(jnp.where(even, high_part, low_part), axis, inner)  13.2 us
    ppermute x6, waiting for transfers between devices, swap(): within = lax.ppermute(jnp.where(even, high_part, low_part), axis, inner)  9.97 us
    pallas_call x1, Pallas kernels, first_call(): pl.pallas_call(first_kernel, name='first', out_shape=(jax.ShapeDtypeStruc...  9.9 us
    pallas_call x1, Pallas kernels, second_call(): pl.pallas_call(second_kernel, name='second', out_shape=(jax.ShapeDtypeStr...  7.07 us
    unnamed x26, local copies, waits for them, and re-layouts  7.06 us
  transfers between devices with their start and end apart: 14, of which 8 were waited for; matrix products, arithmetic and copies ran while one was open for 1% of the time, Pallas kernels for 0%

profile of v2, /device:TPU:1, one launch (start us, length us, event | category | flops | bytes accessed | tf_op | source)
XLA Modules:
  0.0 134.5 jit_solution(5212227613577399795)
XLA Ops:
  5.5 5.9 %collective-permute-start = (f32[3,3,2,128]{3,2,1,0:T(2,128)S(1)}, f32[3,3,2,128]{3,2,1,0:T(2,128)S(1)}, u32[]{:S(2)}, u32[]{:S(2)}) collective-permute-start(f32[3,3,2,128]{3,2,1,0:T(2,128)S(1)} %get-tuple-element.44), channel_id=1, source_target_pairs={{0,7},{1,2},{2,1},{3,4},{4,3},{5,6},{6,5},{7,0},{8,15},{9,10},{10,... | collective-permute-start | bytes 27656 | tf_op jit(solution)/shard_map/outer/ppermute | solution.py:518
  11.4 1.9 %collective-permute-start.1 = (f32[3,3,2,128]{3,2,1,0:T(2,128)S(1)}, f32[3,3,2,128]{3,2,1,0:T(2,128)S(1)}, u32[]{:S(2)}, u32[]{:S(2)}) collective-permute-start(f32[3,3,2,128]{3,2,1,0:T(2,128)S(1)} %get-tuple-element.45), channel_id=1, source_target_pairs={{0,1},{1,0},{2,3},{3,2},{4,5},{5,4},{6,7},{7,6},{8,9},{9,8},{10,11... | collective-permute-start | bytes 27656 | tf_op jit(solution)/shard_map/inner/ppermute | solution.py:520
  13.5 2.4 %collective-permute-done.1 = f32[3,3,2,128]{3,2,1,0:T(2,128)S(1)} collective-permute-done((f32[3,3,2,128]{3,2,1,0:T(2,128)S(1)}, f32[3,3,2,128]{3,2,1,0:T(2,128)S(1)}, u32[]{:S(2)}, u32[]{:S(2)}) %collective-permute-start.1) | collective-permute-done | bytes 9248 | tf_op jit(solution)/shard_map/inner/ppermute | solution.py:520
  15.9 8.0 %collective-permute-start.2 = (f32[2,3,8,128]{3,2,1,0:T(8,128)S(1)}, f32[2,3,8,128]{3,2,1,0:T(8,128)S(1)}, u32[]{:S(2)}, u32[]{:S(2)}) collective-permute-start(f32[2,3,8,128]{3,2,1,0:T(8,128)S(1)} %get-tuple-element.38), channel_id=1, source_target_pairs={{0,704},{64,128},{128,64},{192,256},{256,192},{320,384},{384,320},... | collective-permute-start | bytes 73736 | tf_op jit(solution)/shard_map/outer/ppermute | solution.py:518
  23.9 1.9 %collective-permute-start.3 = (f32[2,3,8,128]{3,2,1,0:T(8,128)S(1)}, f32[2,3,8,128]{3,2,1,0:T(8,128)S(1)}, u32[]{:S(2)}, u32[]{:S(2)}) collective-permute-start(f32[2,3,8,128]{3,2,1,0:T(8,128)S(1)} %get-tuple-element.39), channel_id=1, source_target_pairs={{0,64},{64,0},{128,192},{192,128},{256,320},{320,256},{384,448},{4... | collective-permute-start | bytes 73736 | tf_op jit(solution)/shard_map/inner/ppermute | solution.py:520
  26.0 2.5 %collective-permute-done.3 = f32[2,3,8,128]{3,2,1,0:T(8,128)S(1)} collective-permute-done((f32[2,3,8,128]{3,2,1,0:T(8,128)S(1)}, f32[2,3,8,128]{3,2,1,0:T(8,128)S(1)}, u32[]{:S(2)}, u32[]{:S(2)}) %collective-permute-start.3) | collective-permute-done | bytes 24608 | tf_op jit(solution)/shard_map/inner/ppermute | solution.py:520
  28.6 12.2 %collective-permute-start.4 = (f32[7,2,8,128]{3,2,1,0:T(8,128)S(1)}, f32[7,2,8,128]{3,2,1,0:T(8,128)S(1)}, u32[]{:S(2)}, u32[]{:S(2)}) collective-permute-start(f32[7,2,8,128]{3,2,1,0:T(8,128)S(1)} %get-tuple-element.29), channel_id=1, source_target_pairs={{0,56},{8,16},{16,8},{24,32},{32,24},{40,48},{48,40},{56,0},{1,57}... | collective-permute-start | bytes 172040 | tf_op jit(solution)/shard_map/outer/ppermute | solution.py:518
  40.8 2.5 %collective-permute-start.5 = (f32[7,2,8,128]{3,2,1,0:T(8,128)S(1)}, f32[7,2,8,128]{3,2,1,0:T(8,128)S(1)}, u32[]{:S(2)}, u32[]{:S(2)}) collective-permute-start(f32[7,2,8,128]{3,2,1,0:T(8,128)S(1)} %get-tuple-element.28), channel_id=1, source_target_pairs={{0,8},{8,0},{16,24},{24,16},{32,40},{40,32},{48,56},{56,48},{1,9},... | collective-permute-start | bytes 172040 | tf_op jit(solution)/shard_map/inner/ppermute | solution.py:520
  46.4 9.9 %first.1 = (f32[72,128]{1,0:T(8,128)S(1)}, f32[72,128]{1,0:T(8,128)S(1)}, f32[1,128]{1,0:T(1,128)S(1)}, f32[52,16,128]{2,1,0:T(8,128)S(1)}, s32[2]{0:T(128)S(1)}) custom-call(f32[7,2,8,128]{3,2,1,0:T(8,128)S(1)} %get-tuple-element.25.low, f32[7,3,8,128]{3,2,1,0:T(8,128)S(1)} %fusion.1.own, f32[7,2,8,128]{3,2,1,0:T(8,128)S(1)} %get-tuple-element.24.high, ...), custom_call_target="tpu_custom_call" | custom-call | tf_op jit(solution)/shard_map/first/pallas_call | solution.py:466
  56.4 2.6 %collective-permute-start.6 = (f32[3,3,2,128]{3,2,1,0:T(2,128)S(1)}, f32[3,3,2,128]{3,2,1,0:T(2,128)S(1)}, u32[]{:S(2)}, u32[]{:S(2)}) collective-permute-start(f32[3,3,2,128]{3,2,1,0:T(2,128)S(1)} %get-tuple-element.36), channel_id=1, source_target_pairs={{0,7},{1,2},{2,1},{3,4},{4,3},{5,6},{6,5},{7,0},{8,15},{9,10},{10,... | collective-permute-start | bytes 27656 | tf_op jit(solution)/shard_map/outer/ppermute | solution.py:518
  59.0 2.9 %collective-permute-start.7 = (f32[3,3,2,128]{3,2,1,0:T(2,128)S(1)}, f32[3,3,2,128]{3,2,1,0:T(2,128)S(1)}, u32[]{:S(2)}, u32[]{:S(2)}) collective-permute-start(f32[3,3,2,128]{3,2,1,0:T(2,128)S(1)} %get-tuple-element.37), channel_id=1, source_target_pairs={{0,1},{1,0},{2,3},{3,2},{4,5},{5,4},{6,7},{7,6},{8,9},{9,8},{10,11... | collective-permute-start | bytes 27656 | tf_op jit(solution)/shard_map/inner/ppermute | solution.py:520
  62.0 1.4 %collective-permute-done.7 = f32[3,3,2,128]{3,2,1,0:T(2,128)S(1)} collective-permute-done((f32[3,3,2,128]{3,2,1,0:T(2,128)S(1)}, f32[3,3,2,128]{3,2,1,0:T(2,128)S(1)}, u32[]{:S(2)}, u32[]{:S(2)}) %collective-permute-start.7) | collective-permute-done | bytes 9248 | tf_op jit(solution)/shard_map/inner/ppermute | solution.py:520
  63.5 7.0 %collective-permute-start.8 = (f32[2,3,8,128]{3,2,1,0:T(8,128)S(1)}, f32[2,3,8,128]{3,2,1,0:T(8,128)S(1)}, u32[]{:S(2)}, u32[]{:S(2)}) collective-permute-start(f32[2,3,8,128]{3,2,1,0:T(8,128)S(1)} %get-tuple-element.34), channel_id=1, source_target_pairs={{0,704},{64,128},{128,64},{192,256},{256,192},{320,384},{384,320},... | collective-permute-start | bytes 73736 | tf_op jit(solution)/shard_map/outer/ppermute | solution.py:518
  70.5 1.9 %collective-permute-start.9 = (f32[2,3,8,128]{3,2,1,0:T(8,128)S(1)}, f32[2,3,8,128]{3,2,1,0:T(8,128)S(1)}, u32[]{:S(2)}, u32[]{:S(2)}) collective-permute-start(f32[2,3,8,128]{3,2,1,0:T(8,128)S(1)} %get-tuple-element.35), channel_id=1, source_target_pairs={{0,64},{64,0},{128,192},{192,128},{256,320},{320,256},{384,448},{4... | collective-permute-start | bytes 73736 | tf_op jit(solution)/shard_map/inner/ppermute | solution.py:520
  72.4 2.6 %collective-permute-done.9 = f32[2,3,8,128]{3,2,1,0:T(8,128)S(1)} collective-permute-done((f32[2,3,8,128]{3,2,1,0:T(8,128)S(1)}, f32[2,3,8,128]{3,2,1,0:T(8,128)S(1)}, u32[]{:S(2)}, u32[]{:S(2)}) %collective-permute-start.9) | collective-permute-done | bytes 24608 | tf_op jit(solution)/shard_map/inner/ppermute | solution.py:520
  75.1 9.5 %collective-permute-start.10 = (f32[7,2,8,128]{3,2,1,0:T(8,128)S(1)}, f32[7,2,8,128]{3,2,1,0:T(8,128)S(1)}, u32[]{:S(2)}, u32[]{:S(2)}) collective-permute-start(f32[7,2,8,128]{3,2,1,0:T(8,128)S(1)} %get-tuple-element.27), channel_id=1, source_target_pairs={{0,56},{8,16},{16,8},{24,32},{32,24},{40,48},{48,40},{56,0},{1,57}... | collective-permute-start | bytes 172040 | tf_op jit(solution)/shard_map/outer/ppermute | solution.py:518
  84.7 1.9 %collective-permute-start.11 = (f32[7,2,8,128]{3,2,1,0:T(8,128)S(1)}, f32[7,2,8,128]{3,2,1,0:T(8,128)S(1)}, u32[]{:S(2)}, u32[]{:S(2)}) collective-permute-start(f32[7,2,8,128]{3,2,1,0:T(8,128)S(1)} %get-tuple-element.26), channel_id=1, source_target_pairs={{0,8},{8,0},{16,24},{24,16},{32,40},{40,32},{48,56},{56,48},{1,9},... | collective-permute-start | bytes 172040 | tf_op jit(solution)/shard_map/inner/ppermute | solution.py:520
  86.8 1.0 collective-permute-done.11
  87.8 7.1 %second.1 = (f32[72,128]{1,0:T(8,128)S(1)}, f32[1,128]{1,0:T(1,128)S(1)}) custom-call(f32[7,2,8,128]{3,2,1,0:T(8,128)S(1)} %get-tuple-element.23.low, f32[7,3,8,128]{3,2,1,0:T(8,128)S(1)} %fusion.3.own, f32[7,2,8,128]{3,2,1,0:T(8,128)S(1)} %get-tuple-element.22.high, bf16[128,16]{1,0:T(8,128)(2,1)S(1)} %copy.43.w1t, ...), custom_call_target="tpu_custom_call" | custom-call | tf_op jit(solution)/shard_map/second/pallas_call | solution.py:492
  95.5 14.9 %all-to-all-start = ((f32[96,1,128]{2,1,0:T(1,128)}), f32[96,1,128]{2,1,0:T(1,128)S(1)}, u32[]{:S(2)}, u32[]{:S(2)}) async-start(f32[96,1,128]{2,1,0:T(1,128)} %broadcast_in_dim.22), calls=%async_computation | async-start | bytes 98304 | tf_op jit(solution)/shard_map/all_to_all | solution.py:527
  110.7 11.5 %all-to-all-done = f32[96,1,128]{2,1,0:T(1,128)S(1)} async-done(((f32[96,1,128]{2,1,0:T(1,128)}), f32[96,1,128]{2,1,0:T(1,128)S(1)}, u32[]{:S(2)}, u32[]{:S(2)}) %all-to-all-start) | async-done | bytes 49184 | tf_op jit(solution)/shard_map/all_to_all | solution.py:527
  122.8 3.4 %all-to-all-start.1 = ((f32[8,1,128]{2,1,0:T(1,128)}), f32[8,1,128]{2,1,0:T(1,128)S(1)}, u32[]{:S(2)}, u32[]{:S(2)}) async-start(f32[8,1,128]{2,1,0:T(1,128)} %broadcast_in_dim.23), calls=%async_computation.1 | async-start | bytes 8192 | tf_op jit(solution)/shard_map/all_to_all | solution.py:527
  127.2 5.6 %all-to-all-done.1 = f32[8,1,128]{2,1,0:T(1,128)S(1)} async-done(((f32[8,1,128]{2,1,0:T(1,128)}), f32[8,1,128]{2,1,0:T(1,128)S(1)}, u32[]{:S(2)}, u32[]{:S(2)}) %all-to-all-start.1) | async-done | bytes 4128 | tf_op jit(solution)/shard_map/all_to_all | solution.py:527
  133.4 1.1 divide_bitcast_fusion
  (83 shorter events, 11.4 us)
Async XLA Ops:
  0.6 0.7 copy-start.9
  1.5 0.7 copy-start.6
  2.4 0.8 copy-start.3
  3.4 0.7 copy-start.4
  4.2 0.7 copy-start.5
  5.5 8.0 %collective-permute-start = (f32[3,3,2,128]{3,2,1,0:T(2,128)S(1)}, f32[3,3,2,128]{3,2,1,0:T(2,128)S(1)}, u32[]{:S(2)}, u32[]{:S(2)}) collective-permute-start(f32[3,3,2,128]{3,2,1,0:T(2,128)S(1)} %get-tuple-element.44), channel_id=1, source_target_pairs={{0,7},{1,2},{2,1},{3,4},{4,3},{5,6},{6,5},{7,0},{8,15},{9,10},{10,... | collective-permute-start | bytes 27656 | tf_op jit(solution)/shard_map/outer/ppermute | solution.py:518
  11.4 4.4 %collective-permute-start.1 = (f32[3,3,2,128]{3,2,1,0:T(2,128)S(1)}, f32[3,3,2,128]{3,2,1,0:T(2,128)S(1)}, u32[]{:S(2)}, u32[]{:S(2)}) collective-permute-start(f32[3,3,2,128]{3,2,1,0:T(2,128)S(1)} %get-tuple-element.45), channel_id=1, source_target_pairs={{0,1},{1,0},{2,3},{3,2},{4,5},{5,4},{6,7},{7,6},{8,9},{9,8},{10,11... | collective-permute-start | bytes 27656 | tf_op jit(solution)/shard_map/inner/ppermute | solution.py:520
  15.9 10.0 %copy-start.8 = (bf16[8,128]{1,0:T(8,128)(2,1)S(1)}, bf16[8,128]{1,0:T(8,128)(2,1)}, u32[]{:S(2)}) copy-start(bf16[8,128]{1,0:T(8,128)(2,1)} %param.16) | copy-start | bytes 6148
  15.9 10.0 %copy-start.7 = (bf16[5,128]{1,0:T(8,128)(2,1)S(1)}, bf16[5,128]{1,0:T(8,128)(2,1)}, u32[]{:S(2)}) copy-start(bf16[5,128]{1,0:T(8,128)(2,1)} %param.17) | copy-start | bytes 3844
  15.9 10.0 %collective-permute-start.2 = (f32[2,3,8,128]{3,2,1,0:T(8,128)S(1)}, f32[2,3,8,128]{3,2,1,0:T(8,128)S(1)}, u32[]{:S(2)}, u32[]{:S(2)}) collective-permute-start(f32[2,3,8,128]{3,2,1,0:T(8,128)S(1)} %get-tuple-element.38), channel_id=1, source_target_pairs={{0,704},{64,128},{128,64},{192,256},{256,192},{320,384},{384,320},... | collective-permute-start | bytes 73736 | tf_op jit(solution)/shard_map/outer/ppermute | solution.py:518
  23.9 4.6 %collective-permute-start.3 = (f32[2,3,8,128]{3,2,1,0:T(8,128)S(1)}, f32[2,3,8,128]{3,2,1,0:T(8,128)S(1)}, u32[]{:S(2)}, u32[]{:S(2)}) collective-permute-start(f32[2,3,8,128]{3,2,1,0:T(8,128)S(1)} %get-tuple-element.39), channel_id=1, source_target_pairs={{0,64},{64,0},{128,192},{192,128},{256,320},{320,256},{384,448},{4... | collective-permute-start | bytes 73736 | tf_op jit(solution)/shard_map/inner/ppermute | solution.py:520
  28.6 16.4 %collective-permute-start.4 = (f32[7,2,8,128]{3,2,1,0:T(8,128)S(1)}, f32[7,2,8,128]{3,2,1,0:T(8,128)S(1)}, u32[]{:S(2)}, u32[]{:S(2)}) collective-permute-start(f32[7,2,8,128]{3,2,1,0:T(8,128)S(1)} %get-tuple-element.29), channel_id=1, source_target_pairs={{0,56},{8,16},{16,8},{24,32},{32,24},{40,48},{48,40},{56,0},{1,57}... | collective-permute-start | bytes 172040 | tf_op jit(solution)/shard_map/outer/ppermute | solution.py:518
  40.8 4.2 %collective-permute-start.5 = (f32[7,2,8,128]{3,2,1,0:T(8,128)S(1)}, f32[7,2,8,128]{3,2,1,0:T(8,128)S(1)}, u32[]{:S(2)}, u32[]{:S(2)}) collective-permute-start(f32[7,2,8,128]{3,2,1,0:T(8,128)S(1)} %get-tuple-element.28), channel_id=1, source_target_pairs={{0,8},{8,0},{16,24},{24,16},{32,40},{40,32},{48,56},{56,48},{1,9},... | collective-permute-start | bytes 172040 | tf_op jit(solution)/shard_map/inner/ppermute | solution.py:520
  43.4 0.7 copy-start.1
  44.2 0.7 copy-start
  45.8 0.7 copy-start.2
  56.4 5.6 %collective-permute-start.6 = (f32[3,3,2,128]{3,2,1,0:T(2,128)S(1)}, f32[3,3,2,128]{3,2,1,0:T(2,128)S(1)}, u32[]{:S(2)}, u32[]{:S(2)}) collective-permute-start(f32[3,3,2,128]{3,2,1,0:T(2,128)S(1)} %get-tuple-element.36), channel_id=1, source_target_pairs={{0,7},{1,2},{2,1},{3,4},{4,3},{5,6},{6,5},{7,0},{8,15},{9,10},{10,... | collective-permute-start | bytes 27656 | tf_op jit(solution)/shard_map/outer/ppermute | solution.py:518
  59.0 4.4 %collective-permute-start.7 = (f32[3,3,2,128]{3,2,1,0:T(2,128)S(1)}, f32[3,3,2,128]{3,2,1,0:T(2,128)S(1)}, u32[]{:S(2)}, u32[]{:S(2)}) collective-permute-start(f32[3,3,2,128]{3,2,1,0:T(2,128)S(1)} %get-tuple-element.37), channel_id=1, source_target_pairs={{0,1},{1,0},{2,3},{3,2},{4,5},{5,4},{6,7},{7,6},{8,9},{9,8},{10,11... | collective-permute-start | bytes 27656 | tf_op jit(solution)/shard_map/inner/ppermute | solution.py:520
  63.5 9.0 %collective-permute-start.8 = (f32[2,3,8,128]{3,2,1,0:T(8,128)S(1)}, f32[2,3,8,128]{3,2,1,0:T(8,128)S(1)}, u32[]{:S(2)}, u32[]{:S(2)}) collective-permute-start(f32[2,3,8,128]{3,2,1,0:T(8,128)S(1)} %get-tuple-element.34), channel_id=1, source_target_pairs={{0,704},{64,128},{128,64},{192,256},{256,192},{320,384},{384,320},... | collective-permute-start | bytes 73736 | tf_op jit(solution)/shard_map/outer/ppermute | solution.py:518
  70.5 4.6 %collective-permute-start.9 = (f32[2,3,8,128]{3,2,1,0:T(8,128)S(1)}, f32[2,3,8,128]{3,2,1,0:T(8,128)S(1)}, u32[]{:S(2)}, u32[]{:S(2)}) collective-permute-start(f32[2,3,8,128]{3,2,1,0:T(8,128)S(1)} %get-tuple-element.35), channel_id=1, source_target_pairs={{0,64},{64,0},{128,192},{192,128},{256,320},{320,256},{384,448},{4... | collective-permute-start | bytes 73736 | tf_op jit(solution)/shard_map/inner/ppermute | solution.py:520
  75.1 11.7 %collective-permute-start.10 = (f32[7,2,8,128]{3,2,1,0:T(8,128)S(1)}, f32[7,2,8,128]{3,2,1,0:T(8,128)S(1)}, u32[]{:S(2)}, u32[]{:S(2)}) collective-permute-start(f32[7,2,8,128]{3,2,1,0:T(8,128)S(1)} %get-tuple-element.27), channel_id=1, source_target_pairs={{0,56},{8,16},{16,8},{24,32},{32,24},{40,48},{48,40},{56,0},{1,57}... | collective-permute-start | bytes 172040 | tf_op jit(solution)/shard_map/outer/ppermute | solution.py:518
  84.7 3.1 %collective-permute-start.11 = (f32[7,2,8,128]{3,2,1,0:T(8,128)S(1)}, f32[7,2,8,128]{3,2,1,0:T(8,128)S(1)}, u32[]{:S(2)}, u32[]{:S(2)}) collective-permute-start(f32[7,2,8,128]{3,2,1,0:T(8,128)S(1)} %get-tuple-element.26), channel_id=1, source_target_pairs={{0,8},{8,0},{16,24},{24,16},{32,40},{40,32},{48,56},{56,48},{1,9},... | collective-permute-start | bytes 172040 | tf_op jit(solution)/shard_map/inner/ppermute | solution.py:520
  95.5 26.7 %all-to-all-start = ((f32[96,1,128]{2,1,0:T(1,128)}), f32[96,1,128]{2,1,0:T(1,128)S(1)}, u32[]{:S(2)}, u32[]{:S(2)}) async-start(f32[96,1,128]{2,1,0:T(1,128)} %broadcast_in_dim.22), calls=%async_computation | async-start | bytes 98304 | tf_op jit(solution)/shard_map/all_to_all | solution.py:527
  122.8 10.0 %all-to-all-start.1 = ((f32[8,1,128]{2,1,0:T(1,128)}), f32[8,1,128]{2,1,0:T(1,128)S(1)}, u32[]{:S(2)}, u32[]{:S(2)}) async-start(f32[8,1,128]{2,1,0:T(1,128)} %broadcast_in_dim.23), calls=%async_computation.1 | async-start | bytes 8192 | tf_op jit(solution)/shard_map/all_to_all | solution.py:527
  (1 other events, 0.7 us)

commit v3 on v2

--- a/solution.py
+++ b/solution.py
@@ -1,4 +1,3 @@
-import functools
 import math
 
 import jax
@@ -8,6 +7,7 @@
 from jax.experimental.pallas import tpu as pltpu
 from jax.sharding import PartitionSpec as P
 
+
 cutoff = 6.0
 env_scale = 0.25
 domain_side = 18.0
@@ -19,14 +19,16 @@
 NB = 8
 NSPEC = 5
 LIST = 24
+LISTED = 40
 USED = 392
 ROWS = 400
 DEPTH = 512
 INNER = 256
 OWN = 80
-TILES = 52
+WIDE = 256
+TILES = 26
 LANES = 128
-POS, KIND, KIND3, NEIGH, VEL, LIVE3, LIVE = 0, 6, 8, 16, 64, 72, 80
+POS, KIND, VEL, LIVE, NEIGH = 0, 6, 8, 14, 16
 MISC = NEIGH + 2 * LIST
 F32 = jnp.float32
 BF16 = jnp.bfloat16
@@ -75,59 +77,71 @@
 
 
 def one_hot(index, count, depth):
-    hit = (iota((count, LANES), 0) == index).astype(F32).astype(BF16)
-    if depth > count:
-        hit = jnp.concatenate([hit, jnp.zeros((depth - count, LANES), BF16)], axis=0)
-    return hit
-
-
-def build_pairs(rows_ref, table, off_ref, end_ref, pairs_ref, listed_t):
-    shape = (ROWS, LANES)
-    lane = iota(shape, 1)
-    row = iota(shape, 0)
-    x, y, z = row_coords(row)
+    hit = (iota((count, index.shape[1]), 0) == index).astype(F32).astype(BF16)
+    return deepen(hit, depth)
+
+
+def deepen(values, depth):
+    more = depth - values.shape[0]
+    if more == 0:
+        return values
+    return jnp.concatenate([values, jnp.zeros((more, values.shape[1]), values.dtype)], axis=0)
+
+
+def build_pairs(rows_ref, base_ref, below_ref, table, off_ref, end_ref, pairs_ref, listed_t):
+    lane = iota((ROWS, LANES), 1)
     entry = rows_ref[0:ROWS]
-    in_list = (lane >= NEIGH) & (lane < MISC)
-    listed = in_list & (entry >= 0.0) & (z < 6.5) & (row < USED)
-    far, _, _ = far_coords(x, y, z, entry)
-    nearest = jnp.minimum(away(x, y, z), away(*far))
-    kept = (listed & (nearest < 1.5), listed & (nearest > 1.5) & (nearest < 2.5))
-    upper = (iota((LANES, LANES), 0) <= iota((LANES, LANES), 1)).astype(F32).astype(BF16)
+    listed = (lane >= NEIGH) & (lane < MISC) & (entry >= 0.0)
+    q = jnp.floor(entry * 0.5)
+    a = jnp.floor((q + 0.5) * (1.0 / 25.0))
+    ab = jnp.floor((q + 0.5) * (1.0 / 5.0))
+    far = jnp.maximum(jnp.abs(base_ref[0] + a), jnp.abs(base_ref[1] + (ab - 5.0 * a)))
+    far = jnp.maximum(far, jnp.abs(base_ref[2] + (q - 5.0 * ab)))
+    nearest = jnp.where(listed, jnp.minimum(base_ref[3], far), 9.0)
+    kept = (nearest < 1.5, (nearest > 1.5) & (nearest < 2.5))
+    upto = iota((2 * LIST, LANES), 0) + NEIGH
+    place = iota((2 * LIST, LANES), 1)
+    keys = (place <= upto).astype(F32) + (place < upto).astype(F32)
+    keys = keys.astype(BF16)
     ones = jnp.ones((LANES, LANES), BF16)
-    below = (iota((ROWS, DEPTH), 1) < iota((ROWS, DEPTH), 0)).astype(F32).astype(BF16)
-    start = jnp.int32(0)
-    counts = []
+    cx, cy, cz = row_coords(iota((1, DEPTH), 1))
+    first = jnp.float32(0.0)
+    totals = []
     for keep in kept:
-        keep = keep.astype(F32)
-        keep16 = keep.astype(BF16)
-        rank = mm(keep16, upper) * keep
+        keep16 = deepen(keep.astype(F32).astype(BF16), DEPTH)
+        key_t = mm_nt(keys, keep16)
         count = mm(keep16, ones)
-        padded = jnp.concatenate(
-            [count.astype(BF16), jnp.zeros((DEPTH - ROWS, LANES), BF16)], axis=0
-        )
-        offset = mm(below, padded)
-        end = offset + count
+        count_t = mm_nt(ones[0:16], keep16)
+        below = below_ref[...]
+        offset = mm(below, count.astype(BF16)) + first
+        offset_t = mm_nt(count_t.astype(BF16), below)[0:1] + first
+        end = offset + count[0:ROWS]
         off_ref[...] = offset
         end_ref[...] = end
         total = jnp.max(end)
-        high = jnp.floor(offset * (1.0 / 256.0))
-        fields = jnp.where(in_list, rank, 0.0)
-        for at, value in enumerate((high, offset - 256.0 * high, x, y, z)):
-            fields = jnp.where(lane == float(MISC + at), value, fields)
-        fields = jnp.concatenate([fields, jnp.zeros((DEPTH - ROWS, LANES), F32)], axis=0)
-        fields_t = jnp.transpose(fields)
+        offset_t = jnp.concatenate([offset_t, jnp.zeros((1, DEPTH - ROWS), F32)], axis=1)
+        high = jnp.floor(offset_t * (1.0 / 256.0))
+        misc = jnp.concatenate(
+            [high, offset_t - 256.0 * high, cx, cy, cz, jnp.zeros((11, DEPTH), F32)], axis=0
+        )
         table[0 : 2 * LIST] = listed_t
-        table[2 * LIST : 4 * LIST + 16] = fields_t[NEIGH : MISC + 16].astype(BF16)
-        tiles = (total.astype(jnp.int32) + (LANES - 1)) // LANES
-
-        def body(k, carry, start=start, total=total):
-            place = iota((1, LANES), 1) + (k * LANES).astype(F32)
-            hit = (off_ref[...] <= place) & (end_ref[...] > place)
-            hit = hit.astype(F32).astype(BF16)
-            hit = jnp.concatenate([hit, jnp.zeros((DEPTH - ROWS, LANES), BF16)], axis=0)
-            got = mm(table[...], hit)
+        table[2 * LIST : 4 * LIST] = key_t.astype(BF16)
+        table[4 * LIST :] = misc.astype(BF16)
+
+        def body(k, carry, first=first, total=total):
+            place = iota((1, WIDE), 1) + (k * WIDE).astype(F32)
+            offset = off_ref[...]
+            end = end_ref[...]
+            hit = jnp.concatenate(
+                [
+                    ((offset <= part) & (end > part)).astype(F32).astype(BF16)
+                    for part in (place[:, 0:LANES], place[:, LANES:])
+                ],
+                axis=1,
+            )
+            got = mm(table[...], deepen(hit, DEPTH))
             misc = got[4 * LIST :]
-            wanted = place - (256.0 * misc[0:1] + misc[1:2]) + 1.0
+            wanted = 2.0 * (place - (256.0 * misc[0:1] + misc[1:2])) + 1.0
             chosen = (got[2 * LIST : 4 * LIST] == wanted).astype(F32)
             entry = jnp.sum(chosen * got[0 : 2 * LIST], axis=0, keepdims=True)
             slot = jnp.sum(chosen[LIST:], axis=0, keepdims=True)
@@ -161,15 +175,18 @@
                 valid.astype(F32),
                 *shift,
                 (valid & (away_i < 1.5)).astype(F32),
-                jnp.zeros((3, LANES), F32),
+                jnp.zeros((3, WIDE), F32),
             ]
-            pairs_ref[start + k] = jnp.concatenate(lines, axis=0)
+            pairs_ref[k] = jnp.where(place < first, pairs_ref[k], jnp.concatenate(lines, axis=0))
             return carry
 
-        lax.fori_loop(0, tiles, body, jnp.int32(0))
-        start = start + tiles
-        counts.append(start)
-    return counts
+        last = total.astype(jnp.int32)
+        lax.fori_loop(
+            first.astype(jnp.int32) // WIDE, (last + (WIDE - 1)) // WIDE, body, jnp.int32(0)
+        )
+        totals.append((last + (WIDE - 1)) // WIDE)
+        first = total
+    return totals
 
 
 def turns(radius):
@@ -188,12 +205,15 @@
 
 
 def evaluate(refs, scratch, counts, own_out):
-    pos_t, pairs_ref, w1t, w1, wmt, wm, smt, sm, eo = refs
+    pos_t, pairs_ref, w1t, w1, wmt, wm, smt, sm, eo_ref = refs
     env_ref, envs_ref, grad_ref, geo_ref, lat_ref, slope_ref, h_ref, wb_ref, hp_ref, en_ref = (
         scratch
     )
     front, every = counts
     norm = math.sqrt(2.0 / cutoff)
+
+    def eo():
+        return jnp.concatenate([eo_ref[...], eo_ref[...]], axis=1)
 
     env_ref[...] = jnp.zeros(env_ref.shape, F32)
     grad_ref[...] = jnp.zeros(grad_ref.shape, F32)
@@ -237,9 +257,9 @@
             (near_kind == float(k)).astype(F32) + (far_kind == float(k)).astype(F32)
             for k in range(NSPEC)
         ]
-        feats = jnp.concatenate(basis + kinds + [jnp.zeros((3, LANES), F32)], axis=0)
-        geo_ref[t] = jnp.concatenate(
-            [u, inverse, f, fd, jnp.zeros((2, LANES), F32)] + slope, axis=0
+        feats = jnp.concatenate(basis + kinds + [jnp.zeros((3, WIDE), F32)], axis=0)
+        geo_ref[t, 0:16] = jnp.concatenate(
+            [u, inverse, f, fd, jnp.zeros((2, WIDE), F32)] + slope, axis=0
         )
         pre = mm(w1t[...], feats.astype(BF16))
         gate = sigmoid(pre)
@@ -283,9 +303,9 @@
         arg = lat_ref[t].astype(F32) + mm(smt[...], coupling)
         gate = sigmoid(arg)
         hidden = arg * gate
-        dotted = jnp.sum(hidden * eo[...], axis=0, keepdims=True)
+        dotted = jnp.sum(hidden * eo(), axis=0, keepdims=True)
         en_ref[0:1] += f * dotted * pair[12:13]
-        arg_bar = (f * valid) * eo[...] * (gate * (1.0 + arg * (1.0 - gate)))
+        arg_bar = (f * valid) * eo() * (gate * (1.0 + arg * (1.0 - gate)))
         arg_bar = arg_bar.astype(BF16)
         hp_ref[t] = arg_bar
         c_bar = mm(sm[...], arg_bar).astype(BF16).astype(F32)
@@ -296,7 +316,7 @@
             jnp.sum(al_bar * env[(k + 1) * CH : (k + 2) * CH], axis=0, keepdims=True)
             for k in range(3)
         ]
-        pairs_ref[t, 13:16] = jnp.concatenate(u_bar, axis=0)
+        geo_ref[t, 16:19] = jnp.concatenate(u_bar, axis=0)
         high, low = split2(
             jnp.concatenate([al_bar, al_bar * u[0:1], al_bar * u[1:2], al_bar * u[2:3]], axis=0)
         )
@@ -324,7 +344,7 @@
         h = h_ref[t]
         w = h * (f * valid)
         w_bar = wb_ref[t] + g0 + u[0:1] * parts[0] + u[1:2] * parts[1] + u[2:3] * parts[2]
-        u_bar = pair[13:16] + jnp.concatenate(
+        u_bar = geo[16:19] + jnp.concatenate(
             [jnp.sum(w * part, axis=0, keepdims=True) for part in parts], axis=0
         )
         f_bar = geo[6:7] + jnp.sum(h * w_bar, axis=0, keepdims=True)
@@ -335,7 +355,7 @@
         r_bar = jnp.sum(basis_bar * geo[8:16], axis=0, keepdims=True) + f_bar * fd
         along = jnp.sum(u * u_bar, axis=0, keepdims=True)
         d_bar = (r_bar * u + (u_bar - u * along) * inverse) * valid
-        blank = jnp.zeros((2, LANES), F32)
+        blank = jnp.zeros((2, WIDE), F32)
 
         def slotted(values, slot):
             second = slot > 0.5
@@ -346,7 +366,7 @@
         pulls = jnp.concatenate(
             [slotted(d_bar, pair[1:2]), slotted(-d_bar, pair[3:4])], axis=1
         )
-        high, low = split2(jnp.concatenate([pulls, jnp.zeros((120, 2 * LANES), F32)], axis=0))
+        high, low = split2(jnp.concatenate([pulls, jnp.zeros((120, 2 * WIDE), F32)], axis=0))
         where = jnp.concatenate([one_hot(pair[6:7], OWN, OWN), one_hot(pair[7:8], OWN, OWN)], axis=1)
         own_out[...] += mm_nt(where, high) + mm_nt(where, low)
         return carry
@@ -390,90 +410,252 @@
     )
 
 
-def first_kernel(low, own, high, w1t, w1, wmt, wm, smt, sm, eo, table_energy,
+def fetch(copies, sems):
+    made = [pltpu.make_async_copy(src, dst, sems.at[i]) for i, (src, dst) in enumerate(copies)]
+    for copy in made:
+        copy.start()
+
+    def wait():
+        for copy in made:
+            copy.wait()
+
+    return wait
+
+
+def pack_kernel(pos_in, vel_in, kind_in, count_in, list_in, out, pos, vel, kind, count, lists, sems,
+                grid, first_list, second_list):
+    fetch(
+        ((pos_in, pos), (vel_in, vel), (kind_in, kind), (count_in, count), (list_in, lists)), sems
+    )()
+    for x in range(3):
+        for y in range(3):
+            at = (3 * x + y) * 16
+            for s in range(2):
+                for c in range(3):
+                    grid[at + POS + 3 * s + c : at + POS + 3 * s + c + 1, 2:5] = pos[c, x, y, s : s + 1]
+                    grid[at + VEL + 3 * s + c : at + VEL + 3 * s + c + 1, 2:5] = vel[c, x, y, s : s + 1]
+                grid[at + KIND + s : at + KIND + s + 1, 2:5] = kind[x, y, s : s + 1].astype(F32)
+                grid[at + LIVE + s : at + LIVE + s + 1, 2:5] = (
+                    count[x, y : y + 1] > s
+                ).astype(F32)
+            row = (3 * x + y) * 8 + 2
+            first_list[row : row + 3, 0:LISTED] = lists[x, y, :, 0].astype(F32)
+            second_list[row : row + 3, 0:LISTED] = lists[x, y, :, 1].astype(F32)
+    turned = jnp.concatenate(
+        [jnp.transpose(grid[0:128])[0:8], jnp.transpose(grid[128:256])[0:8]], axis=1
+    )
+    lane = iota((8, LANES), 1)
+    row = iota((8, LANES), 0)
+    inside = (row > 1.5) & (row < 4.5)
+    for xy in range(9):
+        half = turned[:, 0:LANES] if xy < 8 else turned[:, LANES:]
+        shift = (xy % 8) * 16
+        fields = pltpu.roll(half, (LANES - shift) % LANES, 1)
+        one = pltpu.roll(first_list[xy * 8 : xy * 8 + 8], NEIGH, 1)
+        two = pltpu.roll(second_list[xy * 8 : xy * 8 + 8], NEIGH + LIST, 1)
+        merged = jnp.where(lane < NEIGH, fields, jnp.where(lane < NEIGH + LIST, one, two))
+        out[xy] = jnp.where(inside & (lane < MISC), merged, 0.0)
+
+
+def prep_kernel(bw_in, se_in, wmt_in, sm_in, eo_in, table_in,
+                w1t, w1, wmt, wm, smt, sm, eo, base, below, levels, bw, se, table, sems):
+    fetch(
+        (
+            (bw_in, bw),
+            (se_in, se),
+            (wmt_in, wmt),
+            (sm_in, sm),
+            (eo_in, eo.at[0:1]),
+            (table_in, table),
+        ),
+        sems,
+    )()
+    for k in range(NSPEC):
+        levels[k : k + 1] = jnp.broadcast_to(table[0:1, k : k + 1], (1, LANES))
+    both = jnp.concatenate(
+        [bw[...].astype(F32), se[...].astype(F32), jnp.zeros((3, LAT), F32)], axis=0
+    )
+    w1[...] = both.astype(BF16)
+    w1t[...] = jnp.transpose(deepen(both, LANES)).astype(BF16)[:, 0:16]
+    wm[...] = jnp.transpose(deepen(wmt[...].astype(F32), LANES)).astype(BF16)[:, 0:CH]
+    smt[...] = jnp.transpose(deepen(sm[...].astype(F32), LANES)).astype(BF16)[:, 0:CH]
+    eo[...] = jnp.transpose(jnp.broadcast_to(eo[0:1], (LAT, LANES)))
+    row = iota((ROWS, LANES), 0)
+    x, y, z = row_coords(row)
+    unused = (z > 6.5) | (row > USED - 0.5)
+    for i, v in enumerate((x, y, z)):
+        base[i] = jnp.where(unused, 99.0, 3.0 * jnp.floor((v + 1.5) * (1.0 / 3.0)) - 5.0)
+    base[3] = jnp.where(unused, 99.0, away(x, y, z))
+    below[...] = (iota((ROWS, DEPTH), 1) < iota((ROWS, DEPTH), 0)).astype(F32).astype(BF16)
+
+
+def lanes_of(values, lane, first, second):
+    return jnp.where(lane < 2.5, values[:, first : first + 1], values[:, second : second + 1])
+
+
+def own_lane_row():
+    lane = iota((72, LANES), 1)
+    row = iota((72, LANES), 0)
+    z = row - 8.0 * jnp.floor(row * 0.125)
+    return lane, (z > 1.5) & (z < 4.5)
+
+
+def first_kernel(low, own, high, w1t, w1, wmt, wm, smt, sm, eo, base, below, levels,
                  force_out, moved_out, energy_out, pairs_ref, counts_ref,
                  rows_ref, table, off_ref, end_ref, pos_t, own_ref, *scratch):
     load_rows(rows_ref, low, own, high)
     turned = position_rows(rows_ref, pos_t)
     front, every = build_pairs(
-        rows_ref, table, off_ref, end_ref, pairs_ref, turned[NEIGH:MISC].astype(BF16)
+        rows_ref, base, below, table, off_ref, end_ref, pairs_ref, turned[NEIGH:MISC].astype(BF16)
     )
     counts_ref[0] = front
     counts_ref[1] = every
     refs = (pos_t, pairs_ref, w1t, w1, wmt, wm, smt, sm, eo)
     evaluate(refs, scratch, (front, every), own_ref)
     mine = own_rows(rows_ref)
-    lane = iota((72, LANES), 1)
-    row = iota((72, LANES), 0)
-    z = row - 8.0 * jnp.floor(row * 0.125)
-    inside = (z > 1.5) & (z < 4.5)
-    live3 = pltpu.roll(mine, LANES - LIVE3, 1)
-    kind3 = pltpu.roll(mine, LANES - KIND3, 1)
+    lane, inside = own_lane_row()
+    kind3 = lanes_of(mine, lane, KIND, KIND + 1)
     speed = pltpu.roll(mine, LANES - VEL, 1)
-    force = own_ref[0:72] * live3
+    force = own_ref[0:72] * lanes_of(mine, lane, LIVE, LIVE + 1)
     force = jnp.where(inside & (lane < 6.0), force, 0.0)
     force_out[...] = force
     inverse_mass = jnp.zeros((72, LANES), F32)
     for k, mass in enumerate(atom_masses):
         inverse_mass = jnp.where(kind3 == float(k), 1.0 / mass, inverse_mass)
     moved = mine + time_step * speed + 0.5 * time_step * time_step * inverse_mass * force
-    moved_out[...] = jnp.where(lane < 6.0, moved, jnp.where(lane < 8.0, mine, 0.0))
+    moved_out[...] = jnp.where(lane < 6.0, moved, jnp.where(lane < float(NEIGH), mine, 0.0))
     live = pltpu.roll(mine, LANES - LIVE + KIND, 1)
-    here = inside & (lane > 5.5) & (lane < 7.5)
-    live = jnp.where(here, live, 0.0)
+    live = jnp.where(inside & (lane > 5.5) & (lane < 7.5), live, 0.0)
     atom = jnp.zeros((72, LANES), F32)
     for k in range(NSPEC):
-        atom = jnp.where(mine == float(k), table_energy[k], atom)
+        atom = jnp.where(mine == float(k), levels[k : k + 1], atom)
     atoms = jnp.sum(atom * live)
     energy_out[...] = energy_row(jnp.sum(scratch[-1][0:1]) + atoms, atoms, jnp.sum(live))
 
 
-def second_kernel(low, own, high, w1t, w1, wmt, wm, smt, sm, eo, pairs_in, counts_ref, kept_in, energy_in,
-                  force_out, energy_out,
-                  rows_ref, pos_t, own_ref, pairs_ref, *scratch):
+def second_kernel(low, own, high, w1t, w1, wmt, wm, smt, sm, eo, pairs_ref, counts_ref, energy_in,
+                  force_out, energy_out, rows_ref, pos_t, own_ref, *scratch):
     load_rows(rows_ref, low, own, high)
     position_rows(rows_ref, pos_t)
-    front, every = counts_ref[0], counts_ref[1]
-    pairs_ref[...] = pairs_in[...]
     refs = (pos_t, pairs_ref, w1t, w1, wmt, wm, smt, sm, eo)
-    evaluate(refs, scratch, (front, every), own_ref)
-    lane = iota((72, LANES), 1)
-    row = iota((72, LANES), 0)
-    z = row - 8.0 * jnp.floor(row * 0.125)
-    force = own_ref[0:72] * kept_in[...]
-    force_out[...] = jnp.where((z > 1.5) & (z < 4.5) & (lane < 6.0), force, 0.0)
+    evaluate(refs, scratch, (counts_ref[0], counts_ref[1]), own_ref)
+    mine = own_rows(rows_ref)
+    lane, inside = own_lane_row()
+    force = own_ref[0:72] * lanes_of(mine, lane, LIVE, LIVE + 1)
+    force_out[...] = jnp.where(inside & (lane < 6.0), force, 0.0)
     energy_out[...] = energy_in[...] + energy_row(0.0, jnp.sum(scratch[-1][0:1]), 0.0)
+
+
+def energy_row(first, second, live):
+    lane = iota((1, LANES), 1)
+    return (
+        jnp.where(lane == 0.0, first, 0.0)
+        + jnp.where(lane == 1.0, second, 0.0)
+        + jnp.where((lane == 2.0) | (lane == 3.0), live, 0.0)
+    )
 
 
 EVAL_SCRATCH = (
     pltpu.VMEM((4 * CH, INNER), F32),
     pltpu.VMEM((4 * CH, 2 * INNER), BF16),
     pltpu.VMEM((4 * CH, INNER), F32),
-    pltpu.VMEM((TILES, 16, LANES), F32),
-    pltpu.VMEM((TILES, LAT, LANES), BF16),
-    pltpu.VMEM((TILES, LAT, LANES), F32),
-    pltpu.VMEM((TILES, CH, LANES), F32),
-    pltpu.VMEM((TILES, CH, LANES), F32),
-    pltpu.VMEM((TILES, LAT, LANES), BF16),
-    pltpu.VMEM((8, LANES), F32),
+    pltpu.VMEM((TILES, 24, WIDE), F32),
+    pltpu.VMEM((TILES, LAT, WIDE), BF16),
+    pltpu.VMEM((TILES, LAT, WIDE), F32),
+    pltpu.VMEM((TILES, CH, WIDE), F32),
+    pltpu.VMEM((TILES, CH, WIDE), F32),
+    pltpu.VMEM((TILES, LAT, WIDE), BF16),
+    pltpu.VMEM((8, WIDE), F32),
 )
-PARAMS = pltpu.CompilerParams(vmem_limit_bytes=20 * 2**20)
 VM = pl.BlockSpec(memory_space=pltpu.VMEM)
 SM = pl.BlockSpec(memory_space=pltpu.SMEM)
-
-
-def first_call(pieces, weights, table_energy):
+HB = pl.BlockSpec(memory_space=pltpu.HBM)
+
+
+def limit(mebibytes):
+    return pltpu.CompilerParams(vmem_limit_bytes=mebibytes * 2**20)
+
+
+def shape(*dims, kind=F32):
+    return jax.ShapeDtypeStruct(dims, kind)
+
+
+def pack_call(positions, velocity, species, region_count, neighbours):
+    return pl.pallas_call(
+        pack_kernel,
+        name="pack",
+        out_shape=shape(9, 8, LANES),
+        in_specs=[HB] * 5,
+        out_specs=VM,
+        scratch_shapes=(
+            pltpu.VMEM((3, 3, 3, 2, 3), F32),
+            pltpu.VMEM((3, 3, 3, 2, 3), F32),
+            pltpu.VMEM((3, 3, 2, 3), jnp.int32),
+            pltpu.VMEM((3, 3, 3), jnp.int32),
+            pltpu.VMEM((3, 3, 3, 2, LISTED), jnp.int32),
+            pltpu.SemaphoreType.DMA((5,)),
+            pltpu.VMEM((256, LANES), F32),
+            pltpu.VMEM((72, LANES), F32),
+            pltpu.VMEM((72, LANES), F32),
+        ),
+        compiler_params=limit(4),
+    )(
+        positions.transpose(0, 1, 2, 4, 3),
+        velocity.transpose(0, 1, 2, 4, 3),
+        species.transpose(0, 1, 3, 2),
+        region_count,
+        neighbours,
+    )
+
+
+def prep_call(basis_weight, species_embed, weight_map, scalar_map, energy_out, species_energy):
+    return pl.pallas_call(
+        prep_kernel,
+        name="prep",
+        out_shape=(
+            shape(LAT, 16, kind=BF16),
+            shape(16, LAT, kind=BF16),
+            shape(CH, LAT, kind=BF16),
+            shape(LAT, CH, kind=BF16),
+            shape(LAT, CH, kind=BF16),
+            shape(CH, LAT, kind=BF16),
+            shape(LAT, LANES),
+            shape(4, ROWS, LANES),
+            shape(ROWS, DEPTH, kind=BF16),
+            shape(8, LANES),
+        ),
+        in_specs=[HB] * 6,
+        out_specs=(VM,) * 10,
+        scratch_shapes=(
+            pltpu.VMEM((NB, LAT), BF16),
+            pltpu.VMEM((NSPEC, LAT), BF16),
+            pltpu.VMEM((1, NSPEC), F32),
+            pltpu.SemaphoreType.DMA((6,)),
+        ),
+        compiler_params=limit(4),
+        cost_estimate=pl.CostEstimate(flops=1000000, transcendentals=0, bytes_accessed=2000000),
+    )(
+        basis_weight,
+        species_embed,
+        weight_map.T,
+        scalar_map,
+        energy_out[None, :],
+        species_energy[None, :],
+    )
+
+
+def first_call(pieces, prepared):
     return pl.pallas_call(
         first_kernel,
         name="first",
         out_shape=(
-            jax.ShapeDtypeStruct((72, LANES), F32),
-            jax.ShapeDtypeStruct((72, LANES), F32),
-            jax.ShapeDtypeStruct((1, LANES), F32),
-            jax.ShapeDtypeStruct((TILES, 16, LANES), F32),
-            jax.ShapeDtypeStruct((2,), jnp.int32),
+            shape(72, LANES),
+            shape(72, LANES),
+            shape(1, LANES),
+            shape(TILES, 16, WIDE),
+            shape(2, kind=jnp.int32),
         ),
-        in_specs=[VM] * (len(pieces) + len(weights)) + [SM],
+        in_specs=[VM] * (len(pieces) + len(prepared)),
         out_specs=(VM, VM, VM, VM, SM),
         scratch_shapes=(
             pltpu.VMEM((ROWS, LANES), F32),
@@ -484,40 +666,35 @@
             pltpu.VMEM((OWN, LANES), F32),
             *EVAL_SCRATCH,
         ),
-        compiler_params=PARAMS,
-    )(*pieces, *weights, table_energy)
-
-
-def second_call(pieces, weights, pairs, counts, live3, energy):
+        compiler_params=limit(20),
+    )(*pieces, *prepared)
+
+
+def second_call(pieces, weights, pairs, counts, energy):
     return pl.pallas_call(
         second_kernel,
         name="second",
-        out_shape=(
-            jax.ShapeDtypeStruct((72, LANES), F32),
-            jax.ShapeDtypeStruct((1, LANES), F32),
-        ),
-        in_specs=[VM] * (len(pieces) + len(weights) + 1) + [SM, VM, VM],
+        out_shape=(shape(72, LANES), shape(1, LANES)),
+        in_specs=[VM] * (len(pieces) + len(weights) + 1) + [SM, VM],
         out_specs=(VM, VM),
         scratch_shapes=(
             pltpu.VMEM((ROWS, LANES), F32),
             pltpu.VMEM((32, DEPTH), BF16),
             pltpu.VMEM((OWN, LANES), F32),
-            pltpu.VMEM((TILES, 16, LANES), F32),
             *EVAL_SCRATCH,
         ),
-        compiler_params=PARAMS,
-    )(*pieces, *weights, pairs, counts, live3, energy)
+        compiler_params=limit(20),
+    )(*pieces, *weights, pairs, counts, energy)
 
 
 def swap(low_part, high_part, axis):
     count = lax.axis_size(axis)
     even = lax.axis_index(axis) % 2 == 0
+    across, within = jnp.where(even, low_part, high_part), jnp.where(even, high_part, low_part)
     inner = [(i, i ^ 1) for i in range(count)]
     outer = [(i, (i - 1) % count if i % 2 == 0 else (i + 1) % count) for i in range(count)]
-    with jax.named_scope("outer"):
-        across = lax.ppermute(jnp.where(even, low_part, high_part), axis, outer)
-    with jax.named_scope("inner"):
-        within = lax.ppermute(jnp.where(even, high_part, low_part), axis, inner)
+    across = lax.ppermute(across, axis, outer)
+    within = lax.ppermute(within, axis, inner)
     return jnp.where(even, across, within), jnp.where(even, within, across)
 
 
@@ -528,35 +705,17 @@
     return jnp.sum(rows, axis=0)
 
 
-def spread(rows):
-    low, high = swap(rows[:, :, 0:2], rows[:, :, 1:3], "gz")
-    rows = jnp.concatenate([low, rows, high, jnp.zeros((3, 3, 1, LANES), F32)], axis=2)
+def spread(rows, beside):
+    rows = rows.reshape(3, 3, 8, LANES)
+    low, high = swap(rows[:, :, 2:4], rows[:, :, 3:5], "gz")
+    rows = jnp.concatenate(
+        [low, rows[:, :, 2:5], high, jnp.zeros((3, 3, 1, LANES), F32)], axis=2
+    )
     low, high = swap(rows[0:2], rows[1:3], "gx")
     rows = jnp.concatenate([low, rows, high], axis=0)
+    rows, beside = lax.optimization_barrier((rows, beside))
     low, high = swap(rows[:, 0:2], rows[:, 1:3], "gy")
-    return low, rows, high
-
-
-def pack(positions, velocity, species, region_count, neighbours):
-    slots = lax.broadcasted_iota(jnp.int32, (3, 3, 3, 2), 3)
-    live = (slots < region_count[..., None]).astype(F32)
-    kind = species.astype(F32)
-    lists = neighbours[..., :LIST].astype(F32).reshape(3, 3, 3, 2 * LIST)
-
-    def thrice(v):
-        return jnp.broadcast_to(v[..., None], (3, 3, 3, 2, 3)).reshape(3, 3, 3, 6)
-
-    def vectors(v):
-        return v.transpose(1, 2, 3, 4, 0).reshape(3, 3, 3, 6)
-
-    def pad(count):
-        return jnp.zeros((3, 3, 3, count), F32)
-
-    return jnp.concatenate(
-        [vectors(positions), kind, thrice(kind), pad(2), lists, vectors(velocity), pad(2),
-         thrice(live), pad(2), live, pad(LANES - LIVE - 2)],
-        axis=-1,
-    ), thrice(live)
+    return (low, rows, high), beside
 
 
 def unpack(force):
@@ -566,28 +725,17 @@
 
 def shards(positions, velocity, species, region_count, neighbours,
            basis_weight, species_embed, weight_map, scalar_map, energy_out, species_energy):
-    rows, live3 = pack(positions, velocity, species, region_count, neighbours)
-    w1 = jnp.concatenate([basis_weight, species_embed, jnp.zeros((3, LAT), BF16)], axis=0)
-    weights = (
-        w1.T,
-        w1,
-        weight_map.T,
-        weight_map,
-        scalar_map.T,
-        scalar_map,
-        jnp.broadcast_to(energy_out[:, None], (LAT, LANES)),
-    )
-    live_rows = jnp.pad(live3, ((0, 0), (0, 0), (2, 3), (0, LANES - 6))).reshape(72, LANES)
-    force_one, moved, energy_one, pairs, counts = first_call(
-        spread(rows), weights, species_energy
-    )
-    moved = moved.reshape(3, 3, 8, LANES)[:, :, 2:5]
-    force_two, energies = second_call(
-        spread(moved), weights, pairs, counts, live_rows, energy_one
-    )
+    rows = pack_call(positions, velocity, species, region_count, neighbours)
+    prepared = prep_call(
+        basis_weight, species_embed, weight_map, scalar_map, energy_out, species_energy
+    )
+    pieces, prepared = spread(rows, prepared)
+    force_one, moved, energy_one, pairs, counts = first_call(pieces, prepared)
+    pieces, _ = spread(moved, ())
+    force_two, energies = second_call(pieces, prepared[0:7], pairs, counts, energy_one)
     totals = everywhere(everywhere(energies, ("gx", "gy")), ("gz",))
     forces = jnp.stack([unpack(force_one), unpack(force_two)])
-    return forces, totals[0, 0:2] / totals[0, 2]
+    return forces, totals[0, 0:2] / totals[0, 2:4]
 
 
 def solution(mesh):

time: 136 us -> 128 us (0.941)
  waiting for transfers between devices: 27.3 us -> 32 us
  local copies, waits for them, and re-layouts: 10.7 us -> 6.01 us
  Pallas kernels: 17 us -> 13.1 us
  starting transfers between devices: 76.9 us -> 73.6 us
    ppermute x12, waiting for transfers between devices: 10.2 us -> 14.9 us  [the longest x6 7.72 us: swap(): within = lax.ppermute(within, axis, inner)]
    pallas_call x2 -> x4, Pallas kernels: 17 us -> 13.1 us  [the longest x1 7.02 us: first_call(): pl.pallas_call(first_kernel, name='first', out_shape=(shape(72, LANES), s...]
    unnamed x26 -> x23, local copies, waits for them, and re-layouts: 7.06 us -> 4.55 us
    ppermute x12, starting transfers between devices: 58.5 us -> 56.1 us  [the longest x6 36.6 us: swap(): across = lax.ppermute(across, axis, outer)]
  transfers between devices with their start and end apart: 14 -> 14, of which waited for: 8 -> 9; matrix products, arithmetic and copies ran while one was open for 1% -> 1% of each run, Pallas kernels for 0% -> 0%
where the time goes in v3:
time: 128 us; the launch traced here: 127 us
  starting transfers between devices  73.6 us (57%)
  waiting for transfers between devices  32 us (25%)
  Pallas kernels  13.1 us (10%)
  local copies, waits for them, and re-layouts  6.01 us (5%)
    ppermute x6, starting transfers between devices, swap(): across = lax.ppermute(across, axis, outer)  36.6 us
    ppermute x6, starting transfers between devices, swap(): within = lax.ppermute(within, axis, inner)  19.5 us
    all_to_all x2, starting transfers between devices, everywhere(): rows = lax.all_to_all(rows, axes, 0, 0, tiled=False)  17.5 us
    all_to_all x2, waiting for transfers between devices, everywhere(): rows = lax.all_to_all(rows, axes, 0, 0, tiled=False)  17.1 us
    ppermute x6, waiting for transfers between devices, swap(): within = lax.ppermute(within, axis, inner)  7.72 us
    ppermute x6, waiting for transfers between devices, swap(): across = lax.ppermute(across, axis, outer)  7.19 us
    pallas_call x1, Pallas kernels, first_call(): pl.pallas_call(first_kernel, name='first', out_shape=(shape(72, LANES), s...  7.02 us
    pallas_call x1, Pallas kernels, second_call(): pl.pallas_call(second_kernel, name='second', out_shape=(shape(72, LANES),...  4.99 us
  transfers between devices with their start and end apart: 14, of which 9 were waited for; matrix products, arithmetic and copies ran while one was open for 1% of the time, Pallas kernels for 0%

profile of v3, /device:TPU:1, one launch (start us, length us, event | category | flops | bytes accessed | tf_op | source)
XLA Modules:
  0.0 126.7 jit_solution(13900701287242930221)
XLA Ops:
  4.1 5.9 %collective-permute-start = (f32[3,3,2,128]{3,2,1,0:T(2,128)S(1)}, f32[3,3,2,128]{3,2,1,0:T(2,128)S(1)}, u32[]{:S(2)}, u32[]{:S(2)}) collective-permute-start(f32[3,3,2,128]{3,2,1,0:T(2,128)S(1)} %get-tuple-element.82), channel_id=1, source_target_pairs={{0,7},{1,2},{2,1},{3,4},{4,3},{5,6},{6,5},{7,0},{8,15},{9,10},{10,... | collective-permute-start | bytes 27656 | tf_op jit(solution)/shard_map/ppermute | solution.py:696
  10.0 1.9 %collective-permute-start.1 = (f32[3,3,2,128]{3,2,1,0:T(2,128)S(1)}, f32[3,3,2,128]{3,2,1,0:T(2,128)S(1)}, u32[]{:S(2)}, u32[]{:S(2)}) collective-permute-start(f32[3,3,2,128]{3,2,1,0:T(2,128)S(1)} %get-tuple-element.83), channel_id=1, source_target_pairs={{0,1},{1,0},{2,3},{3,2},{4,5},{5,4},{6,7},{7,6},{8,9},{9,8},{10,11... | collective-permute-start | bytes 27656 | tf_op jit(solution)/shard_map/ppermute | solution.py:697
  12.0 2.4 %collective-permute-done.1 = f32[3,3,2,128]{3,2,1,0:T(2,128)S(1)} collective-permute-done((f32[3,3,2,128]{3,2,1,0:T(2,128)S(1)}, f32[3,3,2,128]{3,2,1,0:T(2,128)S(1)}, u32[]{:S(2)}, u32[]{:S(2)}) %collective-permute-start.1) | collective-permute-done | bytes 9248 | tf_op jit(solution)/shard_map/ppermute | solution.py:697
  14.5 8.0 %collective-permute-start.2 = (f32[2,3,8,128]{3,2,1,0:T(8,128)S(1)}, f32[2,3,8,128]{3,2,1,0:T(8,128)S(1)}, u32[]{:S(2)}, u32[]{:S(2)}) collective-permute-start(f32[2,3,8,128]{3,2,1,0:T(8,128)S(1)} %get-tuple-element.80), channel_id=1, source_target_pairs={{0,704},{64,128},{128,64},{192,256},{256,192},{320,384},{384,320},... | collective-permute-start | bytes 73736 | tf_op jit(solution)/shard_map/ppermute | solution.py:696
  22.6 1.9 %collective-permute-start.3 = (f32[2,3,8,128]{3,2,1,0:T(8,128)S(1)}, f32[2,3,8,128]{3,2,1,0:T(8,128)S(1)}, u32[]{:S(2)}, u32[]{:S(2)}) collective-permute-start(f32[2,3,8,128]{3,2,1,0:T(8,128)S(1)} %get-tuple-element.81), channel_id=1, source_target_pairs={{0,64},{64,0},{128,192},{192,128},{256,320},{320,256},{384,448},{4... | collective-permute-start | bytes 73736 | tf_op jit(solution)/shard_map/ppermute | solution.py:697
  25.9 1.3 collective-permute-done.3
  27.2 5.7 %collective-permute-start.5 = (f32[7,2,8,128]{3,2,1,0:T(8,128)S(1)}, f32[7,2,8,128]{3,2,1,0:T(8,128)S(1)}, u32[]{:S(2)}, u32[]{:S(2)}) collective-permute-start(f32[7,2,8,128]{3,2,1,0:T(8,128)S(1)} %get-tuple-element.70), channel_id=1, source_target_pairs={{0,8},{8,0},{16,24},{24,16},{32,40},{40,32},{48,56},{56,48},{1,9},... | collective-permute-start | bytes 172040 | tf_op jit(solution)/shard_map/ppermute | solution.py:697
  32.9 8.5 %collective-permute-start.4 = (f32[7,2,8,128]{3,2,1,0:T(8,128)S(1)}, f32[7,2,8,128]{3,2,1,0:T(8,128)S(1)}, u32[]{:S(2)}, u32[]{:S(2)}) collective-permute-start(f32[7,2,8,128]{3,2,1,0:T(8,128)S(1)} %get-tuple-element.71), channel_id=1, source_target_pairs={{0,56},{8,16},{16,8},{24,32},{32,24},{40,48},{48,40},{56,0},{1,57}... | collective-permute-start | bytes 172040 | tf_op jit(solution)/shard_map/ppermute | solution.py:696
  41.4 1.8 %collective-permute-done.4 = f32[7,2,8,128]{3,2,1,0:T(8,128)S(1)} collective-permute-done((f32[7,2,8,128]{3,2,1,0:T(8,128)S(1)}, f32[7,2,8,128]{3,2,1,0:T(8,128)S(1)}, u32[]{:S(2)}, u32[]{:S(2)}) %collective-permute-start.4) | collective-permute-done | bytes 57376 | tf_op jit(solution)/shard_map/ppermute | solution.py:696
  43.2 7.0 %first.1 = (f32[72,128]{1,0:T(8,128)S(1)}, f32[72,128]{1,0:T(8,128)S(1)}, f32[1,128]{1,0:T(1,128)S(1)}, f32[26,16,256]{2,1,0:T(8,128)S(1)}, s32[2]{0:T(128)S(1)}) custom-call(f32[7,2,8,128]{3,2,1,0:T(8,128)S(1)} %get-tuple-element.67.low, f32[7,3,8,128]{3,2,1,0:T(8,128)S(1)} %fusion.1.own, f32[7,2,8,128]{3,2,1,0:T(8,128)S(1)} %get-tuple-element.66.high, ...), custom_call_target="tpu_custom_call" | custom-call | tf_op jit(solution)/shard_map/first/pallas_call | solution.py:648
  50.3 2.3 %collective-permute-start.6 = (f32[3,3,2,128]{3,2,1,0:T(2,128)S(1)}, f32[3,3,2,128]{3,2,1,0:T(2,128)S(1)}, u32[]{:S(2)}, u32[]{:S(2)}) collective-permute-start(f32[3,3,2,128]{3,2,1,0:T(2,128)S(1)} %get-tuple-element.78), channel_id=1, source_target_pairs={{0,7},{1,2},{2,1},{3,4},{4,3},{5,6},{6,5},{7,0},{8,15},{9,10},{10,... | collective-permute-start | bytes 27656 | tf_op jit(solution)/shard_map/ppermute | solution.py:696
  52.6 3.0 %collective-permute-start.7 = (f32[3,3,2,128]{3,2,1,0:T(2,128)S(1)}, f32[3,3,2,128]{3,2,1,0:T(2,128)S(1)}, u32[]{:S(2)}, u32[]{:S(2)}) collective-permute-start(f32[3,3,2,128]{3,2,1,0:T(2,128)S(1)} %get-tuple-element.79), channel_id=1, source_target_pairs={{0,1},{1,0},{2,3},{3,2},{4,5},{5,4},{6,7},{7,6},{8,9},{9,8},{10,11... | collective-permute-start | bytes 27656 | tf_op jit(solution)/shard_map/ppermute | solution.py:697
  55.9 1.1 collective-permute-done.7
  57.1 9.4 %collective-permute-start.8 = (f32[2,3,8,128]{3,2,1,0:T(8,128)S(1)}, f32[2,3,8,128]{3,2,1,0:T(8,128)S(1)}, u32[]{:S(2)}, u32[]{:S(2)}) collective-permute-start(f32[2,3,8,128]{3,2,1,0:T(8,128)S(1)} %get-tuple-element.76), channel_id=1, source_target_pairs={{0,704},{64,128},{128,64},{192,256},{256,192},{320,384},{384,320},... | collective-permute-start | bytes 73736 | tf_op jit(solution)/shard_map/ppermute | solution.py:696
  66.5 1.9 %collective-permute-start.9 = (f32[2,3,8,128]{3,2,1,0:T(8,128)S(1)}, f32[2,3,8,128]{3,2,1,0:T(8,128)S(1)}, u32[]{:S(2)}, u32[]{:S(2)}) collective-permute-start(f32[2,3,8,128]{3,2,1,0:T(8,128)S(1)} %get-tuple-element.77), channel_id=1, source_target_pairs={{0,64},{64,0},{128,192},{192,128},{256,320},{320,256},{384,448},{4... | collective-permute-start | bytes 73736 | tf_op jit(solution)/shard_map/ppermute | solution.py:697
  68.4 2.9 %collective-permute-done.9 = f32[2,3,8,128]{3,2,1,0:T(8,128)S(1)} collective-permute-done((f32[2,3,8,128]{3,2,1,0:T(8,128)S(1)}, f32[2,3,8,128]{3,2,1,0:T(8,128)S(1)}, u32[]{:S(2)}, u32[]{:S(2)}) %collective-permute-start.9) | collective-permute-done | bytes 24608 | tf_op jit(solution)/shard_map/ppermute | solution.py:697
  71.4 5.1 %collective-permute-start.11 = (f32[7,2,8,128]{3,2,1,0:T(8,128)S(1)}, f32[7,2,8,128]{3,2,1,0:T(8,128)S(1)}, u32[]{:S(2)}, u32[]{:S(2)}) collective-permute-start(f32[7,2,8,128]{3,2,1,0:T(8,128)S(1)} %get-tuple-element.68), channel_id=1, source_target_pairs={{0,8},{8,0},{16,24},{24,16},{32,40},{40,32},{48,56},{56,48},{1,9},... | collective-permute-start | bytes 172040 | tf_op jit(solution)/shard_map/ppermute | solution.py:697
  76.5 2.5 %collective-permute-start.10 = (f32[7,2,8,128]{3,2,1,0:T(8,128)S(1)}, f32[7,2,8,128]{3,2,1,0:T(8,128)S(1)}, u32[]{:S(2)}, u32[]{:S(2)}) collective-permute-start(f32[7,2,8,128]{3,2,1,0:T(8,128)S(1)} %get-tuple-element.69), channel_id=1, source_target_pairs={{0,56},{8,16},{16,8},{24,32},{32,24},{40,48},{48,40},{56,0},{1,57}... | collective-permute-start | bytes 172040 | tf_op jit(solution)/shard_map/ppermute | solution.py:696
  79.0 5.1 %collective-permute-done.10 = f32[7,2,8,128]{3,2,1,0:T(8,128)S(1)} collective-permute-done((f32[7,2,8,128]{3,2,1,0:T(8,128)S(1)}, f32[7,2,8,128]{3,2,1,0:T(8,128)S(1)}, u32[]{:S(2)}, u32[]{:S(2)}) %collective-permute-start.10) | collective-permute-done | bytes 57376 | tf_op jit(solution)/shard_map/ppermute | solution.py:696
  84.1 5.0 %second.1 = (f32[72,128]{1,0:T(8,128)S(1)}, f32[1,128]{1,0:T(1,128)S(1)}) custom-call(f32[7,2,8,128]{3,2,1,0:T(8,128)S(1)} %get-tuple-element.65.low, f32[7,3,8,128]{3,2,1,0:T(8,128)S(1)} %fusion.3.own, f32[7,2,8,128]{3,2,1,0:T(8,128)S(1)} %get-tuple-element.64.high, bf16[128,16]{1,0:T(8,128)(2,1)S(1)} %get-tuple-element.41.w1t, ...), custom_call_target="tpu_custom_call" | custom-call | tf_op jit(solution)/shard_map/second/pallas_call | solution.py:674
  89.7 11.6 %all-to-all-start = ((f32[96,1,128]{2,1,0:T(1,128)}), f32[96,1,128]{2,1,0:T(1,128)S(1)}, u32[]{:S(2)}, u32[]{:S(2)}) async-start(f32[96,1,128]{2,1,0:T(1,128)} %broadcast_in_dim.23), calls=%async_computation | async-start | bytes 98304 | tf_op jit(solution)/shard_map/all_to_all | solution.py:704
  101.5 11.5 %all-to-all-done = f32[96,1,128]{2,1,0:T(1,128)S(1)} async-done(((f32[96,1,128]{2,1,0:T(1,128)}), f32[96,1,128]{2,1,0:T(1,128)S(1)}, u32[]{:S(2)}, u32[]{:S(2)}) %all-to-all-start) | async-done | bytes 49184 | tf_op jit(solution)/shard_map/all_to_all | solution.py:704
  113.7 5.9 %all-to-all-start.1 = ((f32[8,1,128]{2,1,0:T(1,128)}), f32[8,1,128]{2,1,0:T(1,128)S(1)}, u32[]{:S(2)}, u32[]{:S(2)}) async-start(f32[8,1,128]{2,1,0:T(1,128)} %broadcast_in_dim.24), calls=%async_computation.1 | async-start | bytes 8192 | tf_op jit(solution)/shard_map/all_to_all | solution.py:704
  120.5 5.6 %all-to-all-done.1 = f32[8,1,128]{2,1,0:T(1,128)S(1)} async-done(((f32[8,1,128]{2,1,0:T(1,128)}), f32[8,1,128]{2,1,0:T(1,128)S(1)}, u32[]{:S(2)}, u32[]{:S(2)}) %all-to-all-start.1) | async-done | bytes 4128 | tf_op jit(solution)/shard_map/all_to_all | solution.py:704
  (60 shorter events, 8.3 us)
Async XLA Ops:
  0.6 0.7 copy-start
  0.6 0.7 copy-start.6
  1.4 0.7 copy-start.1
  2.1 0.7 copy-start.2
  2.9 0.7 copy-start.5
  4.1 7.9 %collective-permute-start = (f32[3,3,2,128]{3,2,1,0:T(2,128)S(1)}, f32[3,3,2,128]{3,2,1,0:T(2,128)S(1)}, u32[]{:S(2)}, u32[]{:S(2)}) collective-permute-start(f32[3,3,2,128]{3,2,1,0:T(2,128)S(1)} %get-tuple-element.82), channel_id=1, source_target_pairs={{0,7},{1,2},{2,1},{3,4},{4,3},{5,6},{6,5},{7,0},{8,15},{9,10},{10,... | collective-permute-start | bytes 27656 | tf_op jit(solution)/shard_map/ppermute | solution.py:696
  10.0 4.4 %collective-permute-start.1 = (f32[3,3,2,128]{3,2,1,0:T(2,128)S(1)}, f32[3,3,2,128]{3,2,1,0:T(2,128)S(1)}, u32[]{:S(2)}, u32[]{:S(2)}) collective-permute-start(f32[3,3,2,128]{3,2,1,0:T(2,128)S(1)} %get-tuple-element.83), channel_id=1, source_target_pairs={{0,1},{1,0},{2,3},{3,2},{4,5},{5,4},{6,7},{7,6},{8,9},{9,8},{10,11... | collective-permute-start | bytes 27656 | tf_op jit(solution)/shard_map/ppermute | solution.py:697
  14.5 10.0 %copy-start.8 = (bf16[5,128]{1,0:T(8,128)(2,1)S(1)}, bf16[5,128]{1,0:T(8,128)(2,1)}, u32[]{:S(2)}) copy-start(bf16[5,128]{1,0:T(8,128)(2,1)} %se_in.1) | copy-start | bytes 3844
  14.5 11.3 %collective-permute-start.2 = (f32[2,3,8,128]{3,2,1,0:T(8,128)S(1)}, f32[2,3,8,128]{3,2,1,0:T(8,128)S(1)}, u32[]{:S(2)}, u32[]{:S(2)}) collective-permute-start(f32[2,3,8,128]{3,2,1,0:T(8,128)S(1)} %get-tuple-element.80), channel_id=1, source_target_pairs={{0,704},{64,128},{128,64},{192,256},{256,192},{320,384},{384,320},... | collective-permute-start | bytes 73736 | tf_op jit(solution)/shard_map/ppermute | solution.py:696
  22.5 2.0 %copy-start.9 = (f32[128]{0:T(128)S(1)}, f32[128]{0:T(128)}, u32[]{:S(2)}) copy-start(f32[128]{0:T(128)} %param.20) | copy-start | bytes 1540
  22.5 2.0 %copy-start.10 = (f32[5]{0:T(128)S(1)}, f32[5]{0:T(128)}, u32[]{:S(2)}) copy-start(f32[5]{0:T(128)} %param.21) | copy-start | bytes 64
  22.6 4.6 %collective-permute-start.3 = (f32[2,3,8,128]{3,2,1,0:T(8,128)S(1)}, f32[2,3,8,128]{3,2,1,0:T(8,128)S(1)}, u32[]{:S(2)}, u32[]{:S(2)}) collective-permute-start(f32[2,3,8,128]{3,2,1,0:T(8,128)S(1)} %get-tuple-element.81), channel_id=1, source_target_pairs={{0,64},{64,0},{128,192},{192,128},{256,320},{320,256},{384,448},{4... | collective-permute-start | bytes 73736 | tf_op jit(solution)/shard_map/ppermute | solution.py:697
  24.5 0.7 copy-start.3
  24.5 0.7 copy-start.4
  27.2 14.2 %collective-permute-start.5 = (f32[7,2,8,128]{3,2,1,0:T(8,128)S(1)}, f32[7,2,8,128]{3,2,1,0:T(8,128)S(1)}, u32[]{:S(2)}, u32[]{:S(2)}) collective-permute-start(f32[7,2,8,128]{3,2,1,0:T(8,128)S(1)} %get-tuple-element.70), channel_id=1, source_target_pairs={{0,8},{8,0},{16,24},{24,16},{32,40},{40,32},{48,56},{56,48},{1,9},... | collective-permute-start | bytes 172040 | tf_op jit(solution)/shard_map/ppermute | solution.py:697
  32.9 10.3 %collective-permute-start.4 = (f32[7,2,8,128]{3,2,1,0:T(8,128)S(1)}, f32[7,2,8,128]{3,2,1,0:T(8,128)S(1)}, u32[]{:S(2)}, u32[]{:S(2)}) collective-permute-start(f32[7,2,8,128]{3,2,1,0:T(8,128)S(1)} %get-tuple-element.71), channel_id=1, source_target_pairs={{0,56},{8,16},{16,8},{24,32},{32,24},{40,48},{48,40},{56,0},{1,57}... | collective-permute-start | bytes 172040 | tf_op jit(solution)/shard_map/ppermute | solution.py:696
  50.3 5.6 %collective-permute-start.6 = (f32[3,3,2,128]{3,2,1,0:T(2,128)S(1)}, f32[3,3,2,128]{3,2,1,0:T(2,128)S(1)}, u32[]{:S(2)}, u32[]{:S(2)}) collective-permute-start(f32[3,3,2,128]{3,2,1,0:T(2,128)S(1)} %get-tuple-element.78), channel_id=1, source_target_pairs={{0,7},{1,2},{2,1},{3,4},{4,3},{5,6},{6,5},{7,0},{8,15},{9,10},{10,... | collective-permute-start | bytes 27656 | tf_op jit(solution)/shard_map/ppermute | solution.py:696
  52.6 4.4 %collective-permute-start.7 = (f32[3,3,2,128]{3,2,1,0:T(2,128)S(1)}, f32[3,3,2,128]{3,2,1,0:T(2,128)S(1)}, u32[]{:S(2)}, u32[]{:S(2)}) collective-permute-start(f32[3,3,2,128]{3,2,1,0:T(2,128)S(1)} %get-tuple-element.79), channel_id=1, source_target_pairs={{0,1},{1,0},{2,3},{3,2},{4,5},{5,4},{6,7},{7,6},{8,9},{9,8},{10,11... | collective-permute-start | bytes 27656 | tf_op jit(solution)/shard_map/ppermute | solution.py:697
  57.1 11.3 %collective-permute-start.8 = (f32[2,3,8,128]{3,2,1,0:T(8,128)S(1)}, f32[2,3,8,128]{3,2,1,0:T(8,128)S(1)}, u32[]{:S(2)}, u32[]{:S(2)}) collective-permute-start(f32[2,3,8,128]{3,2,1,0:T(8,128)S(1)} %get-tuple-element.76), channel_id=1, source_target_pairs={{0,704},{64,128},{128,64},{192,256},{256,192},{320,384},{384,320},... | collective-permute-start | bytes 73736 | tf_op jit(solution)/shard_map/ppermute | solution.py:696
  66.5 4.9 %collective-permute-start.9 = (f32[2,3,8,128]{3,2,1,0:T(8,128)S(1)}, f32[2,3,8,128]{3,2,1,0:T(8,128)S(1)}, u32[]{:S(2)}, u32[]{:S(2)}) collective-permute-start(f32[2,3,8,128]{3,2,1,0:T(8,128)S(1)} %get-tuple-element.77), channel_id=1, source_target_pairs={{0,64},{64,0},{128,192},{192,128},{256,320},{320,256},{384,448},{4... | collective-permute-start | bytes 73736 | tf_op jit(solution)/shard_map/ppermute | solution.py:697
  71.4 7.6 %collective-permute-start.11 = (f32[7,2,8,128]{3,2,1,0:T(8,128)S(1)}, f32[7,2,8,128]{3,2,1,0:T(8,128)S(1)}, u32[]{:S(2)}, u32[]{:S(2)}) collective-permute-start(f32[7,2,8,128]{3,2,1,0:T(8,128)S(1)} %get-tuple-element.68), channel_id=1, source_target_pairs={{0,8},{8,0},{16,24},{24,16},{32,40},{40,32},{48,56},{56,48},{1,9},... | collective-permute-start | bytes 172040 | tf_op jit(solution)/shard_map/ppermute | solution.py:697
  76.5 7.6 %collective-permute-start.10 = (f32[7,2,8,128]{3,2,1,0:T(8,128)S(1)}, f32[7,2,8,128]{3,2,1,0:T(8,128)S(1)}, u32[]{:S(2)}, u32[]{:S(2)}) collective-permute-start(f32[7,2,8,128]{3,2,1,0:T(8,128)S(1)} %get-tuple-element.69), channel_id=1, source_target_pairs={{0,56},{8,16},{16,8},{24,32},{32,24},{40,48},{48,40},{56,0},{1,57}... | collective-permute-start | bytes 172040 | tf_op jit(solution)/shard_map/ppermute | solution.py:696
  89.7 23.3 %all-to-all-start = ((f32[96,1,128]{2,1,0:T(1,128)}), f32[96,1,128]{2,1,0:T(1,128)S(1)}, u32[]{:S(2)}, u32[]{:S(2)}) async-start(f32[96,1,128]{2,1,0:T(1,128)} %broadcast_in_dim.23), calls=%async_computation | async-start | bytes 98304 | tf_op jit(solution)/shard_map/all_to_all | solution.py:704
  113.7 12.5 %all-to-all-start.1 = ((f32[8,1,128]{2,1,0:T(1,128)}), f32[8,1,128]{2,1,0:T(1,128)S(1)}, u32[]{:S(2)}, u32[]{:S(2)}) async-start(f32[8,1,128]{2,1,0:T(1,128)} %broadcast_in_dim.24), calls=%async_computation.1 | async-start | bytes 8192 | tf_op jit(solution)/shard_map/all_to_all | solution.py:704
  (1 other events, 0.7 us)

commit v4 on v3

--- a/solution.py
+++ b/solution.py
@@ -22,12 +22,14 @@
 LISTED = 40
 USED = 392
 ROWS = 400
+SPARSE = 448
 DEPTH = 512
 INNER = 256
 OWN = 80
 WIDE = 256
 TILES = 26
 LANES = 128
+HALF = 64
 POS, KIND, VEL, LIVE, NEIGH = 0, 6, 8, 14, 16
 MISC = NEIGH + 2 * LIST
 F32 = jnp.float32
@@ -105,33 +107,38 @@
     keys = keys.astype(BF16)
     ones = jnp.ones((LANES, LANES), BF16)
     cx, cy, cz = row_coords(iota((1, DEPTH), 1))
-    first = jnp.float32(0.0)
-    totals = []
-    for keep in kept:
-        keep16 = deepen(keep.astype(F32).astype(BF16), DEPTH)
-        key_t = mm_nt(keys, keep16)
-        count = mm(keep16, ones)
-        count_t = mm_nt(ones[0:16], keep16)
-        below = below_ref[...]
-        offset = mm(below, count.astype(BF16)) + first
-        offset_t = mm_nt(count_t.astype(BF16), below)[0:1] + first
-        end = offset + count[0:ROWS]
-        off_ref[...] = offset
-        end_ref[...] = end
-        total = jnp.max(end)
+    keeps = [deepen(keep.astype(F32).astype(BF16), DEPTH) for keep in kept]
+    counts = [mm(keep, ones) for keep in keeps]
+    counts_t = [mm_nt(ones[0:16], keep).astype(BF16) for keep in keeps]
+    below = below_ref[...]
+    offsets = mm(below, jnp.concatenate(counts, axis=1).astype(BF16))
+    offsets_t = mm_nt(jnp.concatenate(counts_t, axis=0), below)
+    first = jnp.zeros((1, 1), F32)
+    ends = []
+    for which, keep in enumerate(keeps):
+        offset = offsets[:, which * LANES : (which + 1) * LANES] + first
+        end = offset + counts[which][0:ROWS]
+        off_ref[which] = offset
+        end_ref[which] = end
+        offset_t = offsets_t[16 * which : 16 * which + 1] + first
         offset_t = jnp.concatenate([offset_t, jnp.zeros((1, DEPTH - ROWS), F32)], axis=1)
         high = jnp.floor(offset_t * (1.0 / 256.0))
         misc = jnp.concatenate(
             [high, offset_t - 256.0 * high, cx, cy, cz, jnp.zeros((11, DEPTH), F32)], axis=0
         )
-        table[0 : 2 * LIST] = listed_t
-        table[2 * LIST : 4 * LIST] = key_t.astype(BF16)
-        table[4 * LIST :] = misc.astype(BF16)
-
-        def body(k, carry, first=first, total=total):
+        table[which, 0 : 2 * LIST] = listed_t
+        table[which, 2 * LIST : 4 * LIST] = mm_nt(keys, keep).astype(BF16)
+        table[which, 4 * LIST :] = misc.astype(BF16)
+        first = jnp.max(jnp.max(end, axis=0, keepdims=True), axis=1, keepdims=True)
+        ends.append(jnp.max(first))
+    first = jnp.float32(0.0)
+    totals = []
+    for which, total in enumerate(ends):
+
+        def body(k, carry, which=which, first=first, total=total):
             place = iota((1, WIDE), 1) + (k * WIDE).astype(F32)
-            offset = off_ref[...]
-            end = end_ref[...]
+            offset = off_ref[which]
+            end = end_ref[which]
             hit = jnp.concatenate(
                 [
                     ((offset <= part) & (end > part)).astype(F32).astype(BF16)
@@ -139,7 +146,7 @@
                 ],
                 axis=1,
             )
-            got = mm(table[...], deepen(hit, DEPTH))
+            got = mm(table[which], deepen(hit, DEPTH))
             misc = got[4 * LIST :]
             wanted = 2.0 * (place - (256.0 * misc[0:1] + misc[1:2])) + 1.0
             chosen = (got[2 * LIST : 4 * LIST] == wanted).astype(F32)
@@ -153,8 +160,8 @@
             def where(flag, value):
                 return jnp.where(flag, value, -1.0)
 
-            def region(c):
-                return (c[0] * 7.0 + c[1]) * 8.0 + c[2]
+            def region(c, layers):
+                return (c[0] * layers + c[1]) * 8.0 + c[2]
 
             def inner(c, s):
                 return (((c[0] - 1.0) * 5.0 + (c[1] - 1.0)) * 5.0 + (c[2] - 1.0)) * 2.0 + s
@@ -164,9 +171,9 @@
 
             near = (x, y, z)
             lines = [
-                where(valid, region(near)),
+                where(valid, region(near, 7.0)),
                 slot,
-                where(valid, region(far)),
+                where(valid, region(far, 7.0)),
                 far_slot,
                 where(valid & (away_i < 2.5), inner(near, slot)),
                 where(valid & (away_j < 2.5), inner(far, far_slot)),
@@ -175,7 +182,9 @@
                 valid.astype(F32),
                 *shift,
                 (valid & (away_i < 1.5)).astype(F32),
-                jnp.zeros((3, WIDE), F32),
+                where(valid, region(near, 8.0)),
+                where(valid, region(far, 8.0)),
+                jnp.zeros((9, WIDE), F32),
             ]
             pairs_ref[k] = jnp.where(place < first, pairs_ref[k], jnp.concatenate(lines, axis=0))
             return carry
@@ -204,7 +213,7 @@
     return 2.0 * s * c, 1.0 - 2.0 * s * s
 
 
-def evaluate(refs, scratch, counts, own_out):
+def evaluate(refs, scratch, counts, own_out, moved):
     pos_t, pairs_ref, w1t, w1, wmt, wm, smt, sm, eo_ref = refs
     env_ref, envs_ref, grad_ref, geo_ref, lat_ref, slope_ref, h_ref, wb_ref, hp_ref, en_ref = (
         scratch
@@ -221,7 +230,7 @@
     own_out[...] = jnp.zeros(own_out.shape, F32)
 
     def gathered(index, slot):
-        got = mm(pos_t[...], one_hot(index, ROWS, DEPTH))
+        got = mm(pos_t[...], one_hot(index, SPARSE if moved else ROWS, DEPTH))
         full = got[0:8] + got[8:16] + got[16:24]
         second = slot > 0.5
         point = jnp.where(second, full[3:6], full[0:3])
@@ -230,8 +239,14 @@
     def stage_one(t, carry):
         pair = pairs_ref[t]
         valid = pair[8:9]
-        near, near_kind = gathered(pair[0:1], pair[1:2])
-        far, far_kind = gathered(pair[2:3], pair[3:4])
+        if moved:
+            near, _ = gathered(pair[13:14], pair[1:2])
+            far, _ = gathered(pair[14:15], pair[3:4])
+            near_kind, far_kind = pair[15:16], pair[16:17]
+        else:
+            near, near_kind = gathered(pair[0:1], pair[1:2])
+            far, far_kind = gathered(pair[2:3], pair[3:4])
+            pairs_ref[t, 15:17] = jnp.concatenate([near_kind, far_kind], axis=0)
         d = far - near + pair[9:12]
         square = jnp.sum(d * d, axis=0, keepdims=True)
         square = jnp.where(valid > 0.5, square, 1.0)
@@ -377,10 +392,13 @@
 def load_rows(rows_ref, low, own, high):
     rows_ref[0:ROWS] = jnp.zeros((ROWS, LANES), F32)
     for i in range(7):
-        for piece, start, width in ((low, 0, 2), (own, 2, 3), (high, 5, 2)):
-            for j in range(width):
-                at = (i * 7 + start + j) * 8
-                rows_ref[at : at + 8] = piece[i, j]
+        at = i * 56
+        for piece, start in ((low, 0), (high, 40)):
+            both = piece[i]
+            rows_ref[at + start : at + start + 8] = both
+            rows_ref[at + start + 8 : at + start + 16] = pltpu.roll(both, HALF, 1)
+        for j in range(3):
+            rows_ref[at + 16 + 8 * j : at + 24 + 8 * j, 0:HALF] = own[i, j]
 
 
 def own_rows(rows_ref):
@@ -389,10 +407,7 @@
     )
 
 
-def position_rows(rows_ref, pos_t):
-    rows = jnp.concatenate([rows_ref[0:ROWS], jnp.zeros((DEPTH - ROWS, LANES), F32)], axis=0)
-    turned = jnp.transpose(rows)
-    top = turned[0:8]
+def put_positions(top, pos_t):
     one = top.astype(BF16)
     rest = top - one.astype(F32)
     two = rest.astype(BF16)
@@ -400,14 +415,6 @@
     pos_t[...] = jnp.concatenate(
         [one.astype(F32), two.astype(F32), three.astype(F32), jnp.zeros((8, DEPTH), F32)], axis=0
     ).astype(BF16)
-    return turned
-
-
-def energy_row(first, second, live):
-    lane = iota((1, LANES), 1)
-    return jnp.where(lane == 0.0, first, 0.0) + jnp.where(lane == 1.0, second, 0.0) + jnp.where(
-        lane == 2.0, live, 0.0
-    )
 
 
 def fetch(copies, sems):
@@ -422,8 +429,9 @@
     return wait
 
 
-def pack_kernel(pos_in, vel_in, kind_in, count_in, list_in, out, pos, vel, kind, count, lists, sems,
-                grid, first_list, second_list):
+def pack_kernel(pos_in, vel_in, kind_in, count_in, list_in, out, across, within,
+                pos, vel, kind, count, lists, sems, grid, first_list, second_list):
+    even = lax.axis_index("gz") % 2 == 0
     fetch(
         ((pos_in, pos), (vel_in, vel), (kind_in, kind), (count_in, count), (list_in, lists)), sems
     )()
@@ -454,7 +462,10 @@
         one = pltpu.roll(first_list[xy * 8 : xy * 8 + 8], NEIGH, 1)
         two = pltpu.roll(second_list[xy * 8 : xy * 8 + 8], NEIGH + LIST, 1)
         merged = jnp.where(lane < NEIGH, fields, jnp.where(lane < NEIGH + LIST, one, two))
-        out[xy] = jnp.where(inside & (lane < MISC), merged, 0.0)
+        merged = jnp.where(inside & (lane < MISC), merged, 0.0)
+        out[xy] = merged
+        across[xy] = jnp.where(even, merged[2:4], merged[3:5])
+        within[xy] = jnp.where(even, merged[3:5], merged[2:4])
 
 
 def prep_kernel(bw_in, se_in, wmt_in, sm_in, eo_in, table_in,
@@ -501,29 +512,36 @@
 
 
 def first_kernel(low, own, high, w1t, w1, wmt, wm, smt, sm, eo, base, below, levels,
-                 force_out, moved_out, energy_out, pairs_ref, counts_ref,
+                 force_out, moved_out, live_out, energy_out, pairs_ref, counts_ref,
                  rows_ref, table, off_ref, end_ref, pos_t, own_ref, *scratch):
     load_rows(rows_ref, low, own, high)
-    turned = position_rows(rows_ref, pos_t)
+    turned = jnp.transpose(deepen(rows_ref[0:ROWS], DEPTH))
+    put_positions(turned[0:8], pos_t)
     front, every = build_pairs(
         rows_ref, base, below, table, off_ref, end_ref, pairs_ref, turned[NEIGH:MISC].astype(BF16)
     )
     counts_ref[0] = front
     counts_ref[1] = every
     refs = (pos_t, pairs_ref, w1t, w1, wmt, wm, smt, sm, eo)
-    evaluate(refs, scratch, (front, every), own_ref)
+    evaluate(refs, scratch, (front, every), own_ref, False)
     mine = own_rows(rows_ref)
     lane, inside = own_lane_row()
     kind3 = lanes_of(mine, lane, KIND, KIND + 1)
     speed = pltpu.roll(mine, LANES - VEL, 1)
-    force = own_ref[0:72] * lanes_of(mine, lane, LIVE, LIVE + 1)
-    force = jnp.where(inside & (lane < 6.0), force, 0.0)
+    live3 = jnp.where(inside & (lane < 6.0), lanes_of(mine, lane, LIVE, LIVE + 1), 0.0)
+    live_out[...] = live3
+    force = jnp.where(inside & (lane < 6.0), own_ref[0:72] * live3, 0.0)
     force_out[...] = force
     inverse_mass = jnp.zeros((72, LANES), F32)
     for k, mass in enumerate(atom_masses):
         inverse_mass = jnp.where(kind3 == float(k), 1.0 / mass, inverse_mass)
     moved = mine + time_step * speed + 0.5 * time_step * time_step * inverse_mass * force
-    moved_out[...] = jnp.where(lane < 6.0, moved, jnp.where(lane < float(NEIGH), mine, 0.0))
+    moved = jnp.where(lane < 6.0, moved, 0.0)
+    for y in range(3):
+        moved_out[y] = sum(
+            pltpu.roll(moved[(x * 3 + y) * 8 : (x * 3 + y) * 8 + 8], (x + 2) * 16, 1)
+            for x in range(3)
+        )
     live = pltpu.roll(mine, LANES - LIVE + KIND, 1)
     live = jnp.where(inside & (lane > 5.5) & (lane < 7.5), live, 0.0)
     atom = jnp.zeros((72, LANES), F32)
@@ -534,15 +552,16 @@
 
 
 def second_kernel(low, own, high, w1t, w1, wmt, wm, smt, sm, eo, pairs_ref, counts_ref, energy_in,
-                  force_out, energy_out, rows_ref, pos_t, own_ref, *scratch):
-    load_rows(rows_ref, low, own, high)
-    position_rows(rows_ref, pos_t)
+                  live, force_out, energy_out, pos_t, own_ref, *scratch):
+    layers = [piece[i] for piece, width in ((low, 2), (own, 3), (high, 2)) for i in range(width)]
+    turned = jnp.transpose(deepen(jnp.concatenate(layers, axis=0), LANES))
+    blocks = [turned[x * 16 : x * 16 + 8] for x in range(7)] + [jnp.zeros((8, LANES), F32)]
+    top = [blocks[x] + pltpu.roll(blocks[x + 1], HALF, 1) for x in range(0, 8, 2)]
+    put_positions(jnp.concatenate(top, axis=1), pos_t)
     refs = (pos_t, pairs_ref, w1t, w1, wmt, wm, smt, sm, eo)
-    evaluate(refs, scratch, (counts_ref[0], counts_ref[1]), own_ref)
-    mine = own_rows(rows_ref)
+    evaluate(refs, scratch, (counts_ref[0], counts_ref[1]), own_ref, True)
     lane, inside = own_lane_row()
-    force = own_ref[0:72] * lanes_of(mine, lane, LIVE, LIVE + 1)
-    force_out[...] = jnp.where(inside & (lane < 6.0), force, 0.0)
+    force_out[...] = jnp.where(inside & (lane < 6.0), own_ref[0:72] * live[...], 0.0)
     energy_out[...] = energy_in[...] + energy_row(0.0, jnp.sum(scratch[-1][0:1]), 0.0)
 
 
@@ -584,9 +603,9 @@
     return pl.pallas_call(
         pack_kernel,
         name="pack",
-        out_shape=shape(9, 8, LANES),
+        out_shape=(shape(9, 8, LANES), shape(9, 2, LANES), shape(9, 2, LANES)),
         in_specs=[HB] * 5,
-        out_specs=VM,
+        out_specs=(VM, VM, VM),
         scratch_shapes=(
             pltpu.VMEM((3, 3, 3, 2, 3), F32),
             pltpu.VMEM((3, 3, 3, 2, 3), F32),
@@ -598,7 +617,6 @@
             pltpu.VMEM((72, LANES), F32),
             pltpu.VMEM((72, LANES), F32),
         ),
-        compiler_params=limit(4),
     )(
         positions.transpose(0, 1, 2, 4, 3),
         velocity.transpose(0, 1, 2, 4, 3),
@@ -650,18 +668,19 @@
         name="first",
         out_shape=(
             shape(72, LANES),
+            shape(3, 8, LANES),
             shape(72, LANES),
             shape(1, LANES),
-            shape(TILES, 16, WIDE),
+            shape(TILES, 24, WIDE),
             shape(2, kind=jnp.int32),
         ),
         in_specs=[VM] * (len(pieces) + len(prepared)),
-        out_specs=(VM, VM, VM, VM, SM),
+        out_specs=(VM, VM, VM, VM, VM, SM),
         scratch_shapes=(
             pltpu.VMEM((ROWS, LANES), F32),
-            pltpu.VMEM((4 * LIST + 16, DEPTH), BF16),
-            pltpu.VMEM((ROWS, LANES), F32),
-            pltpu.VMEM((ROWS, LANES), F32),
+            pltpu.VMEM((2, 4 * LIST + 16, DEPTH), BF16),
+            pltpu.VMEM((2, ROWS, LANES), F32),
+            pltpu.VMEM((2, ROWS, LANES), F32),
             pltpu.VMEM((32, DEPTH), BF16),
             pltpu.VMEM((OWN, LANES), F32),
             *EVAL_SCRATCH,
@@ -670,32 +689,39 @@
     )(*pieces, *prepared)
 
 
-def second_call(pieces, weights, pairs, counts, energy):
+def second_call(pieces, weights, pairs, counts, energy, live):
     return pl.pallas_call(
         second_kernel,
         name="second",
         out_shape=(shape(72, LANES), shape(1, LANES)),
-        in_specs=[VM] * (len(pieces) + len(weights) + 1) + [SM, VM],
+        in_specs=[VM] * (len(pieces) + len(weights) + 1) + [SM, VM, VM],
         out_specs=(VM, VM),
         scratch_shapes=(
-            pltpu.VMEM((ROWS, LANES), F32),
             pltpu.VMEM((32, DEPTH), BF16),
             pltpu.VMEM((OWN, LANES), F32),
             *EVAL_SCRATCH,
         ),
         compiler_params=limit(20),
-    )(*pieces, *weights, pairs, counts, energy)
-
-
-def swap(low_part, high_part, axis):
+    )(*pieces, *weights, pairs, counts, energy, live)
+
+
+def is_even(axis):
+    return lax.axis_index(axis) % 2 == 0
+
+
+def trade(across, within, axis):
     count = lax.axis_size(axis)
-    even = lax.axis_index(axis) % 2 == 0
-    across, within = jnp.where(even, low_part, high_part), jnp.where(even, high_part, low_part)
     inner = [(i, i ^ 1) for i in range(count)]
     outer = [(i, (i - 1) % count if i % 2 == 0 else (i + 1) % count) for i in range(count)]
     across = lax.ppermute(across, axis, outer)
     within = lax.ppermute(within, axis, inner)
+    even = is_even(axis)
     return jnp.where(even, across, within), jnp.where(even, within, across)
+
+
+def swap(low_part, high_part, axis):
+    even = is_even(axis)
+    return trade(jnp.where(even, low_part, high_part), jnp.where(even, high_part, low_part), axis)
 
 
 def everywhere(row, axes):
@@ -705,17 +731,34 @@
     return jnp.sum(rows, axis=0)
 
 
-def spread(rows, beside):
-    rows = rows.reshape(3, 3, 8, LANES)
-    low, high = swap(rows[:, :, 2:4], rows[:, :, 3:5], "gz")
+def spread_rows(rows, across, within, beside):
+    low, high = trade(across, within, "gz")
+    low, high = (v.reshape(3, 3, 2, LANES)[..., 0:HALF] for v in (low, high))
+    rows = rows.reshape(3, 3, 8, LANES)[:, :, 2:5, 0:HALF]
+    rows = jnp.concatenate([low, rows, high, jnp.zeros((3, 3, 1, HALF), F32)], axis=2)
+
+    def joined(one, two):
+        return jnp.concatenate([one, two], axis=-1)
+
+    def parted(both):
+        return jnp.stack([both[..., 0:HALF], both[..., HALF:]])
+
+    low, high = swap(joined(rows[0], rows[1]), joined(rows[1], rows[2]), "gx")
+    rows = jnp.concatenate([parted(low), rows, parted(high)], axis=0)
+    rows, beside = lax.optimization_barrier((rows, beside))
+    low, high = swap(joined(rows[:, 0], rows[:, 1]), joined(rows[:, 1], rows[:, 2]), "gy")
+    return (low, rows, high), beside
+
+
+def spread_moved(rows):
+    low, high = swap(rows[:, 2:4], rows[:, 3:5], "gz")
+    rows = jnp.concatenate([low, rows[:, 2:5], high, jnp.zeros((3, 1, LANES), F32)], axis=1)
+    low, high = trade(rows, rows, "gx")
     rows = jnp.concatenate(
-        [low, rows[:, :, 2:5], high, jnp.zeros((3, 3, 1, LANES), F32)], axis=2
-    )
-    low, high = swap(rows[0:2], rows[1:3], "gx")
-    rows = jnp.concatenate([low, rows, high], axis=0)
-    rows, beside = lax.optimization_barrier((rows, beside))
-    low, high = swap(rows[:, 0:2], rows[:, 1:3], "gy")
-    return (low, rows, high), beside
+        [low[..., 48:80], rows[..., 32:80], high[..., 32:64], jnp.zeros((3, 8, 16), F32)], axis=-1
+    )
+    low, high = swap(rows[0:2], rows[1:3], "gy")
+    return low, rows, high
 
 
 def unpack(force):
@@ -725,14 +768,15 @@
 
 def shards(positions, velocity, species, region_count, neighbours,
            basis_weight, species_embed, weight_map, scalar_map, energy_out, species_energy):
-    rows = pack_call(positions, velocity, species, region_count, neighbours)
+    sent = pack_call(positions, velocity, species, region_count, neighbours)
     prepared = prep_call(
         basis_weight, species_embed, weight_map, scalar_map, energy_out, species_energy
     )
-    pieces, prepared = spread(rows, prepared)
-    force_one, moved, energy_one, pairs, counts = first_call(pieces, prepared)
-    pieces, _ = spread(moved, ())
-    force_two, energies = second_call(pieces, prepared[0:7], pairs, counts, energy_one)
+    pieces, prepared = spread_rows(*sent, prepared)
+    force_one, moved, live, energy_one, pairs, counts = first_call(pieces, prepared)
+    force_two, energies = second_call(
+        spread_moved(moved), prepared[0:7], pairs, counts, energy_one, live
+    )
     totals = everywhere(everywhere(energies, ("gx", "gy")), ("gz",))
     forces = jnp.stack([unpack(force_one), unpack(force_two)])
     return forces, totals[0, 0:2] / totals[0, 2:4]

time: 128 us -> 120 us (0.938)
  waiting for transfers between devices: 32 us -> 26.8 us
  local copies, waits for them, and re-layouts: 6.01 us -> 3.5 us
  starting transfers between devices: 73.6 us -> 72.3 us
    ppermute x12, waiting for transfers between devices: 14.9 us -> 9.66 us  [the longest x6 9.52 us: trade(): within = lax.ppermute(within, axis, inner)]
    unnamed x23 -> x19, local copies, waits for them, and re-layouts: 4.55 us -> 1.73 us
    pallas_call x1, Pallas kernels: 0.5 us -> 1.85 us  [pack_call(): pl.pallas_call(pack_kernel, name='pack', out_shape=(shape(9, 8, LANES), s...]
    all_to_all x2, starting transfers between devices: 17.5 us -> 16.1 us  [everywhere(): rows = lax.all_to_all(rows, axes, 0, 0, tiled=False)]
  transfers between devices with their start and end apart: 14 -> 14, of which waited for: 9 -> 9; matrix products, arithmetic and copies ran while one was open for 1% -> 1% of each run, Pallas kernels for 0% -> 1%
where the time goes in v4:
time: 120 us; the launch traced here: 119 us
  starting transfers between devices  72.3 us (60%)
  waiting for transfers between devices  26.8 us (22%)
  Pallas kernels  14.1 us (12%)
  local copies, waits for them, and re-layouts  3.5 us (3%)
    ppermute x6, starting transfers between devices, trade(): across = lax.ppermute(across, axis, outer)  43 us
    all_to_all x2, waiting for transfers between devices, everywhere(): rows = lax.all_to_all(rows, axes, 0, 0, tiled=False)  17.1 us
    all_to_all x2, starting transfers between devices, everywhere(): rows = lax.all_to_all(rows, axes, 0, 0, tiled=False)  16.1 us
    ppermute x6, starting transfers between devices, trade(): within = lax.ppermute(within, axis, inner)  13.2 us
    ppermute x6, waiting for transfers between devices, trade(): within = lax.ppermute(within, axis, inner)  9.52 us
    pallas_call x1, Pallas kernels, first_call(): pl.pallas_call(first_kernel, name='first', out_shape=(shape(72, LANES), s...  6.59 us
    pallas_call x1, Pallas kernels, second_call(): pl.pallas_call(second_kernel, name='second', out_shape=(shape(72, LANES),...  5.06 us
  transfers between devices with their start and end apart: 14, of which 9 were waited for; matrix products, arithmetic and copies ran while one was open for 1% of the time, Pallas kernels for 1%

profile of v4, /device:TPU:1, one launch (start us, length us, event | category | flops | bytes accessed | tf_op | source)
XLA Modules:
  0.0 118.9 jit_solution(10568422856928618857)
XLA Ops:
  0.6 1.8 %pack.1 = (f32[9,8,128]{2,1,0:T(8,128)}, f32[9,2,128]{2,1,0:T(2,128)}, f32[9,2,128]{2,1,0:T(2,128)}) custom-call(f32[3,3,3,2,3]{4,3,2,1,0:T(2,128)} %bitcast.66, f32[3,3,3,2,3]{4,3,2,1,0:T(2,128)} %bitcast.67, s32[3,3,2,3]{3,2,1,0:T(2,128)} %bitcast.69, s32[3,3,3]{2,1,0:T(4,128)} %count_in.1, s32[3,3,3,2,40]{4,3,2,1,0:T(2,128)} %list_in.1), custom_call_target="tpu_custom_call" | custom-call | tf_op jit(solution)/shard_map/pack/pallas_call | solution.py:603
  2.5 5.9 %collective-permute-start = (f32[9,2,128]{2,1,0:T(2,128)}, f32[9,2,128]{2,1,0:T(2,128)S(1)}, u32[]{:S(2)}, u32[]{:S(2)}) collective-permute-start(f32[9,2,128]{2,1,0:T(2,128)} %get-tuple-element.34), channel_id=1, source_target_pairs={{0,7},{1,2},{2,1},{3,4},{4,3},{5,6},{6,5},{7,0},{8,15},{9,10},{10,... | collective-permute-start | bytes 27656 | tf_op jit(solution)/shard_map/ppermute | solution.py:716
  8.4 1.9 %collective-permute-start.1 = (f32[9,2,128]{2,1,0:T(2,128)}, f32[9,2,128]{2,1,0:T(2,128)S(1)}, u32[]{:S(2)}, u32[]{:S(2)}) collective-permute-start(f32[9,2,128]{2,1,0:T(2,128)} %get-tuple-element.35), channel_id=1, source_target_pairs={{0,1},{1,0},{2,3},{3,2},{4,5},{5,4},{6,7},{7,6},{8,9},{9,8},{10,11... | collective-permute-start | bytes 27656 | tf_op jit(solution)/shard_map/ppermute | solution.py:717
  10.5 2.6 %collective-permute-done.1 = f32[9,2,128]{2,1,0:T(2,128)S(1)} collective-permute-done((f32[9,2,128]{2,1,0:T(2,128)}, f32[9,2,128]{2,1,0:T(2,128)S(1)}, u32[]{:S(2)}, u32[]{:S(2)}) %collective-permute-start.1) | collective-permute-done | bytes 9248 | tf_op jit(solution)/shard_map/ppermute | solution.py:717
  13.2 8.0 %collective-permute-start.2 = (f32[3,8,128]{2,1,0:T(8,128)S(1)}, f32[3,8,128]{2,1,0:T(8,128)S(1)}, u32[]{:S(2)}, u32[]{:S(2)}) collective-permute-start(f32[3,8,128]{2,1,0:T(8,128)S(1)} %get-tuple-element.79), channel_id=1, source_target_pairs={{0,704},{64,128},{128,64},{192,256},{256,192},{320,384},{384,320},... | collective-permute-start | bytes 36872 | tf_op jit(solution)/shard_map/ppermute | solution.py:716
  21.2 1.9 %collective-permute-start.3 = (f32[3,8,128]{2,1,0:T(8,128)S(1)}, f32[3,8,128]{2,1,0:T(8,128)S(1)}, u32[]{:S(2)}, u32[]{:S(2)}) collective-permute-start(f32[3,8,128]{2,1,0:T(8,128)S(1)} %get-tuple-element.78), channel_id=1, source_target_pairs={{0,64},{64,0},{128,192},{192,128},{256,320},{320,256},{384,448},{4... | collective-permute-start | bytes 36872 | tf_op jit(solution)/shard_map/ppermute | solution.py:717
  24.6 1.1 collective-permute-done.3
  25.9 12.2 %collective-permute-start.4 = (f32[7,8,128]{2,1,0:T(8,128)S(1)}, f32[7,8,128]{2,1,0:T(8,128)S(1)}, u32[]{:S(2)}, u32[]{:S(2)}) collective-permute-start(f32[7,8,128]{2,1,0:T(8,128)S(1)} %get-tuple-element.73), channel_id=1, source_target_pairs={{0,56},{8,16},{16,8},{24,32},{32,24},{40,48},{48,40},{56,0},{1,57}... | collective-permute-start | bytes 86024 | tf_op jit(solution)/shard_map/ppermute | solution.py:716
  38.2 2.5 %collective-permute-start.5 = (f32[7,8,128]{2,1,0:T(8,128)S(1)}, f32[7,8,128]{2,1,0:T(8,128)S(1)}, u32[]{:S(2)}, u32[]{:S(2)}) collective-permute-start(f32[7,8,128]{2,1,0:T(8,128)S(1)} %get-tuple-element.72), channel_id=1, source_target_pairs={{0,8},{8,0},{16,24},{24,16},{32,40},{40,32},{48,56},{56,48},{1,9},... | collective-permute-start | bytes 86024 | tf_op jit(solution)/shard_map/ppermute | solution.py:717
  41.6 6.6 %first.1 = (f32[72,128]{1,0:T(8,128)S(1)}, f32[3,8,128]{2,1,0:T(8,128)S(1)}, f32[72,128]{1,0:T(8,128)S(1)}, f32[1,128]{1,0:T(1,128)S(1)}, f32[26,24,256]{2,1,0:T(8,128)S(1)}, /*index=5*/s32[2]{0:T(128)S(1)}) custom-call(f32[7,8,128]{2,1,0:T(8,128)S(1)} %get-tuple-element.77.low, f32[7,3,8,64]{3,2,1,0:T(8,128)S(1)} %fusion.own, ...), custom_call_target="tpu_custom_call" | custom-call | tf_op jit(solution)/shard_map/first/pallas_call | solution.py:666
  48.2 2.6 %collective-permute-start.6 = (f32[3,2,128]{2,1,0:T(2,128)S(1)}, f32[3,2,128]{2,1,0:T(2,128)S(1)}, u32[]{:S(2)}, u32[]{:S(2)}) collective-permute-start(f32[3,2,128]{2,1,0:T(2,128)S(1)} %get-tuple-element.93), channel_id=1, source_target_pairs={{0,7},{1,2},{2,1},{3,4},{4,3},{5,6},{6,5},{7,0},{8,15},{9,10},{10,... | collective-permute-start | bytes 9224 | tf_op jit(solution)/shard_map/ppermute | solution.py:716
  50.8 2.9 %collective-permute-start.7 = (f32[3,2,128]{2,1,0:T(2,128)S(1)}, f32[3,2,128]{2,1,0:T(2,128)S(1)}, u32[]{:S(2)}, u32[]{:S(2)}) collective-permute-start(f32[3,2,128]{2,1,0:T(2,128)S(1)} %get-tuple-element.94), channel_id=1, source_target_pairs={{0,1},{1,0},{2,3},{3,2},{4,5},{5,4},{6,7},{7,6},{8,9},{9,8},{10,11... | collective-permute-start | bytes 9224 | tf_op jit(solution)/shard_map/ppermute | solution.py:717
  53.8 1.4 %collective-permute-done.7 = f32[3,2,128]{2,1,0:T(2,128)S(1)} collective-permute-done((f32[3,2,128]{2,1,0:T(2,128)S(1)}, f32[3,2,128]{2,1,0:T(2,128)S(1)}, u32[]{:S(2)}, u32[]{:S(2)}) %collective-permute-start.7) | collective-permute-done | bytes 3104 | tf_op jit(solution)/shard_map/ppermute | solution.py:717
  55.3 5.2 %collective-permute-start.8 = (f32[3,8,128]{2,1,0:T(8,128)S(1)}, f32[3,8,128]{2,1,0:T(8,128)S(1)}, u32[]{:S(2)}, u32[]{:S(2)}) collective-permute-start(f32[3,8,128]{2,1,0:T(8,128)S(1)} %maximum_maximum_fusion.1), channel_id=1, source_target_pairs={{0,704},{64,128},{128,64},{192,256},{256,192},{320,384},{384,320},... | collective-permute-start | bytes 36872 | tf_op jit(solution)/shard_map/ppermute | solution.py:716
  60.5 1.9 %collective-permute-start.9 = (f32[3,8,128]{2,1,0:T(8,128)S(1)}, f32[3,8,128]{2,1,0:T(8,128)S(1)}, u32[]{:S(2)}, u32[]{:S(2)}) collective-permute-start(f32[3,8,128]{2,1,0:T(8,128)S(1)} %maximum_maximum_fusion.1), channel_id=1, source_target_pairs={{0,64},{64,0},{128,192},{192,128},{256,320},{320,256},{384,448},{4... | collective-permute-start | bytes 36872 | tf_op jit(solution)/shard_map/ppermute | solution.py:717
  62.7 2.5 %collective-permute-done.9 = f32[3,8,128]{2,1,0:T(8,128)S(1)} collective-permute-done((f32[3,8,128]{2,1,0:T(8,128)S(1)}, f32[3,8,128]{2,1,0:T(8,128)S(1)}, u32[]{:S(2)}, u32[]{:S(2)}) %collective-permute-start.9) | collective-permute-done | bytes 12320 | tf_op jit(solution)/shard_map/ppermute | solution.py:717
  65.4 9.0 %collective-permute-start.10 = (f32[2,8,128]{2,1,0:T(8,128)S(1)}, f32[2,8,128]{2,1,0:T(8,128)S(1)}, u32[]{:S(2)}, u32[]{:S(2)}) collective-permute-start(f32[2,8,128]{2,1,0:T(8,128)S(1)} %get-tuple-element.92), channel_id=1, source_target_pairs={{0,56},{8,16},{16,8},{24,32},{32,24},{40,48},{48,40},{56,0},{1,57}... | collective-permute-start | bytes 24584 | tf_op jit(solution)/shard_map/ppermute | solution.py:716
  74.4 1.9 %collective-permute-start.11 = (f32[2,8,128]{2,1,0:T(8,128)S(1)}, f32[2,8,128]{2,1,0:T(8,128)S(1)}, u32[]{:S(2)}, u32[]{:S(2)}) collective-permute-start(f32[2,8,128]{2,1,0:T(8,128)S(1)} %get-tuple-element.91), channel_id=1, source_target_pairs={{0,8},{8,0},{16,24},{24,16},{32,40},{40,32},{48,56},{56,48},{1,9},... | collective-permute-start | bytes 24584 | tf_op jit(solution)/shard_map/ppermute | solution.py:717
  76.4 1.1 collective-permute-done.11
  77.5 5.1 %second.1 = (f32[72,128]{1,0:T(8,128)S(1)}, f32[1,128]{1,0:T(1,128)S(1)}) custom-call(f32[2,8,128]{2,1,0:T(8,128)S(1)} %get-tuple-element.90.low, f32[3,8,128]{2,1,0:T(8,128)S(1)} %maximum_maximum_fusion.2.own, f32[2,8,128]{2,1,0:T(8,128)S(1)} %get-tuple-element.89.high, bf16[128,16]{1,0:T(8,128)(2,1)S(1)} %get-tuple-element.48.w1t, ...), custom_call_target="tpu_custom_call" | custom-call | tf_op jit(solution)/shard_map/second/pallas_call | solution.py:693
  83.2 10.2 %all-to-all-start = ((f32[96,1,128]{2,1,0:T(1,128)}), f32[96,1,128]{2,1,0:T(1,128)S(1)}, u32[]{:S(2)}, u32[]{:S(2)}) async-start(f32[96,1,128]{2,1,0:T(1,128)} %broadcast_in_dim.35), calls=%async_computation | async-start | bytes 98304 | tf_op jit(solution)/shard_map/all_to_all | solution.py:730
  93.7 11.5 %all-to-all-done = f32[96,1,128]{2,1,0:T(1,128)S(1)} async-done(((f32[96,1,128]{2,1,0:T(1,128)}), f32[96,1,128]{2,1,0:T(1,128)S(1)}, u32[]{:S(2)}, u32[]{:S(2)}) %all-to-all-start) | async-done | bytes 49184 | tf_op jit(solution)/shard_map/all_to_all | solution.py:730
  105.8 5.9 %all-to-all-start.1 = ((f32[8,1,128]{2,1,0:T(1,128)}), f32[8,1,128]{2,1,0:T(1,128)S(1)}, u32[]{:S(2)}, u32[]{:S(2)}) async-start(f32[8,1,128]{2,1,0:T(1,128)} %broadcast_in_dim.36), calls=%async_computation.1 | async-start | bytes 8192 | tf_op jit(solution)/shard_map/all_to_all | solution.py:730
  112.7 5.6 %all-to-all-done.1 = f32[8,1,128]{2,1,0:T(1,128)S(1)} async-done(((f32[8,1,128]{2,1,0:T(1,128)}), f32[8,1,128]{2,1,0:T(1,128)S(1)}, u32[]{:S(2)}, u32[]{:S(2)}) %all-to-all-start.1) | async-done | bytes 4128 | tf_op jit(solution)/shard_map/all_to_all | solution.py:730
  (60 shorter events, 6.3 us)
Async XLA Ops:
  2.5 7.9 %copy-start.6 = (f32[9,8,128]{2,1,0:T(8,128)S(1)}, f32[9,8,128]{2,1,0:T(8,128)}, u32[]{:S(2)}) copy-start(f32[9,8,128]{2,1,0:T(8,128)} %get-tuple-element.36) | copy-start | bytes 110596
  2.5 8.0 %collective-permute-start = (f32[9,2,128]{2,1,0:T(2,128)}, f32[9,2,128]{2,1,0:T(2,128)S(1)}, u32[]{:S(2)}, u32[]{:S(2)}) collective-permute-start(f32[9,2,128]{2,1,0:T(2,128)} %get-tuple-element.34), channel_id=1, source_target_pairs={{0,7},{1,2},{2,1},{3,4},{4,3},{5,6},{6,5},{7,0},{8,15},{9,10},{10,... | collective-permute-start | bytes 27656 | tf_op jit(solution)/shard_map/ppermute | solution.py:716
  8.4 4.6 %collective-permute-start.1 = (f32[9,2,128]{2,1,0:T(2,128)}, f32[9,2,128]{2,1,0:T(2,128)S(1)}, u32[]{:S(2)}, u32[]{:S(2)}) collective-permute-start(f32[9,2,128]{2,1,0:T(2,128)} %get-tuple-element.35), channel_id=1, source_target_pairs={{0,1},{1,0},{2,3},{3,2},{4,5},{5,4},{6,7},{7,6},{8,9},{9,8},{10,11... | collective-permute-start | bytes 27656 | tf_op jit(solution)/shard_map/ppermute | solution.py:717
  13.1 10.1 %copy-start.3 = (bf16[5,128]{1,0:T(8,128)(2,1)S(1)}, bf16[5,128]{1,0:T(8,128)(2,1)}, u32[]{:S(2)}) copy-start(bf16[5,128]{1,0:T(8,128)(2,1)} %se_in.1) | copy-start | bytes 3844
  13.2 11.3 %collective-permute-start.2 = (f32[3,8,128]{2,1,0:T(8,128)S(1)}, f32[3,8,128]{2,1,0:T(8,128)S(1)}, u32[]{:S(2)}, u32[]{:S(2)}) collective-permute-start(f32[3,8,128]{2,1,0:T(8,128)S(1)} %get-tuple-element.79), channel_id=1, source_target_pairs={{0,704},{64,128},{128,64},{192,256},{256,192},{320,384},{384,320},... | collective-permute-start | bytes 36872 | tf_op jit(solution)/shard_map/ppermute | solution.py:716
  21.2 2.0 %copy-start.4 = (f32[128]{0:T(128)S(1)}, f32[128]{0:T(128)}, u32[]{:S(2)}) copy-start(f32[128]{0:T(128)} %param.20) | copy-start | bytes 1540
  21.2 2.0 %copy-start.5 = (f32[5]{0:T(128)S(1)}, f32[5]{0:T(128)}, u32[]{:S(2)}) copy-start(f32[5]{0:T(128)} %param.21) | copy-start | bytes 64
  21.2 4.4 %collective-permute-start.3 = (f32[3,8,128]{2,1,0:T(8,128)S(1)}, f32[3,8,128]{2,1,0:T(8,128)S(1)}, u32[]{:S(2)}, u32[]{:S(2)}) collective-permute-start(f32[3,8,128]{2,1,0:T(8,128)S(1)} %get-tuple-element.78), channel_id=1, source_target_pairs={{0,64},{64,0},{128,192},{192,128},{256,320},{320,256},{384,448},{4... | collective-permute-start | bytes 36872 | tf_op jit(solution)/shard_map/ppermute | solution.py:717
  23.2 0.7 copy-start.2
  23.2 0.7 copy-start
  23.2 0.7 copy-start.1
  25.9 14.8 %collective-permute-start.4 = (f32[7,8,128]{2,1,0:T(8,128)S(1)}, f32[7,8,128]{2,1,0:T(8,128)S(1)}, u32[]{:S(2)}, u32[]{:S(2)}) collective-permute-start(f32[7,8,128]{2,1,0:T(8,128)S(1)} %get-tuple-element.73), channel_id=1, source_target_pairs={{0,56},{8,16},{16,8},{24,32},{32,24},{40,48},{48,40},{56,0},{1,57}... | collective-permute-start | bytes 86024 | tf_op jit(solution)/shard_map/ppermute | solution.py:716
  38.2 3.4 %collective-permute-start.5 = (f32[7,8,128]{2,1,0:T(8,128)S(1)}, f32[7,8,128]{2,1,0:T(8,128)S(1)}, u32[]{:S(2)}, u32[]{:S(2)}) collective-permute-start(f32[7,8,128]{2,1,0:T(8,128)S(1)} %get-tuple-element.72), channel_id=1, source_target_pairs={{0,8},{8,0},{16,24},{24,16},{32,40},{40,32},{48,56},{56,48},{1,9},... | collective-permute-start | bytes 86024 | tf_op jit(solution)/shard_map/ppermute | solution.py:717
  48.2 5.6 %collective-permute-start.6 = (f32[3,2,128]{2,1,0:T(2,128)S(1)}, f32[3,2,128]{2,1,0:T(2,128)S(1)}, u32[]{:S(2)}, u32[]{:S(2)}) collective-permute-start(f32[3,2,128]{2,1,0:T(2,128)S(1)} %get-tuple-element.93), channel_id=1, source_target_pairs={{0,7},{1,2},{2,1},{3,4},{4,3},{5,6},{6,5},{7,0},{8,15},{9,10},{10,... | collective-permute-start | bytes 9224 | tf_op jit(solution)/shard_map/ppermute | solution.py:716
  50.8 4.3 %collective-permute-start.7 = (f32[3,2,128]{2,1,0:T(2,128)S(1)}, f32[3,2,128]{2,1,0:T(2,128)S(1)}, u32[]{:S(2)}, u32[]{:S(2)}) collective-permute-start(f32[3,2,128]{2,1,0:T(2,128)S(1)} %get-tuple-element.94), channel_id=1, source_target_pairs={{0,1},{1,0},{2,3},{3,2},{4,5},{5,4},{6,7},{7,6},{8,9},{9,8},{10,11... | collective-permute-start | bytes 9224 | tf_op jit(solution)/shard_map/ppermute | solution.py:717
  55.3 7.4 %collective-permute-start.8 = (f32[3,8,128]{2,1,0:T(8,128)S(1)}, f32[3,8,128]{2,1,0:T(8,128)S(1)}, u32[]{:S(2)}, u32[]{:S(2)}) collective-permute-start(f32[3,8,128]{2,1,0:T(8,128)S(1)} %maximum_maximum_fusion.1), channel_id=1, source_target_pairs={{0,704},{64,128},{128,64},{192,256},{256,192},{320,384},{384,320},... | collective-permute-start | bytes 36872 | tf_op jit(solution)/shard_map/ppermute | solution.py:716
  60.5 4.7 %collective-permute-start.9 = (f32[3,8,128]{2,1,0:T(8,128)S(1)}, f32[3,8,128]{2,1,0:T(8,128)S(1)}, u32[]{:S(2)}, u32[]{:S(2)}) collective-permute-start(f32[3,8,128]{2,1,0:T(8,128)S(1)} %maximum_maximum_fusion.1), channel_id=1, source_target_pairs={{0,64},{64,0},{128,192},{192,128},{256,320},{320,256},{384,448},{4... | collective-permute-start | bytes 36872 | tf_op jit(solution)/shard_map/ppermute | solution.py:717
  65.4 11.0 %collective-permute-start.10 = (f32[2,8,128]{2,1,0:T(8,128)S(1)}, f32[2,8,128]{2,1,0:T(8,128)S(1)}, u32[]{:S(2)}, u32[]{:S(2)}) collective-permute-start(f32[2,8,128]{2,1,0:T(8,128)S(1)} %get-tuple-element.92), channel_id=1, source_target_pairs={{0,56},{8,16},{16,8},{24,32},{32,24},{40,48},{48,40},{56,0},{1,57}... | collective-permute-start | bytes 24584 | tf_op jit(solution)/shard_map/ppermute | solution.py:716
  74.4 3.1 %collective-permute-start.11 = (f32[2,8,128]{2,1,0:T(8,128)S(1)}, f32[2,8,128]{2,1,0:T(8,128)S(1)}, u32[]{:S(2)}, u32[]{:S(2)}) collective-permute-start(f32[2,8,128]{2,1,0:T(8,128)S(1)} %get-tuple-element.91), channel_id=1, source_target_pairs={{0,8},{8,0},{16,24},{24,16},{32,40},{40,32},{48,56},{56,48},{1,9},... | collective-permute-start | bytes 24584 | tf_op jit(solution)/shard_map/ppermute | solution.py:717
  83.2 22.0 %all-to-all-start = ((f32[96,1,128]{2,1,0:T(1,128)}), f32[96,1,128]{2,1,0:T(1,128)S(1)}, u32[]{:S(2)}, u32[]{:S(2)}) async-start(f32[96,1,128]{2,1,0:T(1,128)} %broadcast_in_dim.35), calls=%async_computation | async-start | bytes 98304 | tf_op jit(solution)/shard_map/all_to_all | solution.py:730
  105.8 12.5 %all-to-all-start.1 = ((f32[8,1,128]{2,1,0:T(1,128)}), f32[8,1,128]{2,1,0:T(1,128)S(1)}, u32[]{:S(2)}, u32[]{:S(2)}) async-start(f32[8,1,128]{2,1,0:T(1,128)} %broadcast_in_dim.36), calls=%async_computation.1 | async-start | bytes 8192 | tf_op jit(solution)/shard_map/all_to_all | solution.py:730

commit v5 on v4

--- a/solution.py
+++ b/solution.py
@@ -22,7 +22,7 @@
 LISTED = 40
 USED = 392
 ROWS = 400
-SPARSE = 448
+LAYER = 64
 DEPTH = 512
 INNER = 256
 OWN = 80
@@ -160,8 +160,8 @@
             def where(flag, value):
                 return jnp.where(flag, value, -1.0)
 
-            def region(c, layers):
-                return (c[0] * layers + c[1]) * 8.0 + c[2]
+            def region(c):
+                return c[1] * 8.0 + c[2]
 
             def inner(c, s):
                 return (((c[0] - 1.0) * 5.0 + (c[1] - 1.0)) * 5.0 + (c[2] - 1.0)) * 2.0 + s
@@ -171,9 +171,9 @@
 
             near = (x, y, z)
             lines = [
-                where(valid, region(near, 7.0)),
+                where(valid, region(near)),
                 slot,
-                where(valid, region(far, 7.0)),
+                where(valid, region(far)),
                 far_slot,
                 where(valid & (away_i < 2.5), inner(near, slot)),
                 where(valid & (away_j < 2.5), inner(far, far_slot)),
@@ -182,8 +182,8 @@
                 valid.astype(F32),
                 *shift,
                 (valid & (away_i < 1.5)).astype(F32),
-                where(valid, region(near, 8.0)),
-                where(valid, region(far, 8.0)),
+                near[0],
+                far[0],
                 jnp.zeros((9, WIDE), F32),
             ]
             pairs_ref[k] = jnp.where(place < first, pairs_ref[k], jnp.concatenate(lines, axis=0))
@@ -215,9 +215,10 @@
 
 def evaluate(refs, scratch, counts, own_out, moved):
     pos_t, pairs_ref, w1t, w1, wmt, wm, smt, sm, eo_ref = refs
-    env_ref, envs_ref, grad_ref, geo_ref, lat_ref, slope_ref, h_ref, wb_ref, hp_ref, en_ref = (
-        scratch
-    )
+    env_ref, envs_ref, grad_ref, geo_ref, feat_ref, lat_ref, slope_ref, h_ref, wb_ref, hp_ref = (
+        scratch[:-1]
+    )
+    en_ref = scratch[-1]
     front, every = counts
     norm = math.sqrt(2.0 / cutoff)
 
@@ -229,23 +230,26 @@
     en_ref[...] = jnp.zeros(en_ref.shape, F32)
     own_out[...] = jnp.zeros(own_out.shape, F32)
 
-    def gathered(index, slot):
-        got = mm(pos_t[...], one_hot(index, SPARSE if moved else ROWS, DEPTH))
-        full = got[0:8] + got[8:16] + got[16:24]
+    def gathered(place, layer, slot):
+        got = mm(pos_t[...], one_hot(place, LAYER, LAYER))
+        full = jnp.zeros((8, WIDE), F32)
+        for x in range(7):
+            at = 8 * x
+            part = got[at : at + 8] + got[LAYER + at : LAYER + at + 8]
+            part = part + got[2 * LAYER + at : 2 * LAYER + at + 8]
+            full = full + jnp.where(layer == float(x), part, 0.0)
         second = slot > 0.5
         point = jnp.where(second, full[3:6], full[0:3])
         return point, jnp.where(second, full[7:8], full[6:7])
 
-    def stage_one(t, carry):
+    def shape_pairs(t):
         pair = pairs_ref[t]
         valid = pair[8:9]
+        near, near_kind = gathered(pair[0:1], pair[13:14], pair[1:2])
+        far, far_kind = gathered(pair[2:3], pair[14:15], pair[3:4])
         if moved:
-            near, _ = gathered(pair[13:14], pair[1:2])
-            far, _ = gathered(pair[14:15], pair[3:4])
             near_kind, far_kind = pair[15:16], pair[16:17]
         else:
-            near, near_kind = gathered(pair[0:1], pair[1:2])
-            far, far_kind = gathered(pair[2:3], pair[3:4])
             pairs_ref[t, 15:17] = jnp.concatenate([near_kind, far_kind], axis=0)
         d = far - near + pair[9:12]
         square = jnp.sum(d * d, axis=0, keepdims=True)
@@ -276,7 +280,14 @@
         geo_ref[t, 0:16] = jnp.concatenate(
             [u, inverse, f, fd, jnp.zeros((2, WIDE), F32)] + slope, axis=0
         )
-        pre = mm(w1t[...], feats.astype(BF16))
+        feat_ref[t] = feats.astype(BF16)
+
+    def stage_one(t, carry):
+        shape_pairs(t)
+        pair = pairs_ref[t]
+        geo = geo_ref[t]
+        valid, u, f = pair[8:9], geo[0:3], geo[4:5]
+        pre = mm(w1t[...], feat_ref[t])
         gate = sigmoid(pre)
         lat = (pre * gate).astype(BF16)
         lat_ref[t] = lat
@@ -286,18 +297,13 @@
         w = h * (f * valid)
         hit_i = one_hot(pair[4:5], INNER, INNER)
         hit_j = one_hot(pair[5:6], INNER, INNER)
-        high, low = split2(
-            jnp.concatenate([w, w * u[0:1], w * u[1:2], w * u[2:3]], axis=0)
-        )
-        moments = jnp.concatenate([high, low], axis=1)
-        plus, minus = hit_i + hit_j, hit_i - hit_j
-        env_ref[0:CH] += mm_nt(moments[0:CH], jnp.concatenate([plus, plus], axis=1))
-        env_ref[CH:] += mm_nt(moments[CH:], jnp.concatenate([minus, minus], axis=1))
+        moments = jnp.concatenate([w, w * u[0:1], w * u[1:2], w * u[2:3]], axis=0).astype(BF16)
+        env_ref[0:CH] += mm_nt(moments[0:CH], hit_i + hit_j)
+        env_ref[CH:] += mm_nt(moments[CH:], hit_i - hit_j)
         return carry
 
     lax.fori_loop(0, every, stage_one, jnp.int32(0))
-    high, low = split2(env_ref[...])
-    envs_ref[...] = jnp.concatenate([high, low], axis=1)
+    envs_ref[...] = env_ref[...].astype(BF16)
 
     def stage_two(t, carry):
         pair = pairs_ref[t]
@@ -306,7 +312,7 @@
         u = geo[0:3]
         f = geo[4:5]
         hit = one_hot(pair[4:5], INNER, INNER)
-        env = mm(envs_ref[...], jnp.concatenate([hit, hit], axis=0))
+        env = mm(envs_ref[...], hit)
         aligned = (
             env[0:CH]
             + u[0:1] * env[CH : 2 * CH]
@@ -332,17 +338,14 @@
             for k in range(3)
         ]
         geo_ref[t, 16:19] = jnp.concatenate(u_bar, axis=0)
-        high, low = split2(
-            jnp.concatenate([al_bar, al_bar * u[0:1], al_bar * u[1:2], al_bar * u[2:3]], axis=0)
+        pulls = jnp.concatenate(
+            [al_bar, al_bar * u[0:1], al_bar * u[1:2], al_bar * u[2:3]], axis=0
         )
-        grad_ref[...] += mm_nt(
-            jnp.concatenate([high, low], axis=1), jnp.concatenate([hit, hit], axis=1)
-        )
+        grad_ref[...] += mm_nt(pulls.astype(BF16), hit)
         return carry
 
     lax.fori_loop(0, every, stage_two, jnp.int32(0))
-    high, low = split2(grad_ref[...])
-    envs_ref[...] = jnp.concatenate([high, low], axis=1)
+    envs_ref[...] = grad_ref[...].astype(BF16)
 
     def stage_three(t, carry):
         pair = pairs_ref[t]
@@ -351,10 +354,9 @@
         u, inverse, f, fd = geo[0:3], geo[3:4], geo[4:5], geo[5:6]
         hit_i = one_hot(pair[4:5], INNER, INNER)
         hit_j = one_hot(pair[5:6], INNER, INNER)
-        plus, minus = hit_i + hit_j, hit_i - hit_j
         grad = envs_ref[...]
-        g0 = mm(grad[0:CH], jnp.concatenate([plus, plus], axis=0))
-        gv = mm(grad[CH:], jnp.concatenate([minus, minus], axis=0))
+        g0 = mm(grad[0:CH], hit_i + hit_j)
+        gv = mm(grad[CH:], hit_i - hit_j)
         parts = [gv[k * CH : (k + 1) * CH] for k in range(3)]
         h = h_ref[t]
         w = h * (f * valid)
@@ -407,14 +409,13 @@
     )
 
 
-def put_positions(top, pos_t):
-    one = top.astype(BF16)
-    rest = top - one.astype(F32)
+def put_positions(turned, pos_t):
+    one = turned.astype(BF16)
+    rest = turned - one.astype(F32)
     two = rest.astype(BF16)
     three = (rest - two.astype(F32)).astype(BF16)
-    pos_t[...] = jnp.concatenate(
-        [one.astype(F32), two.astype(F32), three.astype(F32), jnp.zeros((8, DEPTH), F32)], axis=0
-    ).astype(BF16)
+    for i, part in enumerate((one, two, three)):
+        pos_t[i * LAYER : (i + 1) * LAYER] = part[:, 0:LAYER]
 
 
 def fetch(copies, sems):
@@ -516,7 +517,12 @@
                  rows_ref, table, off_ref, end_ref, pos_t, own_ref, *scratch):
     load_rows(rows_ref, low, own, high)
     turned = jnp.transpose(deepen(rows_ref[0:ROWS], DEPTH))
-    put_positions(turned[0:8], pos_t)
+    lane = iota((56, LANES), 1)
+    layers = sum(
+        pltpu.roll(jnp.where(lane < 8.0, rows_ref[x * 56 : x * 56 + 56], 0.0), 8 * x, 1)
+        for x in range(7)
+    )
+    put_positions(jnp.transpose(deepen(layers, LANES))[0:LAYER], pos_t)
     front, every = build_pairs(
         rows_ref, base, below, table, off_ref, end_ref, pairs_ref, turned[NEIGH:MISC].astype(BF16)
     )
@@ -556,8 +562,7 @@
     layers = [piece[i] for piece, width in ((low, 2), (own, 3), (high, 2)) for i in range(width)]
     turned = jnp.transpose(deepen(jnp.concatenate(layers, axis=0), LANES))
     blocks = [turned[x * 16 : x * 16 + 8] for x in range(7)] + [jnp.zeros((8, LANES), F32)]
-    top = [blocks[x] + pltpu.roll(blocks[x + 1], HALF, 1) for x in range(0, 8, 2)]
-    put_positions(jnp.concatenate(top, axis=1), pos_t)
+    put_positions(jnp.concatenate(blocks, axis=0), pos_t)
     refs = (pos_t, pairs_ref, w1t, w1, wmt, wm, smt, sm, eo)
     evaluate(refs, scratch, (counts_ref[0], counts_ref[1]), own_ref, True)
     lane, inside = own_lane_row()
@@ -576,9 +581,10 @@
 
 EVAL_SCRATCH = (
     pltpu.VMEM((4 * CH, INNER), F32),
-    pltpu.VMEM((4 * CH, 2 * INNER), BF16),
+    pltpu.VMEM((4 * CH, INNER), BF16),
     pltpu.VMEM((4 * CH, INNER), F32),
     pltpu.VMEM((TILES, 24, WIDE), F32),
+    pltpu.VMEM((TILES, 16, WIDE), BF16),
     pltpu.VMEM((TILES, LAT, WIDE), BF16),
     pltpu.VMEM((TILES, LAT, WIDE), F32),
     pltpu.VMEM((TILES, CH, WIDE), F32),
@@ -681,7 +687,7 @@
             pltpu.VMEM((2, 4 * LIST + 16, DEPTH), BF16),
             pltpu.VMEM((2, ROWS, LANES), F32),
             pltpu.VMEM((2, ROWS, LANES), F32),
-            pltpu.VMEM((32, DEPTH), BF16),
+            pltpu.VMEM((3 * LAYER, LAYER), BF16),
             pltpu.VMEM((OWN, LANES), F32),
             *EVAL_SCRATCH,
         ),
@@ -697,7 +703,7 @@
         in_specs=[VM] * (len(pieces) + len(weights) + 1) + [SM, VM, VM],
         out_specs=(VM, VM),
         scratch_shapes=(
-            pltpu.VMEM((32, DEPTH), BF16),
+            pltpu.VMEM((3 * LAYER, LAYER), BF16),
             pltpu.VMEM((OWN, LANES), F32),
             *EVAL_SCRATCH,
         ),
@@ -724,11 +730,20 @@
     return trade(jnp.where(even, low_part, high_part), jnp.where(even, high_part, low_part), axis)
 
 
-def everywhere(row, axes):
-    count = math.prod(lax.axis_size(axis) for axis in axes)
-    rows = jnp.broadcast_to(row[None], (count, 1, LANES))
-    rows = lax.all_to_all(rows, axes, 0, 0, tiled=False)
+def everywhere(row, axes, groups):
+    rows = jnp.broadcast_to(row[None], (len(groups[0]), 1, LANES))
+    rows = lax.all_to_all(rows, axes, 0, 0, axis_index_groups=groups, tiled=False)
     return jnp.sum(rows, axis=0)
+
+
+def everyone(row):
+    nx, ny, nz = (lax.axis_size(axis) for axis in ("gx", "gy", "gz"))
+    part = nx // 3
+    columns = [
+        [(k * part + i) * ny + j for k in range(3) for j in range(ny)] for i in range(part)
+    ]
+    planes = [[(k * part + i) * nz + j for i in range(part) for j in range(nz)] for k in range(3)]
+    return everywhere(everywhere(row, ("gx", "gy"), columns), ("gx", "gz"), planes)
 
 
 def spread_rows(rows, across, within, beside):
@@ -777,7 +792,7 @@
     force_two, energies = second_call(
         spread_moved(moved), prepared[0:7], pairs, counts, energy_one, live
     )
-    totals = everywhere(everywhere(energies, ("gx", "gy")), ("gz",))
+    totals = everyone(energies)
     forces = jnp.stack([unpack(force_one), unpack(force_two)])
     return forces, totals[0, 0:2] / totals[0, 2:4]
 

time: 120 us -> 117 us (0.975)
  no operation moved by 1% of the time
where the time goes in v5:
time: 117 us
  starting transfers between devices  71.4 us (61%)
  waiting for transfers between devices  26.4 us (23%)
  Pallas kernels  13 us (11%)
  local copies, waits for them, and re-layouts  3.48 us (3%)
  other arithmetic  1.17 us (1%)
    ppermute x6, starting transfers between devices, trade(): across = lax.ppermute(across, axis, outer)  42.8 us
    all_to_all x2, waiting for transfers between devices, everywhere(): lax.all_to_all(rows, axes, 0, 0, axis_index_groups=groups, tiled=False)  16.8 us
    all_to_all x2, starting transfers between devices, everywhere(): lax.all_to_all(rows, axes, 0, 0, axis_index_groups=groups, tiled=False)  15.4 us
    ppermute x6, starting transfers between devices, trade(): within = lax.ppermute(within, axis, inner)  13.2 us
    ppermute x6, waiting for transfers between devices, trade(): within = lax.ppermute(within, axis, inner)  9.31 us
    pallas_call x1, Pallas kernels, first_call(): pl.pallas_call(first_kernel, name='first', out_shape=(shape(72, LANES), s...  6.11 us
    pallas_call x1, Pallas kernels, second_call(): pl.pallas_call(second_kernel, name='second', out_shape=(shape(72, LANES),...  4.45 us
  transfers between devices with their start and end apart: 14, of which 9 were waited for; matrix products, arithmetic and copies ran while one was open for 1% of the time, Pallas kernels for 1%

profile of v5, /device:TPU:1, one launch (start us, length us, event | category | flops | bytes accessed | tf_op | source)
XLA Modules:
  0.0 116.6 jit_solution(6325744077643002056)
XLA Ops:
  0.6 1.8 %pack.1 = (f32[9,8,128]{2,1,0:T(8,128)}, f32[9,2,128]{2,1,0:T(2,128)}, f32[9,2,128]{2,1,0:T(2,128)}) custom-call(f32[3,3,3,2,3]{4,3,2,1,0:T(2,128)} %bitcast.67, f32[3,3,3,2,3]{4,3,2,1,0:T(2,128)} %bitcast.68, s32[3,3,2,3]{3,2,1,0:T(2,128)} %bitcast.69, s32[3,3,3]{2,1,0:T(4,128)} %count_in.1, s32[3,3,3,2,40]{4,3,2,1,0:T(2,128)} %list_in.1), custom_call_target="tpu_custom_call" | custom-call | tf_op jit(solution)/shard_map/pack/pallas_call | solution.py:609
  2.5 5.9 %collective-permute-start = (f32[9,2,128]{2,1,0:T(2,128)}, f32[9,2,128]{2,1,0:T(2,128)S(1)}, u32[]{:S(2)}, u32[]{:S(2)}) collective-permute-start(f32[9,2,128]{2,1,0:T(2,128)} %get-tuple-element.34), channel_id=1, source_target_pairs={{0,7},{1,2},{2,1},{3,4},{4,3},{5,6},{6,5},{7,0},{8,15},{9,10},{10,... | collective-permute-start | bytes 27656 | tf_op jit(solution)/shard_map/ppermute | solution.py:722
  8.4 1.9 %collective-permute-start.1 = (f32[9,2,128]{2,1,0:T(2,128)}, f32[9,2,128]{2,1,0:T(2,128)S(1)}, u32[]{:S(2)}, u32[]{:S(2)}) collective-permute-start(f32[9,2,128]{2,1,0:T(2,128)} %get-tuple-element.35), channel_id=1, source_target_pairs={{0,1},{1,0},{2,3},{3,2},{4,5},{5,4},{6,7},{7,6},{8,9},{9,8},{10,11... | collective-permute-start | bytes 27656 | tf_op jit(solution)/shard_map/ppermute | solution.py:723
  10.5 2.6 %collective-permute-done.1 = f32[9,2,128]{2,1,0:T(2,128)S(1)} collective-permute-done((f32[9,2,128]{2,1,0:T(2,128)}, f32[9,2,128]{2,1,0:T(2,128)S(1)}, u32[]{:S(2)}, u32[]{:S(2)}) %collective-permute-start.1) | collective-permute-done | bytes 9248 | tf_op jit(solution)/shard_map/ppermute | solution.py:723
  13.2 8.0 %collective-permute-start.2 = (f32[3,8,128]{2,1,0:T(8,128)S(1)}, f32[3,8,128]{2,1,0:T(8,128)S(1)}, u32[]{:S(2)}, u32[]{:S(2)}) collective-permute-start(f32[3,8,128]{2,1,0:T(8,128)S(1)} %get-tuple-element.79), channel_id=1, source_target_pairs={{0,704},{64,128},{128,64},{192,256},{256,192},{320,384},{384,320},... | collective-permute-start | bytes 36872 | tf_op jit(solution)/shard_map/ppermute | solution.py:722
  21.2 1.9 %collective-permute-start.3 = (f32[3,8,128]{2,1,0:T(8,128)S(1)}, f32[3,8,128]{2,1,0:T(8,128)S(1)}, u32[]{:S(2)}, u32[]{:S(2)}) collective-permute-start(f32[3,8,128]{2,1,0:T(8,128)S(1)} %get-tuple-element.78), channel_id=1, source_target_pairs={{0,64},{64,0},{128,192},{192,128},{256,320},{320,256},{384,448},{4... | collective-permute-start | bytes 36872 | tf_op jit(solution)/shard_map/ppermute | solution.py:723
  24.6 1.1 collective-permute-done.3
  25.9 12.2 %collective-permute-start.4 = (f32[7,8,128]{2,1,0:T(8,128)S(1)}, f32[7,8,128]{2,1,0:T(8,128)S(1)}, u32[]{:S(2)}, u32[]{:S(2)}) collective-permute-start(f32[7,8,128]{2,1,0:T(8,128)S(1)} %get-tuple-element.73), channel_id=1, source_target_pairs={{0,56},{8,16},{16,8},{24,32},{32,24},{40,48},{48,40},{56,0},{1,57}... | collective-permute-start | bytes 86024 | tf_op jit(solution)/shard_map/ppermute | solution.py:722
  38.2 2.5 %collective-permute-start.5 = (f32[7,8,128]{2,1,0:T(8,128)S(1)}, f32[7,8,128]{2,1,0:T(8,128)S(1)}, u32[]{:S(2)}, u32[]{:S(2)}) collective-permute-start(f32[7,8,128]{2,1,0:T(8,128)S(1)} %get-tuple-element.72), channel_id=1, source_target_pairs={{0,8},{8,0},{16,24},{24,16},{32,40},{40,32},{48,56},{56,48},{1,9},... | collective-permute-start | bytes 86024 | tf_op jit(solution)/shard_map/ppermute | solution.py:723
  41.6 6.1 %first.1 = (f32[72,128]{1,0:T(8,128)S(1)}, f32[3,8,128]{2,1,0:T(8,128)S(1)}, f32[72,128]{1,0:T(8,128)S(1)}, f32[1,128]{1,0:T(1,128)S(1)}, f32[26,24,256]{2,1,0:T(8,128)S(1)}, /*index=5*/s32[2]{0:T(128)S(1)}) custom-call(f32[7,8,128]{2,1,0:T(8,128)S(1)} %get-tuple-element.77.low, f32[7,3,8,64]{3,2,1,0:T(8,128)S(1)} %fusion.own, ...), custom_call_target="tpu_custom_call" | custom-call | tf_op jit(solution)/shard_map/first/pallas_call | solution.py:672
  47.7 2.6 %collective-permute-start.6 = (f32[3,2,128]{2,1,0:T(2,128)S(1)}, f32[3,2,128]{2,1,0:T(2,128)S(1)}, u32[]{:S(2)}, u32[]{:S(2)}) collective-permute-start(f32[3,2,128]{2,1,0:T(2,128)S(1)} %get-tuple-element.93), channel_id=1, source_target_pairs={{0,7},{1,2},{2,1},{3,4},{4,3},{5,6},{6,5},{7,0},{8,15},{9,10},{10,... | collective-permute-start | bytes 9224 | tf_op jit(solution)/shard_map/ppermute | solution.py:722
  50.4 2.9 %collective-permute-start.7 = (f32[3,2,128]{2,1,0:T(2,128)S(1)}, f32[3,2,128]{2,1,0:T(2,128)S(1)}, u32[]{:S(2)}, u32[]{:S(2)}) collective-permute-start(f32[3,2,128]{2,1,0:T(2,128)S(1)} %get-tuple-element.94), channel_id=1, source_target_pairs={{0,1},{1,0},{2,3},{3,2},{4,5},{5,4},{6,7},{7,6},{8,9},{9,8},{10,11... | collective-permute-start | bytes 9224 | tf_op jit(solution)/shard_map/ppermute | solution.py:723
  53.3 1.4 %collective-permute-done.7 = f32[3,2,128]{2,1,0:T(2,128)S(1)} collective-permute-done((f32[3,2,128]{2,1,0:T(2,128)S(1)}, f32[3,2,128]{2,1,0:T(2,128)S(1)}, u32[]{:S(2)}, u32[]{:S(2)}) %collective-permute-start.7) | collective-permute-done | bytes 3104 | tf_op jit(solution)/shard_map/ppermute | solution.py:723
  54.8 5.0 %collective-permute-start.8 = (f32[3,8,128]{2,1,0:T(8,128)S(1)}, f32[3,8,128]{2,1,0:T(8,128)S(1)}, u32[]{:S(2)}, u32[]{:S(2)}) collective-permute-start(f32[3,8,128]{2,1,0:T(8,128)S(1)} %maximum_maximum_fusion.1), channel_id=1, source_target_pairs={{0,704},{64,128},{128,64},{192,256},{256,192},{320,384},{384,320},... | collective-permute-start | bytes 36872 | tf_op jit(solution)/shard_map/ppermute | solution.py:722
  59.8 1.9 %collective-permute-start.9 = (f32[3,8,128]{2,1,0:T(8,128)S(1)}, f32[3,8,128]{2,1,0:T(8,128)S(1)}, u32[]{:S(2)}, u32[]{:S(2)}) collective-permute-start(f32[3,8,128]{2,1,0:T(8,128)S(1)} %maximum_maximum_fusion.1), channel_id=1, source_target_pairs={{0,64},{64,0},{128,192},{192,128},{256,320},{320,256},{384,448},{4... | collective-permute-start | bytes 36872 | tf_op jit(solution)/shard_map/ppermute | solution.py:723
  62.2 2.3 %collective-permute-done.9 = f32[3,8,128]{2,1,0:T(8,128)S(1)} collective-permute-done((f32[3,8,128]{2,1,0:T(8,128)S(1)}, f32[3,8,128]{2,1,0:T(8,128)S(1)}, u32[]{:S(2)}, u32[]{:S(2)}) %collective-permute-start.9) | collective-permute-done | bytes 12320 | tf_op jit(solution)/shard_map/ppermute | solution.py:723
  64.7 9.0 %collective-permute-start.10 = (f32[2,8,128]{2,1,0:T(8,128)S(1)}, f32[2,8,128]{2,1,0:T(8,128)S(1)}, u32[]{:S(2)}, u32[]{:S(2)}) collective-permute-start(f32[2,8,128]{2,1,0:T(8,128)S(1)} %get-tuple-element.92), channel_id=1, source_target_pairs={{0,56},{8,16},{16,8},{24,32},{32,24},{40,48},{48,40},{56,0},{1,57}... | collective-permute-start | bytes 24584 | tf_op jit(solution)/shard_map/ppermute | solution.py:722
  73.7 1.9 %collective-permute-start.11 = (f32[2,8,128]{2,1,0:T(8,128)S(1)}, f32[2,8,128]{2,1,0:T(8,128)S(1)}, u32[]{:S(2)}, u32[]{:S(2)}) collective-permute-start(f32[2,8,128]{2,1,0:T(8,128)S(1)} %get-tuple-element.91), channel_id=1, source_target_pairs={{0,8},{8,0},{16,24},{24,16},{32,40},{40,32},{48,56},{56,48},{1,9},... | collective-permute-start | bytes 24584 | tf_op jit(solution)/shard_map/ppermute | solution.py:723
  75.7 1.1 collective-permute-done.11
  76.8 4.4 %second.1 = (f32[72,128]{1,0:T(8,128)S(1)}, f32[1,128]{1,0:T(1,128)S(1)}) custom-call(f32[2,8,128]{2,1,0:T(8,128)S(1)} %get-tuple-element.90.low, f32[3,8,128]{2,1,0:T(8,128)S(1)} %maximum_maximum_fusion.2.own, f32[2,8,128]{2,1,0:T(8,128)S(1)} %get-tuple-element.89.high, bf16[128,16]{1,0:T(8,128)(2,1)S(1)} %get-tuple-element.48.w1t, ...), custom_call_target="tpu_custom_call" | custom-call | tf_op jit(solution)/shard_map/second/pallas_call | solution.py:699
  81.9 8.2 %all-to-all-start = ((f32[24,1,128]{2,1,0:T(1,128)}), f32[24,1,128]{2,1,0:T(1,128)S(1)}, u32[]{:S(2)}, u32[]{:S(2)}) async-start(f32[24,1,128]{2,1,0:T(1,128)} %broadcast_in_dim.35), calls=%async_computation | async-start | bytes 24576 | tf_op jit(solution)/shard_map/all_to_all | solution.py:735
  90.3 9.1 %all-to-all-done = f32[24,1,128]{2,1,0:T(1,128)S(1)} async-done(((f32[24,1,128]{2,1,0:T(1,128)}), f32[24,1,128]{2,1,0:T(1,128)S(1)}, u32[]{:S(2)}, u32[]{:S(2)}) %all-to-all-start) | async-done | bytes 12320 | tf_op jit(solution)/shard_map/all_to_all | solution.py:735
  100.1 7.2 %all-to-all-start.1 = ((f32[32,1,128]{2,1,0:T(1,128)}), f32[32,1,128]{2,1,0:T(1,128)S(1)}, u32[]{:S(2)}, u32[]{:S(2)}) async-start(f32[32,1,128]{2,1,0:T(1,128)} %broadcast_in_dim.36), calls=%async_computation.1 | async-start | bytes 32768 | tf_op jit(solution)/shard_map/all_to_all | solution.py:735
  108.3 7.7 %all-to-all-done.1 = f32[32,1,128]{2,1,0:T(1,128)S(1)} async-done(((f32[32,1,128]{2,1,0:T(1,128)}), f32[32,1,128]{2,1,0:T(1,128)S(1)}, u32[]{:S(2)}, u32[]{:S(2)}) %all-to-all-start.1) | async-done | bytes 16416 | tf_op jit(solution)/shard_map/all_to_all | solution.py:735
  (60 shorter events, 6.4 us)
Async XLA Ops:
  2.5 7.9 %copy-start.6 = (f32[9,8,128]{2,1,0:T(8,128)S(1)}, f32[9,8,128]{2,1,0:T(8,128)}, u32[]{:S(2)}) copy-start(f32[9,8,128]{2,1,0:T(8,128)} %get-tuple-element.36) | copy-start | bytes 110596
  2.5 8.0 %collective-permute-start = (f32[9,2,128]{2,1,0:T(2,128)}, f32[9,2,128]{2,1,0:T(2,128)S(1)}, u32[]{:S(2)}, u32[]{:S(2)}) collective-permute-start(f32[9,2,128]{2,1,0:T(2,128)} %get-tuple-element.34), channel_id=1, source_target_pairs={{0,7},{1,2},{2,1},{3,4},{4,3},{5,6},{6,5},{7,0},{8,15},{9,10},{10,... | collective-permute-start | bytes 27656 | tf_op jit(solution)/shard_map/ppermute | solution.py:722
  8.4 4.6 %collective-permute-start.1 = (f32[9,2,128]{2,1,0:T(2,128)}, f32[9,2,128]{2,1,0:T(2,128)S(1)}, u32[]{:S(2)}, u32[]{:S(2)}) collective-permute-start(f32[9,2,128]{2,1,0:T(2,128)} %get-tuple-element.35), channel_id=1, source_target_pairs={{0,1},{1,0},{2,3},{3,2},{4,5},{5,4},{6,7},{7,6},{8,9},{9,8},{10,11... | collective-permute-start | bytes 27656 | tf_op jit(solution)/shard_map/ppermute | solution.py:723
  13.1 10.1 %copy-start.3 = (bf16[5,128]{1,0:T(8,128)(2,1)S(1)}, bf16[5,128]{1,0:T(8,128)(2,1)}, u32[]{:S(2)}) copy-start(bf16[5,128]{1,0:T(8,128)(2,1)} %se_in.1) | copy-start | bytes 3844
  13.2 11.3 %collective-permute-start.2 = (f32[3,8,128]{2,1,0:T(8,128)S(1)}, f32[3,8,128]{2,1,0:T(8,128)S(1)}, u32[]{:S(2)}, u32[]{:S(2)}) collective-permute-start(f32[3,8,128]{2,1,0:T(8,128)S(1)} %get-tuple-element.79), channel_id=1, source_target_pairs={{0,704},{64,128},{128,64},{192,256},{256,192},{320,384},{384,320},... | collective-permute-start | bytes 36872 | tf_op jit(solution)/shard_map/ppermute | solution.py:722
  21.2 2.0 %copy-start.4 = (f32[128]{0:T(128)S(1)}, f32[128]{0:T(128)}, u32[]{:S(2)}) copy-start(f32[128]{0:T(128)} %param.20) | copy-start | bytes 1540
  21.2 2.0 %copy-start.5 = (f32[5]{0:T(128)S(1)}, f32[5]{0:T(128)}, u32[]{:S(2)}) copy-start(f32[5]{0:T(128)} %param.21) | copy-start | bytes 64
  21.2 4.4 %collective-permute-start.3 = (f32[3,8,128]{2,1,0:T(8,128)S(1)}, f32[3,8,128]{2,1,0:T(8,128)S(1)}, u32[]{:S(2)}, u32[]{:S(2)}) collective-permute-start(f32[3,8,128]{2,1,0:T(8,128)S(1)} %get-tuple-element.78), channel_id=1, source_target_pairs={{0,64},{64,0},{128,192},{192,128},{256,320},{320,256},{384,448},{4... | collective-permute-start | bytes 36872 | tf_op jit(solution)/shard_map/ppermute | solution.py:723
  23.2 0.7 copy-start.2
  23.2 0.7 copy-start
  23.2 0.7 copy-start.1
  25.9 14.8 %collective-permute-start.4 = (f32[7,8,128]{2,1,0:T(8,128)S(1)}, f32[7,8,128]{2,1,0:T(8,128)S(1)}, u32[]{:S(2)}, u32[]{:S(2)}) collective-permute-start(f32[7,8,128]{2,1,0:T(8,128)S(1)} %get-tuple-element.73), channel_id=1, source_target_pairs={{0,56},{8,16},{16,8},{24,32},{32,24},{40,48},{48,40},{56,0},{1,57}... | collective-permute-start | bytes 86024 | tf_op jit(solution)/shard_map/ppermute | solution.py:722
  38.2 3.4 %collective-permute-start.5 = (f32[7,8,128]{2,1,0:T(8,128)S(1)}, f32[7,8,128]{2,1,0:T(8,128)S(1)}, u32[]{:S(2)}, u32[]{:S(2)}) collective-permute-start(f32[7,8,128]{2,1,0:T(8,128)S(1)} %get-tuple-element.72), channel_id=1, source_target_pairs={{0,8},{8,0},{16,24},{24,16},{32,40},{40,32},{48,56},{56,48},{1,9},... | collective-permute-start | bytes 86024 | tf_op jit(solution)/shard_map/ppermute | solution.py:723
  47.7 5.6 %collective-permute-start.6 = (f32[3,2,128]{2,1,0:T(2,128)S(1)}, f32[3,2,128]{2,1,0:T(2,128)S(1)}, u32[]{:S(2)}, u32[]{:S(2)}) collective-permute-start(f32[3,2,128]{2,1,0:T(2,128)S(1)} %get-tuple-element.93), channel_id=1, source_target_pairs={{0,7},{1,2},{2,1},{3,4},{4,3},{5,6},{6,5},{7,0},{8,15},{9,10},{10,... | collective-permute-start | bytes 9224 | tf_op jit(solution)/shard_map/ppermute | solution.py:722
  50.4 4.3 %collective-permute-start.7 = (f32[3,2,128]{2,1,0:T(2,128)S(1)}, f32[3,2,128]{2,1,0:T(2,128)S(1)}, u32[]{:S(2)}, u32[]{:S(2)}) collective-permute-start(f32[3,2,128]{2,1,0:T(2,128)S(1)} %get-tuple-element.94), channel_id=1, source_target_pairs={{0,1},{1,0},{2,3},{3,2},{4,5},{5,4},{6,7},{7,6},{8,9},{9,8},{10,11... | collective-permute-start | bytes 9224 | tf_op jit(solution)/shard_map/ppermute | solution.py:723
  54.8 7.4 %collective-permute-start.8 = (f32[3,8,128]{2,1,0:T(8,128)S(1)}, f32[3,8,128]{2,1,0:T(8,128)S(1)}, u32[]{:S(2)}, u32[]{:S(2)}) collective-permute-start(f32[3,8,128]{2,1,0:T(8,128)S(1)} %maximum_maximum_fusion.1), channel_id=1, source_target_pairs={{0,704},{64,128},{128,64},{192,256},{256,192},{320,384},{384,320},... | collective-permute-start | bytes 36872 | tf_op jit(solution)/shard_map/ppermute | solution.py:722
  59.8 4.7 %collective-permute-start.9 = (f32[3,8,128]{2,1,0:T(8,128)S(1)}, f32[3,8,128]{2,1,0:T(8,128)S(1)}, u32[]{:S(2)}, u32[]{:S(2)}) collective-permute-start(f32[3,8,128]{2,1,0:T(8,128)S(1)} %maximum_maximum_fusion.1), channel_id=1, source_target_pairs={{0,64},{64,0},{128,192},{192,128},{256,320},{320,256},{384,448},{4... | collective-permute-start | bytes 36872 | tf_op jit(solution)/shard_map/ppermute | solution.py:723
  64.7 11.0 %collective-permute-start.10 = (f32[2,8,128]{2,1,0:T(8,128)S(1)}, f32[2,8,128]{2,1,0:T(8,128)S(1)}, u32[]{:S(2)}, u32[]{:S(2)}) collective-permute-start(f32[2,8,128]{2,1,0:T(8,128)S(1)} %get-tuple-element.92), channel_id=1, source_target_pairs={{0,56},{8,16},{16,8},{24,32},{32,24},{40,48},{48,40},{56,0},{1,57}... | collective-permute-start | bytes 24584 | tf_op jit(solution)/shard_map/ppermute | solution.py:722
  73.7 3.1 %collective-permute-start.11 = (f32[2,8,128]{2,1,0:T(8,128)S(1)}, f32[2,8,128]{2,1,0:T(8,128)S(1)}, u32[]{:S(2)}, u32[]{:S(2)}) collective-permute-start(f32[2,8,128]{2,1,0:T(8,128)S(1)} %get-tuple-element.91), channel_id=1, source_target_pairs={{0,8},{8,0},{16,24},{24,16},{32,40},{40,32},{48,56},{56,48},{1,9},... | collective-permute-start | bytes 24584 | tf_op jit(solution)/shard_map/ppermute | solution.py:723
  81.9 17.6 %all-to-all-start = ((f32[24,1,128]{2,1,0:T(1,128)}), f32[24,1,128]{2,1,0:T(1,128)S(1)}, u32[]{:S(2)}, u32[]{:S(2)}) async-start(f32[24,1,128]{2,1,0:T(1,128)} %broadcast_in_dim.35), calls=%async_computation | async-start | bytes 24576 | tf_op jit(solution)/shard_map/all_to_all | solution.py:735
  100.1 15.9 %all-to-all-start.1 = ((f32[32,1,128]{2,1,0:T(1,128)}), f32[32,1,128]{2,1,0:T(1,128)S(1)}, u32[]{:S(2)}, u32[]{:S(2)}) async-start(f32[32,1,128]{2,1,0:T(1,128)} %broadcast_in_dim.36), calls=%async_computation.1 | async-start | bytes 32768 | tf_op jit(solution)/shard_map/all_to_all | solution.py:735

commit v6 on v5

--- a/solution.py
+++ b/solution.py
@@ -213,7 +213,7 @@
     return 2.0 * s * c, 1.0 - 2.0 * s * s
 
 
-def evaluate(refs, scratch, counts, own_out, moved):
+def evaluate(refs, scratch, counts, own_out, moved, early=False):
     pos_t, pairs_ref, w1t, w1, wmt, wm, smt, sm, eo_ref = refs
     env_ref, envs_ref, grad_ref, geo_ref, feat_ref, lat_ref, slope_ref, h_ref, wb_ref, hp_ref = (
         scratch[:-1]
@@ -228,7 +228,8 @@
     env_ref[...] = jnp.zeros(env_ref.shape, F32)
     grad_ref[...] = jnp.zeros(grad_ref.shape, F32)
     en_ref[...] = jnp.zeros(en_ref.shape, F32)
-    own_out[...] = jnp.zeros(own_out.shape, F32)
+    if not early:
+        own_out[...] = jnp.zeros(own_out.shape, F32)
 
     def gathered(place, layer, slot):
         got = mm(pos_t[...], one_hot(place, LAYER, LAYER))
@@ -302,10 +303,10 @@
         env_ref[CH:] += mm_nt(moments[CH:], hit_i - hit_j)
         return carry
 
-    lax.fori_loop(0, every, stage_one, jnp.int32(0))
+    lax.fori_loop(0, front if early else every, stage_one, jnp.int32(0))
     envs_ref[...] = env_ref[...].astype(BF16)
 
-    def stage_two(t, carry):
+    def forward(t):
         pair = pairs_ref[t]
         geo = geo_ref[t]
         valid = pair[8:9]
@@ -323,9 +324,20 @@
         coupling = (env_scale * w * aligned).astype(BF16)
         arg = lat_ref[t].astype(F32) + mm(smt[...], coupling)
         gate = sigmoid(arg)
-        hidden = arg * gate
-        dotted = jnp.sum(hidden * eo(), axis=0, keepdims=True)
-        en_ref[0:1] += f * dotted * pair[12:13]
+        dotted = jnp.sum(arg * gate * eo(), axis=0, keepdims=True)
+        return valid, u, f, hit, env, aligned, w, arg, gate, dotted, f * dotted * pair[12:13]
+
+    def stage_energy(t, carry):
+        en_ref[0:1] += forward(t)[-1]
+        return carry
+
+    if early:
+        lax.fori_loop(0, front, stage_energy, jnp.int32(0))
+        return
+
+    def stage_two(t, carry):
+        valid, u, f, hit, env, aligned, w, arg, gate, dotted, energy = forward(t)
+        en_ref[0:1] += energy
         arg_bar = (f * valid) * eo() * (gate * (1.0 + arg * (1.0 - gate)))
         arg_bar = arg_bar.astype(BF16)
         hp_ref[t] = arg_bar
@@ -557,17 +569,28 @@
     energy_out[...] = energy_row(jnp.sum(scratch[-1][0:1]) + atoms, atoms, jnp.sum(live))
 
 
-def second_kernel(low, own, high, w1t, w1, wmt, wm, smt, sm, eo, pairs_ref, counts_ref, energy_in,
-                  live, force_out, energy_out, pos_t, own_ref, *scratch):
+def moved_positions(low, own, high, pos_t):
     layers = [piece[i] for piece, width in ((low, 2), (own, 3), (high, 2)) for i in range(width)]
     turned = jnp.transpose(deepen(jnp.concatenate(layers, axis=0), LANES))
     blocks = [turned[x * 16 : x * 16 + 8] for x in range(7)] + [jnp.zeros((8, LANES), F32)]
     put_positions(jnp.concatenate(blocks, axis=0), pos_t)
+
+
+def energy_kernel(low, own, high, w1t, w1, wmt, wm, smt, sm, eo, pairs_ref, counts_ref, energy_in,
+                  energy_out, pos_t, *scratch):
+    moved_positions(low, own, high, pos_t)
+    refs = (pos_t, pairs_ref, w1t, w1, wmt, wm, smt, sm, eo)
+    evaluate(refs, scratch, (counts_ref[0], counts_ref[1]), None, True, early=True)
+    energy_out[...] = energy_in[...] + energy_row(0.0, jnp.sum(scratch[-1][0:1]), 0.0)
+
+
+def second_kernel(low, own, high, w1t, w1, wmt, wm, smt, sm, eo, pairs_ref, counts_ref, live,
+                  force_out, pos_t, own_ref, *scratch):
+    moved_positions(low, own, high, pos_t)
     refs = (pos_t, pairs_ref, w1t, w1, wmt, wm, smt, sm, eo)
     evaluate(refs, scratch, (counts_ref[0], counts_ref[1]), own_ref, True)
     lane, inside = own_lane_row()
     force_out[...] = jnp.where(inside & (lane < 6.0), own_ref[0:72] * live[...], 0.0)
-    energy_out[...] = energy_in[...] + energy_row(0.0, jnp.sum(scratch[-1][0:1]), 0.0)
 
 
 def energy_row(first, second, live):
@@ -695,20 +718,33 @@
     )(*pieces, *prepared)
 
 
-def second_call(pieces, weights, pairs, counts, energy, live):
+def energy_call(pieces, weights, pairs, counts, energy):
+    return pl.pallas_call(
+        energy_kernel,
+        name="energy",
+        out_shape=shape(1, LANES),
+        in_specs=[VM] * (len(pieces) + len(weights) + 1) + [SM, VM],
+        out_specs=VM,
+        scratch_shapes=(pltpu.VMEM((3 * LAYER, LAYER), BF16), *EVAL_SCRATCH),
+        compiler_params=limit(20),
+    )(*pieces, *weights, pairs, counts, energy)
+
+
+def second_call(pieces, weights, pairs, counts, live):
     return pl.pallas_call(
         second_kernel,
         name="second",
-        out_shape=(shape(72, LANES), shape(1, LANES)),
-        in_specs=[VM] * (len(pieces) + len(weights) + 1) + [SM, VM, VM],
-        out_specs=(VM, VM),
+        out_shape=shape(72, LANES),
+        in_specs=[VM] * (len(pieces) + len(weights) + 1) + [SM, VM],
+        out_specs=VM,
         scratch_shapes=(
             pltpu.VMEM((3 * LAYER, LAYER), BF16),
             pltpu.VMEM((OWN, LANES), F32),
             *EVAL_SCRATCH,
         ),
         compiler_params=limit(20),
-    )(*pieces, *weights, pairs, counts, energy, live)
+        cost_estimate=pl.CostEstimate(flops=400000000, transcendentals=0, bytes_accessed=4000000),
+    )(*pieces, *weights, pairs, counts, live)
 
 
 def is_even(axis):
@@ -743,7 +779,8 @@
         [(k * part + i) * ny + j for k in range(3) for j in range(ny)] for i in range(part)
     ]
     planes = [[(k * part + i) * nz + j for i in range(part) for j in range(nz)] for k in range(3)]
-    return everywhere(everywhere(row, ("gx", "gy"), columns), ("gx", "gz"), planes)
+    row = everywhere(row, ("gx", "gy"), columns)
+    return everywhere(row, ("gx", "gz"), planes)
 
 
 def spread_rows(rows, across, within, beside):
@@ -789,10 +826,10 @@
     )
     pieces, prepared = spread_rows(*sent, prepared)
     force_one, moved, live, energy_one, pairs, counts = first_call(pieces, prepared)
-    force_two, energies = second_call(
-        spread_moved(moved), prepared[0:7], pairs, counts, energy_one, live
-    )
+    pieces = spread_moved(moved)
+    energies = energy_call(pieces, prepared[0:7], pairs, counts, energy_one)
     totals = everyone(energies)
+    force_two = second_call(pieces, prepared[0:7], pairs, counts, live)
     forces = jnp.stack([unpack(force_one), unpack(force_two)])
     return forces, totals[0, 0:2] / totals[0, 2:4]
 

time: 117 us -> 114 us (0.974)
  waiting for transfers between devices: 26.4 us -> 22.1 us
  Pallas kernels: 13 us -> 14.8 us
    all_to_all x2, waiting for transfers between devices: 16.8 us -> 12.5 us  [everywhere(): lax.all_to_all(rows, axes, 0, 0, axis_index_groups=groups, tiled=False)]
    pallas_call x1 -> x2, Pallas kernels: 4.45 us -> 6.27 us  [the longest x1 4.35 us: second_call(): pl.pallas_call(second_kernel, name='second', out_shape=shape(72, LANES),...]
  transfers between devices with their start and end apart: 14 -> 14, of which waited for: 9 -> 9; matrix products, arithmetic and copies ran while one was open for 1% -> 1% of each run, Pallas kernels for 1% -> 4%
where the time goes in v6:
time: 114 us; the launch traced here: 113 us
  starting transfers between devices  70.5 us (62%)
  waiting for transfers between devices  22.1 us (19%)
  Pallas kernels  14.8 us (13%)
  local copies, waits for them, and re-layouts  3.47 us (3%)
  other arithmetic  1.17 us (1%)
    ppermute x6, starting transfers between devices, trade(): across = lax.ppermute(across, axis, outer)  42.8 us
    all_to_all x2, starting transfers between devices, everywhere(): lax.all_to_all(rows, axes, 0, 0, axis_index_groups=groups, tiled=False)  14.5 us
    ppermute x6, starting transfers between devices, trade(): within = lax.ppermute(within, axis, inner)  13.2 us
    all_to_all x2, waiting for transfers between devices, everywhere(): lax.all_to_all(rows, axes, 0, 0, axis_index_groups=groups, tiled=False)  12.5 us
    ppermute x6, waiting for transfers between devices, trade(): within = lax.ppermute(within, axis, inner)  9.2 us
    pallas_call x1, Pallas kernels, first_call(): pl.pallas_call(first_kernel, name='first', out_shape=(shape(72, LANES), s...  6.11 us
    pallas_call x1, Pallas kernels, second_call(): pl.pallas_call(second_kernel, name='second', out_shape=shape(72, LANES),...  4.35 us
  transfers between devices with their start and end apart: 14, of which 9 were waited for; matrix products, arithmetic and copies ran while one was open for 1% of the time, Pallas kernels for 4%

profile of v6, /device:TPU:1, one launch (start us, length us, event | category | flops | bytes accessed | tf_op | source)
XLA Modules:
  0.0 113.1 jit_solution(1191667782961888898)
XLA Ops:
  0.6 1.8 %pack.1 = (f32[9,8,128]{2,1,0:T(8,128)}, f32[9,2,128]{2,1,0:T(2,128)}, f32[9,2,128]{2,1,0:T(2,128)}) custom-call(f32[3,3,3,2,3]{4,3,2,1,0:T(2,128)} %bitcast.67, f32[3,3,3,2,3]{4,3,2,1,0:T(2,128)} %bitcast.68, s32[3,3,2,3]{3,2,1,0:T(2,128)} %bitcast.69, s32[3,3,3]{2,1,0:T(4,128)} %count_in.1, s32[3,3,3,2,40]{4,3,2,1,0:T(2,128)} %list_in.1), custom_call_target="tpu_custom_call" | custom-call | tf_op jit(solution)/shard_map/pack/pallas_call | solution.py:632
  2.5 5.9 %collective-permute-start = (f32[9,2,128]{2,1,0:T(2,128)}, f32[9,2,128]{2,1,0:T(2,128)S(1)}, u32[]{:S(2)}, u32[]{:S(2)}) collective-permute-start(f32[9,2,128]{2,1,0:T(2,128)} %get-tuple-element.32), channel_id=1, source_target_pairs={{0,7},{1,2},{2,1},{3,4},{4,3},{5,6},{6,5},{7,0},{8,15},{9,10},{10,... | collective-permute-start | bytes 27656 | tf_op jit(solution)/shard_map/ppermute | solution.py:758
  8.4 1.9 %collective-permute-start.1 = (f32[9,2,128]{2,1,0:T(2,128)}, f32[9,2,128]{2,1,0:T(2,128)S(1)}, u32[]{:S(2)}, u32[]{:S(2)}) collective-permute-start(f32[9,2,128]{2,1,0:T(2,128)} %get-tuple-element.33), channel_id=1, source_target_pairs={{0,1},{1,0},{2,3},{3,2},{4,5},{5,4},{6,7},{7,6},{8,9},{9,8},{10,11... | collective-permute-start | bytes 27656 | tf_op jit(solution)/shard_map/ppermute | solution.py:759
  10.5 2.6 %collective-permute-done.1 = f32[9,2,128]{2,1,0:T(2,128)S(1)} collective-permute-done((f32[9,2,128]{2,1,0:T(2,128)}, f32[9,2,128]{2,1,0:T(2,128)S(1)}, u32[]{:S(2)}, u32[]{:S(2)}) %collective-permute-start.1) | collective-permute-done | bytes 9248 | tf_op jit(solution)/shard_map/ppermute | solution.py:759
  13.2 8.0 %collective-permute-start.2 = (f32[3,8,128]{2,1,0:T(8,128)S(1)}, f32[3,8,128]{2,1,0:T(8,128)S(1)}, u32[]{:S(2)}, u32[]{:S(2)}) collective-permute-start(f32[3,8,128]{2,1,0:T(8,128)S(1)} %get-tuple-element.75), channel_id=1, source_target_pairs={{0,704},{64,128},{128,64},{192,256},{256,192},{320,384},{384,320},... | collective-permute-start | bytes 36872 | tf_op jit(solution)/shard_map/ppermute | solution.py:758
  21.2 1.9 %collective-permute-start.3 = (f32[3,8,128]{2,1,0:T(8,128)S(1)}, f32[3,8,128]{2,1,0:T(8,128)S(1)}, u32[]{:S(2)}, u32[]{:S(2)}) collective-permute-start(f32[3,8,128]{2,1,0:T(8,128)S(1)} %get-tuple-element.74), channel_id=1, source_target_pairs={{0,64},{64,0},{128,192},{192,128},{256,320},{320,256},{384,448},{4... | collective-permute-start | bytes 36872 | tf_op jit(solution)/shard_map/ppermute | solution.py:759
  24.6 1.1 collective-permute-done.3
  25.9 12.2 %collective-permute-start.4 = (f32[7,8,128]{2,1,0:T(8,128)S(1)}, f32[7,8,128]{2,1,0:T(8,128)S(1)}, u32[]{:S(2)}, u32[]{:S(2)}) collective-permute-start(f32[7,8,128]{2,1,0:T(8,128)S(1)} %get-tuple-element.69), channel_id=1, source_target_pairs={{0,56},{8,16},{16,8},{24,32},{32,24},{40,48},{48,40},{56,0},{1,57}... | collective-permute-start | bytes 86024 | tf_op jit(solution)/shard_map/ppermute | solution.py:758
  38.2 2.5 %collective-permute-start.5 = (f32[7,8,128]{2,1,0:T(8,128)S(1)}, f32[7,8,128]{2,1,0:T(8,128)S(1)}, u32[]{:S(2)}, u32[]{:S(2)}) collective-permute-start(f32[7,8,128]{2,1,0:T(8,128)S(1)} %get-tuple-element.68), channel_id=1, source_target_pairs={{0,8},{8,0},{16,24},{24,16},{32,40},{40,32},{48,56},{56,48},{1,9},... | collective-permute-start | bytes 86024 | tf_op jit(solution)/shard_map/ppermute | solution.py:759
  41.6 6.1 %first.1 = (f32[72,128]{1,0:T(8,128)S(1)}, f32[3,8,128]{2,1,0:T(8,128)S(1)}, f32[72,128]{1,0:T(8,128)S(1)}, f32[1,128]{1,0:T(1,128)S(1)}, f32[26,24,256]{2,1,0:T(8,128)S(1)}, /*index=5*/s32[2]{0:T(128)S(1)}) custom-call(f32[7,8,128]{2,1,0:T(8,128)S(1)} %get-tuple-element.73.low, f32[7,3,8,64]{3,2,1,0:T(8,128)S(1)} %fusion.own, ...), custom_call_target="tpu_custom_call" | custom-call | tf_op jit(solution)/shard_map/first/pallas_call | solution.py:695
  47.7 2.6 %collective-permute-start.6 = (f32[3,2,128]{2,1,0:T(2,128)S(1)}, f32[3,2,128]{2,1,0:T(2,128)S(1)}, u32[]{:S(2)}, u32[]{:S(2)}) collective-permute-start(f32[3,2,128]{2,1,0:T(2,128)S(1)} %get-tuple-element.89), channel_id=1, source_target_pairs={{0,7},{1,2},{2,1},{3,4},{4,3},{5,6},{6,5},{7,0},{8,15},{9,10},{10,... | collective-permute-start | bytes 9224 | tf_op jit(solution)/shard_map/ppermute | solution.py:758
  50.4 2.9 %collective-permute-start.7 = (f32[3,2,128]{2,1,0:T(2,128)S(1)}, f32[3,2,128]{2,1,0:T(2,128)S(1)}, u32[]{:S(2)}, u32[]{:S(2)}) collective-permute-start(f32[3,2,128]{2,1,0:T(2,128)S(1)} %get-tuple-element.90), channel_id=1, source_target_pairs={{0,1},{1,0},{2,3},{3,2},{4,5},{5,4},{6,7},{7,6},{8,9},{9,8},{10,11... | collective-permute-start | bytes 9224 | tf_op jit(solution)/shard_map/ppermute | solution.py:759
  53.3 1.4 %collective-permute-done.7 = f32[3,2,128]{2,1,0:T(2,128)S(1)} collective-permute-done((f32[3,2,128]{2,1,0:T(2,128)S(1)}, f32[3,2,128]{2,1,0:T(2,128)S(1)}, u32[]{:S(2)}, u32[]{:S(2)}) %collective-permute-start.7) | collective-permute-done | bytes 3104 | tf_op jit(solution)/shard_map/ppermute | solution.py:759
  54.8 5.0 %collective-permute-start.8 = (f32[3,8,128]{2,1,0:T(8,128)S(1)}, f32[3,8,128]{2,1,0:T(8,128)S(1)}, u32[]{:S(2)}, u32[]{:S(2)}) collective-permute-start(f32[3,8,128]{2,1,0:T(8,128)S(1)} %maximum_maximum_fusion.1), channel_id=1, source_target_pairs={{0,704},{64,128},{128,64},{192,256},{256,192},{320,384},{384,320},... | collective-permute-start | bytes 36872 | tf_op jit(solution)/shard_map/ppermute | solution.py:758
  59.8 1.9 %collective-permute-start.9 = (f32[3,8,128]{2,1,0:T(8,128)S(1)}, f32[3,8,128]{2,1,0:T(8,128)S(1)}, u32[]{:S(2)}, u32[]{:S(2)}) collective-permute-start(f32[3,8,128]{2,1,0:T(8,128)S(1)} %maximum_maximum_fusion.1), channel_id=1, source_target_pairs={{0,64},{64,0},{128,192},{192,128},{256,320},{320,256},{384,448},{4... | collective-permute-start | bytes 36872 | tf_op jit(solution)/shard_map/ppermute | solution.py:759
  62.2 2.3 %collective-permute-done.9 = f32[3,8,128]{2,1,0:T(8,128)S(1)} collective-permute-done((f32[3,8,128]{2,1,0:T(8,128)S(1)}, f32[3,8,128]{2,1,0:T(8,128)S(1)}, u32[]{:S(2)}, u32[]{:S(2)}) %collective-permute-start.9) | collective-permute-done | bytes 12320 | tf_op jit(solution)/shard_map/ppermute | solution.py:759
  64.7 9.0 %collective-permute-start.10 = (f32[2,8,128]{2,1,0:T(8,128)S(1)}, f32[2,8,128]{2,1,0:T(8,128)S(1)}, u32[]{:S(2)}, u32[]{:S(2)}) collective-permute-start(f32[2,8,128]{2,1,0:T(8,128)S(1)} %get-tuple-element.88), channel_id=1, source_target_pairs={{0,56},{8,16},{16,8},{24,32},{32,24},{40,48},{48,40},{56,0},{1,57}... | collective-permute-start | bytes 24584 | tf_op jit(solution)/shard_map/ppermute | solution.py:758
  73.7 1.9 %collective-permute-start.11 = (f32[2,8,128]{2,1,0:T(8,128)S(1)}, f32[2,8,128]{2,1,0:T(8,128)S(1)}, u32[]{:S(2)}, u32[]{:S(2)}) collective-permute-start(f32[2,8,128]{2,1,0:T(8,128)S(1)} %get-tuple-element.87), channel_id=1, source_target_pairs={{0,8},{8,0},{16,24},{24,16},{32,40},{40,32},{48,56},{56,48},{1,9},... | collective-permute-start | bytes 24584 | tf_op jit(solution)/shard_map/ppermute | solution.py:759
  76.8 1.9 %energy.1 = f32[1,128]{1,0:T(1,128)S(1)} custom-call(f32[2,8,128]{2,1,0:T(8,128)S(1)} %get-tuple-element.86.low, f32[3,8,128]{2,1,0:T(8,128)S(1)} %maximum_maximum_fusion.2.own, f32[2,8,128]{2,1,0:T(8,128)S(1)} %get-tuple-element.85.high, bf16[128,16]{1,0:T(8,128)(2,1)S(1)} %get-tuple-element.46.w1t, bf16[16,128]{1,0:T(8,128)(2,1)S(1)} %get-tuple-element.47.w1, ...), custom_call_target="tpu_custom_call" | custom-call | tf_op jit(solution)/shard_map/energy/pallas_call | solution.py:722
  79.3 8.2 %all-to-all-start = ((f32[24,1,128]{2,1,0:T(1,128)}), f32[24,1,128]{2,1,0:T(1,128)S(1)}, u32[]{:S(2)}, u32[]{:S(2)}) async-start(f32[24,1,128]{2,1,0:T(1,128)} %broadcast_in_dim.35), calls=%async_computation | async-start | bytes 24576 | tf_op jit(solution)/shard_map/all_to_all | solution.py:771
  87.6 4.3 %second.1 = f32[72,128]{1,0:T(8,128)S(1)} custom-call(f32[2,8,128]{2,1,0:T(8,128)S(1)} %get-tuple-element.86.low, f32[3,8,128]{2,1,0:T(8,128)S(1)} %maximum_maximum_fusion.2.own, f32[2,8,128]{2,1,0:T(8,128)S(1)} %get-tuple-element.85.high, bf16[128,16]{1,0:T(8,128)(2,1)S(1)} %get-tuple-element.46.w1t, bf16[16,128]{1,0:T(8,128)(2,1)S(1)} %get-tuple-element.47.w1, ...), custom_call_target="tpu_custom_call" | custom-call | flops 400000000 | bytes 4000000 | tf_op jit(solution)/shard_map/second/pallas_call | solution.py:734
  92.0 4.9 %all-to-all-done = f32[24,1,128]{2,1,0:T(1,128)S(1)} async-done(((f32[24,1,128]{2,1,0:T(1,128)}), f32[24,1,128]{2,1,0:T(1,128)S(1)}, u32[]{:S(2)}, u32[]{:S(2)}) %all-to-all-start) | async-done | bytes 12320 | tf_op jit(solution)/shard_map/all_to_all | solution.py:771
  97.5 6.3 %all-to-all-start.1 = ((f32[32,1,128]{2,1,0:T(1,128)}), f32[32,1,128]{2,1,0:T(1,128)S(1)}, u32[]{:S(2)}, u32[]{:S(2)}) async-start(f32[32,1,128]{2,1,0:T(1,128)} %broadcast_in_dim.36), calls=%async_computation.1 | async-start | bytes 32768 | tf_op jit(solution)/shard_map/all_to_all | solution.py:771
  104.8 7.7 %all-to-all-done.1 = f32[32,1,128]{2,1,0:T(1,128)S(1)} async-done(((f32[32,1,128]{2,1,0:T(1,128)}), f32[32,1,128]{2,1,0:T(1,128)S(1)}, u32[]{:S(2)}, u32[]{:S(2)}) %all-to-all-start.1) | async-done | bytes 16416 | tf_op jit(solution)/shard_map/all_to_all | solution.py:771
  (61 shorter events, 7.5 us)
Async XLA Ops:
  2.5 7.9 %copy-start.6 = (f32[9,8,128]{2,1,0:T(8,128)S(1)}, f32[9,8,128]{2,1,0:T(8,128)}, u32[]{:S(2)}) copy-start(f32[9,8,128]{2,1,0:T(8,128)} %get-tuple-element.34) | copy-start | bytes 110596
  2.5 8.0 %collective-permute-start = (f32[9,2,128]{2,1,0:T(2,128)}, f32[9,2,128]{2,1,0:T(2,128)S(1)}, u32[]{:S(2)}, u32[]{:S(2)}) collective-permute-start(f32[9,2,128]{2,1,0:T(2,128)} %get-tuple-element.32), channel_id=1, source_target_pairs={{0,7},{1,2},{2,1},{3,4},{4,3},{5,6},{6,5},{7,0},{8,15},{9,10},{10,... | collective-permute-start | bytes 27656 | tf_op jit(solution)/shard_map/ppermute | solution.py:758
  8.4 4.6 %collective-permute-start.1 = (f32[9,2,128]{2,1,0:T(2,128)}, f32[9,2,128]{2,1,0:T(2,128)S(1)}, u32[]{:S(2)}, u32[]{:S(2)}) collective-permute-start(f32[9,2,128]{2,1,0:T(2,128)} %get-tuple-element.33), channel_id=1, source_target_pairs={{0,1},{1,0},{2,3},{3,2},{4,5},{5,4},{6,7},{7,6},{8,9},{9,8},{10,11... | collective-permute-start | bytes 27656 | tf_op jit(solution)/shard_map/ppermute | solution.py:759
  13.1 10.1 %copy-start.3 = (bf16[5,128]{1,0:T(8,128)(2,1)S(1)}, bf16[5,128]{1,0:T(8,128)(2,1)}, u32[]{:S(2)}) copy-start(bf16[5,128]{1,0:T(8,128)(2,1)} %se_in.1) | copy-start | bytes 3844
  13.2 11.3 %collective-permute-start.2 = (f32[3,8,128]{2,1,0:T(8,128)S(1)}, f32[3,8,128]{2,1,0:T(8,128)S(1)}, u32[]{:S(2)}, u32[]{:S(2)}) collective-permute-start(f32[3,8,128]{2,1,0:T(8,128)S(1)} %get-tuple-element.75), channel_id=1, source_target_pairs={{0,704},{64,128},{128,64},{192,256},{256,192},{320,384},{384,320},... | collective-permute-start | bytes 36872 | tf_op jit(solution)/shard_map/ppermute | solution.py:758
  21.2 2.0 %copy-start.4 = (f32[128]{0:T(128)S(1)}, f32[128]{0:T(128)}, u32[]{:S(2)}) copy-start(f32[128]{0:T(128)} %param.20) | copy-start | bytes 1540
  21.2 2.0 %copy-start.5 = (f32[5]{0:T(128)S(1)}, f32[5]{0:T(128)}, u32[]{:S(2)}) copy-start(f32[5]{0:T(128)} %param.21) | copy-start | bytes 64
  21.2 4.4 %collective-permute-start.3 = (f32[3,8,128]{2,1,0:T(8,128)S(1)}, f32[3,8,128]{2,1,0:T(8,128)S(1)}, u32[]{:S(2)}, u32[]{:S(2)}) collective-permute-start(f32[3,8,128]{2,1,0:T(8,128)S(1)} %get-tuple-element.74), channel_id=1, source_target_pairs={{0,64},{64,0},{128,192},{192,128},{256,320},{320,256},{384,448},{4... | collective-permute-start | bytes 36872 | tf_op jit(solution)/shard_map/ppermute | solution.py:759
  23.2 0.7 copy-start.2
  23.2 0.7 copy-start
  23.2 0.7 copy-start.1
  25.9 14.8 %collective-permute-start.4 = (f32[7,8,128]{2,1,0:T(8,128)S(1)}, f32[7,8,128]{2,1,0:T(8,128)S(1)}, u32[]{:S(2)}, u32[]{:S(2)}) collective-permute-start(f32[7,8,128]{2,1,0:T(8,128)S(1)} %get-tuple-element.69), channel_id=1, source_target_pairs={{0,56},{8,16},{16,8},{24,32},{32,24},{40,48},{48,40},{56,0},{1,57}... | collective-permute-start | bytes 86024 | tf_op jit(solution)/shard_map/ppermute | solution.py:758
  38.2 3.4 %collective-permute-start.5 = (f32[7,8,128]{2,1,0:T(8,128)S(1)}, f32[7,8,128]{2,1,0:T(8,128)S(1)}, u32[]{:S(2)}, u32[]{:S(2)}) collective-permute-start(f32[7,8,128]{2,1,0:T(8,128)S(1)} %get-tuple-element.68), channel_id=1, source_target_pairs={{0,8},{8,0},{16,24},{24,16},{32,40},{40,32},{48,56},{56,48},{1,9},... | collective-permute-start | bytes 86024 | tf_op jit(solution)/shard_map/ppermute | solution.py:759
  47.7 5.6 %collective-permute-start.6 = (f32[3,2,128]{2,1,0:T(2,128)S(1)}, f32[3,2,128]{2,1,0:T(2,128)S(1)}, u32[]{:S(2)}, u32[]{:S(2)}) collective-permute-start(f32[3,2,128]{2,1,0:T(2,128)S(1)} %get-tuple-element.89), channel_id=1, source_target_pairs={{0,7},{1,2},{2,1},{3,4},{4,3},{5,6},{6,5},{7,0},{8,15},{9,10},{10,... | collective-permute-start | bytes 9224 | tf_op jit(solution)/shard_map/ppermute | solution.py:758
  50.4 4.3 %collective-permute-start.7 = (f32[3,2,128]{2,1,0:T(2,128)S(1)}, f32[3,2,128]{2,1,0:T(2,128)S(1)}, u32[]{:S(2)}, u32[]{:S(2)}) collective-permute-start(f32[3,2,128]{2,1,0:T(2,128)S(1)} %get-tuple-element.90), channel_id=1, source_target_pairs={{0,1},{1,0},{2,3},{3,2},{4,5},{5,4},{6,7},{7,6},{8,9},{9,8},{10,11... | collective-permute-start | bytes 9224 | tf_op jit(solution)/shard_map/ppermute | solution.py:759
  54.8 7.4 %collective-permute-start.8 = (f32[3,8,128]{2,1,0:T(8,128)S(1)}, f32[3,8,128]{2,1,0:T(8,128)S(1)}, u32[]{:S(2)}, u32[]{:S(2)}) collective-permute-start(f32[3,8,128]{2,1,0:T(8,128)S(1)} %maximum_maximum_fusion.1), channel_id=1, source_target_pairs={{0,704},{64,128},{128,64},{192,256},{256,192},{320,384},{384,320},... | collective-permute-start | bytes 36872 | tf_op jit(solution)/shard_map/ppermute | solution.py:758
  59.8 4.7 %collective-permute-start.9 = (f32[3,8,128]{2,1,0:T(8,128)S(1)}, f32[3,8,128]{2,1,0:T(8,128)S(1)}, u32[]{:S(2)}, u32[]{:S(2)}) collective-permute-start(f32[3,8,128]{2,1,0:T(8,128)S(1)} %maximum_maximum_fusion.1), channel_id=1, source_target_pairs={{0,64},{64,0},{128,192},{192,128},{256,320},{320,256},{384,448},{4... | collective-permute-start | bytes 36872 | tf_op jit(solution)/shard_map/ppermute | solution.py:759
  64.7 11.1 %collective-permute-start.10 = (f32[2,8,128]{2,1,0:T(8,128)S(1)}, f32[2,8,128]{2,1,0:T(8,128)S(1)}, u32[]{:S(2)}, u32[]{:S(2)}) collective-permute-start(f32[2,8,128]{2,1,0:T(8,128)S(1)} %get-tuple-element.88), channel_id=1, source_target_pairs={{0,56},{8,16},{16,8},{24,32},{32,24},{40,48},{48,40},{56,0},{1,57}... | collective-permute-start | bytes 24584 | tf_op jit(solution)/shard_map/ppermute | solution.py:758
  73.7 3.1 %collective-permute-start.11 = (f32[2,8,128]{2,1,0:T(8,128)S(1)}, f32[2,8,128]{2,1,0:T(8,128)S(1)}, u32[]{:S(2)}, u32[]{:S(2)}) collective-permute-start(f32[2,8,128]{2,1,0:T(8,128)S(1)} %get-tuple-element.87), channel_id=1, source_target_pairs={{0,8},{8,0},{16,24},{24,16},{32,40},{40,32},{48,56},{56,48},{1,9},... | collective-permute-start | bytes 24584 | tf_op jit(solution)/shard_map/ppermute | solution.py:759
  79.3 17.6 %all-to-all-start = ((f32[24,1,128]{2,1,0:T(1,128)}), f32[24,1,128]{2,1,0:T(1,128)S(1)}, u32[]{:S(2)}, u32[]{:S(2)}) async-start(f32[24,1,128]{2,1,0:T(1,128)} %broadcast_in_dim.35), calls=%async_computation | async-start | bytes 24576 | tf_op jit(solution)/shard_map/all_to_all | solution.py:771
  97.5 15.0 %all-to-all-start.1 = ((f32[32,1,128]{2,1,0:T(1,128)}), f32[32,1,128]{2,1,0:T(1,128)S(1)}, u32[]{:S(2)}, u32[]{:S(2)}) async-start(f32[32,1,128]{2,1,0:T(1,128)} %broadcast_in_dim.36), calls=%async_computation.1 | async-start | bytes 32768 | tf_op jit(solution)/shard_map/all_to_all | solution.py:771

commit v7 on v6

--- a/solution.py
+++ b/solution.py
@@ -226,7 +226,8 @@
         return jnp.concatenate([eo_ref[...], eo_ref[...]], axis=1)
 
     env_ref[...] = jnp.zeros(env_ref.shape, F32)
-    grad_ref[...] = jnp.zeros(grad_ref.shape, F32)
+    if not early:
+        grad_ref[...] = jnp.zeros(grad_ref.shape, F32)
     en_ref[...] = jnp.zeros(en_ref.shape, F32)
     if not early:
         own_out[...] = jnp.zeros(own_out.shape, F32)
@@ -779,8 +780,8 @@
         [(k * part + i) * ny + j for k in range(3) for j in range(ny)] for i in range(part)
     ]
     planes = [[(k * part + i) * nz + j for i in range(part) for j in range(nz)] for k in range(3)]
-    row = everywhere(row, ("gx", "gy"), columns)
-    return everywhere(row, ("gx", "gz"), planes)
+    row = everywhere(row, ("gx", "gz"), planes)
+    return everywhere(row, ("gx", "gy"), columns)
 
 
 def spread_rows(rows, across, within, beside):

time: 114 us -> 115 us (level)
  starting transfers between devices: 70.5 us -> 71.9 us
    all_to_all x2, starting transfers between devices: 14.5 us -> 15.9 us  [everywhere(): lax.all_to_all(rows, axes, 0, 0, axis_index_groups=groups, tiled=False)]
where the time goes in v7:
time: 115 us
  starting transfers between devices  71.9 us (63%)
  waiting for transfers between devices  22.1 us (19%)
  Pallas kernels  14.8 us (13%)
  local copies, waits for them, and re-layouts  3.47 us (3%)
  other arithmetic  1.17 us (1%)
    ppermute x6, starting transfers between devices, trade(): across = lax.ppermute(across, axis, outer)  42.8 us
    all_to_all x2, starting transfers between devices, everywhere(): lax.all_to_all(rows, axes, 0, 0, axis_index_groups=groups, tiled=False)  15.9 us
    ppermute x6, starting transfers between devices, trade(): within = lax.ppermute(within, axis, inner)  13.2 us
    all_to_all x2, waiting for transfers between devices, everywhere(): lax.all_to_all(rows, axes, 0, 0, axis_index_groups=groups, tiled=False)  12.6 us
    ppermute x6, waiting for transfers between devices, trade(): within = lax.ppermute(within, axis, inner)  9.2 us
    pallas_call x1, Pallas kernels, first_call(): pl.pallas_call(first_kernel, name='first', out_shape=(shape(72, LANES), s...  6.11 us
    pallas_call x1, Pallas kernels, second_call(): pl.pallas_call(second_kernel, name='second', out_shape=shape(72, LANES),...  4.35 us
  transfers between devices with their start and end apart: 14, of which 9 were waited for; matrix products, arithmetic and copies ran while one was open for 1% of the time, Pallas kernels for 4%

profile of v7, /device:TPU:1, one launch (start us, length us, event | category | flops | bytes accessed | tf_op | source)
XLA Modules:
  0.0 114.5 jit_solution(14253564941772597573)
XLA Ops:
  0.6 1.8 %pack.1 = (f32[9,8,128]{2,1,0:T(8,128)}, f32[9,2,128]{2,1,0:T(2,128)}, f32[9,2,128]{2,1,0:T(2,128)}) custom-call(f32[3,3,3,2,3]{4,3,2,1,0:T(2,128)} %bitcast.67, f32[3,3,3,2,3]{4,3,2,1,0:T(2,128)} %bitcast.68, s32[3,3,2,3]{3,2,1,0:T(2,128)} %bitcast.69, s32[3,3,3]{2,1,0:T(4,128)} %count_in.1, s32[3,3,3,2,40]{4,3,2,1,0:T(2,128)} %list_in.1), custom_call_target="tpu_custom_call" | custom-call | tf_op jit(solution)/shard_map/pack/pallas_call | solution.py:633
  2.5 5.9 %collective-permute-start = (f32[9,2,128]{2,1,0:T(2,128)}, f32[9,2,128]{2,1,0:T(2,128)S(1)}, u32[]{:S(2)}, u32[]{:S(2)}) collective-permute-start(f32[9,2,128]{2,1,0:T(2,128)} %get-tuple-element.32), channel_id=1, source_target_pairs={{0,7},{1,2},{2,1},{3,4},{4,3},{5,6},{6,5},{7,0},{8,15},{9,10},{10,... | collective-permute-start | bytes 27656 | tf_op jit(solution)/shard_map/ppermute | solution.py:759
  8.4 1.9 %collective-permute-start.1 = (f32[9,2,128]{2,1,0:T(2,128)}, f32[9,2,128]{2,1,0:T(2,128)S(1)}, u32[]{:S(2)}, u32[]{:S(2)}) collective-permute-start(f32[9,2,128]{2,1,0:T(2,128)} %get-tuple-element.33), channel_id=1, source_target_pairs={{0,1},{1,0},{2,3},{3,2},{4,5},{5,4},{6,7},{7,6},{8,9},{9,8},{10,11... | collective-permute-start | bytes 27656 | tf_op jit(solution)/shard_map/ppermute | solution.py:760
  10.5 2.6 %collective-permute-done.1 = f32[9,2,128]{2,1,0:T(2,128)S(1)} collective-permute-done((f32[9,2,128]{2,1,0:T(2,128)}, f32[9,2,128]{2,1,0:T(2,128)S(1)}, u32[]{:S(2)}, u32[]{:S(2)}) %collective-permute-start.1) | collective-permute-done | bytes 9248 | tf_op jit(solution)/shard_map/ppermute | solution.py:760
  13.2 8.0 %collective-permute-start.2 = (f32[3,8,128]{2,1,0:T(8,128)S(1)}, f32[3,8,128]{2,1,0:T(8,128)S(1)}, u32[]{:S(2)}, u32[]{:S(2)}) collective-permute-start(f32[3,8,128]{2,1,0:T(8,128)S(1)} %get-tuple-element.75), channel_id=1, source_target_pairs={{0,704},{64,128},{128,64},{192,256},{256,192},{320,384},{384,320},... | collective-permute-start | bytes 36872 | tf_op jit(solution)/shard_map/ppermute | solution.py:759
  21.2 1.9 %collective-permute-start.3 = (f32[3,8,128]{2,1,0:T(8,128)S(1)}, f32[3,8,128]{2,1,0:T(8,128)S(1)}, u32[]{:S(2)}, u32[]{:S(2)}) collective-permute-start(f32[3,8,128]{2,1,0:T(8,128)S(1)} %get-tuple-element.74), channel_id=1, source_target_pairs={{0,64},{64,0},{128,192},{192,128},{256,320},{320,256},{384,448},{4... | collective-permute-start | bytes 36872 | tf_op jit(solution)/shard_map/ppermute | solution.py:760
  24.6 1.1 collective-permute-done.3
  25.9 12.2 %collective-permute-start.4 = (f32[7,8,128]{2,1,0:T(8,128)S(1)}, f32[7,8,128]{2,1,0:T(8,128)S(1)}, u32[]{:S(2)}, u32[]{:S(2)}) collective-permute-start(f32[7,8,128]{2,1,0:T(8,128)S(1)} %get-tuple-element.69), channel_id=1, source_target_pairs={{0,56},{8,16},{16,8},{24,32},{32,24},{40,48},{48,40},{56,0},{1,57}... | collective-permute-start | bytes 86024 | tf_op jit(solution)/shard_map/ppermute | solution.py:759
  38.2 2.5 %collective-permute-start.5 = (f32[7,8,128]{2,1,0:T(8,128)S(1)}, f32[7,8,128]{2,1,0:T(8,128)S(1)}, u32[]{:S(2)}, u32[]{:S(2)}) collective-permute-start(f32[7,8,128]{2,1,0:T(8,128)S(1)} %get-tuple-element.68), channel_id=1, source_target_pairs={{0,8},{8,0},{16,24},{24,16},{32,40},{40,32},{48,56},{56,48},{1,9},... | collective-permute-start | bytes 86024 | tf_op jit(solution)/shard_map/ppermute | solution.py:760
  41.6 6.1 %first.1 = (f32[72,128]{1,0:T(8,128)S(1)}, f32[3,8,128]{2,1,0:T(8,128)S(1)}, f32[72,128]{1,0:T(8,128)S(1)}, f32[1,128]{1,0:T(1,128)S(1)}, f32[26,24,256]{2,1,0:T(8,128)S(1)}, /*index=5*/s32[2]{0:T(128)S(1)}) custom-call(f32[7,8,128]{2,1,0:T(8,128)S(1)} %get-tuple-element.73.low, f32[7,3,8,64]{3,2,1,0:T(8,128)S(1)} %fusion.own, ...), custom_call_target="tpu_custom_call" | custom-call | tf_op jit(solution)/shard_map/first/pallas_call | solution.py:696
  47.7 2.6 %collective-permute-start.6 = (f32[3,2,128]{2,1,0:T(2,128)S(1)}, f32[3,2,128]{2,1,0:T(2,128)S(1)}, u32[]{:S(2)}, u32[]{:S(2)}) collective-permute-start(f32[3,2,128]{2,1,0:T(2,128)S(1)} %get-tuple-element.89), channel_id=1, source_target_pairs={{0,7},{1,2},{2,1},{3,4},{4,3},{5,6},{6,5},{7,0},{8,15},{9,10},{10,... | collective-permute-start | bytes 9224 | tf_op jit(solution)/shard_map/ppermute | solution.py:759
  50.4 2.9 %collective-permute-start.7 = (f32[3,2,128]{2,1,0:T(2,128)S(1)}, f32[3,2,128]{2,1,0:T(2,128)S(1)}, u32[]{:S(2)}, u32[]{:S(2)}) collective-permute-start(f32[3,2,128]{2,1,0:T(2,128)S(1)} %get-tuple-element.90), channel_id=1, source_target_pairs={{0,1},{1,0},{2,3},{3,2},{4,5},{5,4},{6,7},{7,6},{8,9},{9,8},{10,11... | collective-permute-start | bytes 9224 | tf_op jit(solution)/shard_map/ppermute | solution.py:760
  53.3 1.4 %collective-permute-done.7 = f32[3,2,128]{2,1,0:T(2,128)S(1)} collective-permute-done((f32[3,2,128]{2,1,0:T(2,128)S(1)}, f32[3,2,128]{2,1,0:T(2,128)S(1)}, u32[]{:S(2)}, u32[]{:S(2)}) %collective-permute-start.7) | collective-permute-done | bytes 3104 | tf_op jit(solution)/shard_map/ppermute | solution.py:760
  54.8 5.0 %collective-permute-start.8 = (f32[3,8,128]{2,1,0:T(8,128)S(1)}, f32[3,8,128]{2,1,0:T(8,128)S(1)}, u32[]{:S(2)}, u32[]{:S(2)}) collective-permute-start(f32[3,8,128]{2,1,0:T(8,128)S(1)} %maximum_maximum_fusion.1), channel_id=1, source_target_pairs={{0,704},{64,128},{128,64},{192,256},{256,192},{320,384},{384,320},... | collective-permute-start | bytes 36872 | tf_op jit(solution)/shard_map/ppermute | solution.py:759
  59.8 1.9 %collective-permute-start.9 = (f32[3,8,128]{2,1,0:T(8,128)S(1)}, f32[3,8,128]{2,1,0:T(8,128)S(1)}, u32[]{:S(2)}, u32[]{:S(2)}) collective-permute-start(f32[3,8,128]{2,1,0:T(8,128)S(1)} %maximum_maximum_fusion.1), channel_id=1, source_target_pairs={{0,64},{64,0},{128,192},{192,128},{256,320},{320,256},{384,448},{4... | collective-permute-start | bytes 36872 | tf_op jit(solution)/shard_map/ppermute | solution.py:760
  62.2 2.3 %collective-permute-done.9 = f32[3,8,128]{2,1,0:T(8,128)S(1)} collective-permute-done((f32[3,8,128]{2,1,0:T(8,128)S(1)}, f32[3,8,128]{2,1,0:T(8,128)S(1)}, u32[]{:S(2)}, u32[]{:S(2)}) %collective-permute-start.9) | collective-permute-done | bytes 12320 | tf_op jit(solution)/shard_map/ppermute | solution.py:760
  64.7 9.0 %collective-permute-start.10 = (f32[2,8,128]{2,1,0:T(8,128)S(1)}, f32[2,8,128]{2,1,0:T(8,128)S(1)}, u32[]{:S(2)}, u32[]{:S(2)}) collective-permute-start(f32[2,8,128]{2,1,0:T(8,128)S(1)} %get-tuple-element.88), channel_id=1, source_target_pairs={{0,56},{8,16},{16,8},{24,32},{32,24},{40,48},{48,40},{56,0},{1,57}... | collective-permute-start | bytes 24584 | tf_op jit(solution)/shard_map/ppermute | solution.py:759
  73.7 1.9 %collective-permute-start.11 = (f32[2,8,128]{2,1,0:T(8,128)S(1)}, f32[2,8,128]{2,1,0:T(8,128)S(1)}, u32[]{:S(2)}, u32[]{:S(2)}) collective-permute-start(f32[2,8,128]{2,1,0:T(8,128)S(1)} %get-tuple-element.87), channel_id=1, source_target_pairs={{0,8},{8,0},{16,24},{24,16},{32,40},{40,32},{48,56},{56,48},{1,9},... | collective-permute-start | bytes 24584 | tf_op jit(solution)/shard_map/ppermute | solution.py:760
  76.8 1.9 %energy.1 = f32[1,128]{1,0:T(1,128)S(1)} custom-call(f32[2,8,128]{2,1,0:T(8,128)S(1)} %get-tuple-element.86.low, f32[3,8,128]{2,1,0:T(8,128)S(1)} %maximum_maximum_fusion.2.own, f32[2,8,128]{2,1,0:T(8,128)S(1)} %get-tuple-element.85.high, bf16[128,16]{1,0:T(8,128)(2,1)S(1)} %get-tuple-element.46.w1t, bf16[16,128]{1,0:T(8,128)(2,1)S(1)} %get-tuple-element.47.w1, ...), custom_call_target="tpu_custom_call" | custom-call | tf_op jit(solution)/shard_map/energy/pallas_call | solution.py:723
  79.4 6.3 %all-to-all-start = ((f32[32,1,128]{2,1,0:T(1,128)}), f32[32,1,128]{2,1,0:T(1,128)S(1)}, u32[]{:S(2)}, u32[]{:S(2)}) async-start(f32[32,1,128]{2,1,0:T(1,128)} %broadcast_in_dim.35), calls=%async_computation | async-start | bytes 32768 | tf_op jit(solution)/shard_map/all_to_all | solution.py:772
  85.7 4.3 %second.1 = f32[72,128]{1,0:T(8,128)S(1)} custom-call(f32[2,8,128]{2,1,0:T(8,128)S(1)} %get-tuple-element.86.low, f32[3,8,128]{2,1,0:T(8,128)S(1)} %maximum_maximum_fusion.2.own, f32[2,8,128]{2,1,0:T(8,128)S(1)} %get-tuple-element.85.high, bf16[128,16]{1,0:T(8,128)(2,1)S(1)} %get-tuple-element.46.w1t, bf16[16,128]{1,0:T(8,128)(2,1)S(1)} %get-tuple-element.47.w1, ...), custom_call_target="tpu_custom_call" | custom-call | flops 400000000 | bytes 4000000 | tf_op jit(solution)/shard_map/second/pallas_call | solution.py:735
  90.1 4.2 %all-to-all-done = f32[32,1,128]{2,1,0:T(1,128)S(1)} async-done(((f32[32,1,128]{2,1,0:T(1,128)}), f32[32,1,128]{2,1,0:T(1,128)S(1)}, u32[]{:S(2)}, u32[]{:S(2)}) %all-to-all-start) | async-done | bytes 16416 | tf_op jit(solution)/shard_map/all_to_all | solution.py:772
  94.9 9.6 %all-to-all-start.1 = ((f32[24,1,128]{2,1,0:T(1,128)}), f32[24,1,128]{2,1,0:T(1,128)S(1)}, u32[]{:S(2)}, u32[]{:S(2)}) async-start(f32[24,1,128]{2,1,0:T(1,128)} %broadcast_in_dim.36), calls=%async_computation.1 | async-start | bytes 24576 | tf_op jit(solution)/shard_map/all_to_all | solution.py:772
  105.5 8.4 %all-to-all-done.1 = f32[24,1,128]{2,1,0:T(1,128)S(1)} async-done(((f32[24,1,128]{2,1,0:T(1,128)}), f32[24,1,128]{2,1,0:T(1,128)S(1)}, u32[]{:S(2)}, u32[]{:S(2)}) %all-to-all-start.1) | async-done | bytes 12320 | tf_op jit(solution)/shard_map/all_to_all | solution.py:772
  (61 shorter events, 7.5 us)
Async XLA Ops:
  2.5 7.9 %copy-start.6 = (f32[9,8,128]{2,1,0:T(8,128)S(1)}, f32[9,8,128]{2,1,0:T(8,128)}, u32[]{:S(2)}) copy-start(f32[9,8,128]{2,1,0:T(8,128)} %get-tuple-element.34) | copy-start | bytes 110596
  2.5 8.0 %collective-permute-start = (f32[9,2,128]{2,1,0:T(2,128)}, f32[9,2,128]{2,1,0:T(2,128)S(1)}, u32[]{:S(2)}, u32[]{:S(2)}) collective-permute-start(f32[9,2,128]{2,1,0:T(2,128)} %get-tuple-element.32), channel_id=1, source_target_pairs={{0,7},{1,2},{2,1},{3,4},{4,3},{5,6},{6,5},{7,0},{8,15},{9,10},{10,... | collective-permute-start | bytes 27656 | tf_op jit(solution)/shard_map/ppermute | solution.py:759
  8.4 4.6 %collective-permute-start.1 = (f32[9,2,128]{2,1,0:T(2,128)}, f32[9,2,128]{2,1,0:T(2,128)S(1)}, u32[]{:S(2)}, u32[]{:S(2)}) collective-permute-start(f32[9,2,128]{2,1,0:T(2,128)} %get-tuple-element.33), channel_id=1, source_target_pairs={{0,1},{1,0},{2,3},{3,2},{4,5},{5,4},{6,7},{7,6},{8,9},{9,8},{10,11... | collective-permute-start | bytes 27656 | tf_op jit(solution)/shard_map/ppermute | solution.py:760
  13.1 10.1 %copy-start.3 = (bf16[5,128]{1,0:T(8,128)(2,1)S(1)}, bf16[5,128]{1,0:T(8,128)(2,1)}, u32[]{:S(2)}) copy-start(bf16[5,128]{1,0:T(8,128)(2,1)} %se_in.1) | copy-start | bytes 3844
  13.2 11.3 %collective-permute-start.2 = (f32[3,8,128]{2,1,0:T(8,128)S(1)}, f32[3,8,128]{2,1,0:T(8,128)S(1)}, u32[]{:S(2)}, u32[]{:S(2)}) collective-permute-start(f32[3,8,128]{2,1,0:T(8,128)S(1)} %get-tuple-element.75), channel_id=1, source_target_pairs={{0,704},{64,128},{128,64},{192,256},{256,192},{320,384},{384,320},... | collective-permute-start | bytes 36872 | tf_op jit(solution)/shard_map/ppermute | solution.py:759
  21.2 2.0 %copy-start.4 = (f32[128]{0:T(128)S(1)}, f32[128]{0:T(128)}, u32[]{:S(2)}) copy-start(f32[128]{0:T(128)} %param.20) | copy-start | bytes 1540
  21.2 2.0 %copy-start.5 = (f32[5]{0:T(128)S(1)}, f32[5]{0:T(128)}, u32[]{:S(2)}) copy-start(f32[5]{0:T(128)} %param.21) | copy-start | bytes 64
  21.2 4.4 %collective-permute-start.3 = (f32[3,8,128]{2,1,0:T(8,128)S(1)}, f32[3,8,128]{2,1,0:T(8,128)S(1)}, u32[]{:S(2)}, u32[]{:S(2)}) collective-permute-start(f32[3,8,128]{2,1,0:T(8,128)S(1)} %get-tuple-element.74), channel_id=1, source_target_pairs={{0,64},{64,0},{128,192},{192,128},{256,320},{320,256},{384,448},{4... | collective-permute-start | bytes 36872 | tf_op jit(solution)/shard_map/ppermute | solution.py:760
  23.2 0.7 copy-start.2
  23.2 0.7 copy-start
  23.2 0.7 copy-start.1
  25.9 14.8 %collective-permute-start.4 = (f32[7,8,128]{2,1,0:T(8,128)S(1)}, f32[7,8,128]{2,1,0:T(8,128)S(1)}, u32[]{:S(2)}, u32[]{:S(2)}) collective-permute-start(f32[7,8,128]{2,1,0:T(8,128)S(1)} %get-tuple-element.69), channel_id=1, source_target_pairs={{0,56},{8,16},{16,8},{24,32},{32,24},{40,48},{48,40},{56,0},{1,57}... | collective-permute-start | bytes 86024 | tf_op jit(solution)/shard_map/ppermute | solution.py:759
  38.2 3.4 %collective-permute-start.5 = (f32[7,8,128]{2,1,0:T(8,128)S(1)}, f32[7,8,128]{2,1,0:T(8,128)S(1)}, u32[]{:S(2)}, u32[]{:S(2)}) collective-permute-start(f32[7,8,128]{2,1,0:T(8,128)S(1)} %get-tuple-element.68), channel_id=1, source_target_pairs={{0,8},{8,0},{16,24},{24,16},{32,40},{40,32},{48,56},{56,48},{1,9},... | collective-permute-start | bytes 86024 | tf_op jit(solution)/shard_map/ppermute | solution.py:760
  47.7 5.6 %collective-permute-start.6 = (f32[3,2,128]{2,1,0:T(2,128)S(1)}, f32[3,2,128]{2,1,0:T(2,128)S(1)}, u32[]{:S(2)}, u32[]{:S(2)}) collective-permute-start(f32[3,2,128]{2,1,0:T(2,128)S(1)} %get-tuple-element.89), channel_id=1, source_target_pairs={{0,7},{1,2},{2,1},{3,4},{4,3},{5,6},{6,5},{7,0},{8,15},{9,10},{10,... | collective-permute-start | bytes 9224 | tf_op jit(solution)/shard_map/ppermute | solution.py:759
  50.4 4.3 %collective-permute-start.7 = (f32[3,2,128]{2,1,0:T(2,128)S(1)}, f32[3,2,128]{2,1,0:T(2,128)S(1)}, u32[]{:S(2)}, u32[]{:S(2)}) collective-permute-start(f32[3,2,128]{2,1,0:T(2,128)S(1)} %get-tuple-element.90), channel_id=1, source_target_pairs={{0,1},{1,0},{2,3},{3,2},{4,5},{5,4},{6,7},{7,6},{8,9},{9,8},{10,11... | collective-permute-start | bytes 9224 | tf_op jit(solution)/shard_map/ppermute | solution.py:760
  54.8 7.4 %collective-permute-start.8 = (f32[3,8,128]{2,1,0:T(8,128)S(1)}, f32[3,8,128]{2,1,0:T(8,128)S(1)}, u32[]{:S(2)}, u32[]{:S(2)}) collective-permute-start(f32[3,8,128]{2,1,0:T(8,128)S(1)} %maximum_maximum_fusion.1), channel_id=1, source_target_pairs={{0,704},{64,128},{128,64},{192,256},{256,192},{320,384},{384,320},... | collective-permute-start | bytes 36872 | tf_op jit(solution)/shard_map/ppermute | solution.py:759
  59.8 4.7 %collective-permute-start.9 = (f32[3,8,128]{2,1,0:T(8,128)S(1)}, f32[3,8,128]{2,1,0:T(8,128)S(1)}, u32[]{:S(2)}, u32[]{:S(2)}) collective-permute-start(f32[3,8,128]{2,1,0:T(8,128)S(1)} %maximum_maximum_fusion.1), channel_id=1, source_target_pairs={{0,64},{64,0},{128,192},{192,128},{256,320},{320,256},{384,448},{4... | collective-permute-start | bytes 36872 | tf_op jit(solution)/shard_map/ppermute | solution.py:760
  64.7 11.1 %collective-permute-start.10 = (f32[2,8,128]{2,1,0:T(8,128)S(1)}, f32[2,8,128]{2,1,0:T(8,128)S(1)}, u32[]{:S(2)}, u32[]{:S(2)}) collective-permute-start(f32[2,8,128]{2,1,0:T(8,128)S(1)} %get-tuple-element.88), channel_id=1, source_target_pairs={{0,56},{8,16},{16,8},{24,32},{32,24},{40,48},{48,40},{56,0},{1,57}... | collective-permute-start | bytes 24584 | tf_op jit(solution)/shard_map/ppermute | solution.py:759
  73.7 3.1 %collective-permute-start.11 = (f32[2,8,128]{2,1,0:T(8,128)S(1)}, f32[2,8,128]{2,1,0:T(8,128)S(1)}, u32[]{:S(2)}, u32[]{:S(2)}) collective-permute-start(f32[2,8,128]{2,1,0:T(8,128)S(1)} %get-tuple-element.87), channel_id=1, source_target_pairs={{0,8},{8,0},{16,24},{24,16},{32,40},{40,32},{48,56},{56,48},{1,9},... | collective-permute-start | bytes 24584 | tf_op jit(solution)/shard_map/ppermute | solution.py:760
  79.4 14.9 %all-to-all-start = ((f32[32,1,128]{2,1,0:T(1,128)}), f32[32,1,128]{2,1,0:T(1,128)S(1)}, u32[]{:S(2)}, u32[]{:S(2)}) async-start(f32[32,1,128]{2,1,0:T(1,128)} %broadcast_in_dim.35), calls=%async_computation | async-start | bytes 32768 | tf_op jit(solution)/shard_map/all_to_all | solution.py:772
  94.9 19.0 %all-to-all-start.1 = ((f32[24,1,128]{2,1,0:T(1,128)}), f32[24,1,128]{2,1,0:T(1,128)S(1)}, u32[]{:S(2)}, u32[]{:S(2)}) async-start(f32[24,1,128]{2,1,0:T(1,128)} %broadcast_in_dim.36), calls=%async_computation.1 | async-start | bytes 24576 | tf_op jit(solution)/shard_map/all_to_all | solution.py:772
